TPU v7x, 256 devices: a whole 4x4x8 slice. The times are simulated.
256 devices in a mesh: view: 8 (over y_lo, x), tile: 32 (over y_hi, z, core).
Axes of the slice: x: 4, y: 4 (y_hi: 2, y_lo: 2; y = y_hi * 2 + y_lo), z: 8, core: 2. Of those that a mesh axis runs over, the one named last changes fastest.
Arguments:
- estimate: float32 [1024, 64, 256], P('tile'), may hold values from 0.5 to 2
- measured: bfloat16 [8, 1024, 64, 256], P('view', 'tile'), may hold values from 0.5 to 2
- blur_profile: float32 [8, 256], P('view'), may hold values from 0.1 to 1
- view_offset: int32 [8], P('view'), may hold values from -6 to 6, as said below
- tile_shift: int32 [8], P('view'), may hold values from 0 to 31
Outputs:
- updated: float32 [1024, 64, 256], P('tile')
Inputs may be any that keep to these rules, and one draw needn't show every extreme that they name: `view_offset`: some view has offset 6 and some other view has offset -6.
All inputs are finite; a program needn't handle non-finite values.
Results may differ from a plain program's by a relative error of at most 0.0016.
Values may be sent and summed in bfloat16 or wider, within the bound.
No kernel may reach another device: no remote copies, remote signals or barrier semaphores. Data moves between devices by JAX's collectives and lax.ppermute only.
A program may use at most 64 MiB of HBM per device.

v0:
```python
import jax
import jax.numpy as jnp
from jax import lax
from jax.experimental import pallas as pl
from jax.experimental.pallas import tpu as pltpu
from jax.sharding import Mesh, PartitionSpec as P

PROFILE_SIGMA = 48.0
PAIR_SCALE = 32700.0 / 2.8
TOTAL_SCALE = PAIR_SCALE / 4.0
SLABS, ROWS, LENGTH = 32, 32, 256
TOTAL = SLABS * ROWS
GROUP = 4


def blur_matrix(profile):
    column = lax.broadcasted_iota(jnp.int32, (1, LENGTH), 1)
    distance = jnp.minimum(column, LENGTH - column).astype(jnp.float32)
    weights = profile * jnp.exp(-distance * distance / (2.0 * PROFILE_SIGMA * PROFILE_SIGMA))
    kernel = weights / jnp.sum(weights, axis=1, keepdims=True)
    rows = jnp.broadcast_to(kernel, (LENGTH, LENGTH))
    return pltpu.roll(rows, 0, 1, stride=1, stride_axis=0)


def tile_rows(wide, rest, turn, row):
    tiles = pltpu.roll(wide.reshape(-1, 8, LENGTH), turn, 1)
    count = tiles.shape[0]
    tiles = jnp.where(row < 8 - rest, tiles[: count - 1], tiles[1:])
    return tiles.reshape(8 * count - 8, LENGTH)


def blend_of(column, w):
    a = (w * 4 + column + 1).astype(jnp.float32) / 9.0
    return a, 1.0 - a


def pick_kernel(place_ref, est_ref, out0_ref, out1_ref, lines_ref, sem):
    upper, column, tile = place_ref[0], place_ref[1], place_ref[2]
    tile_y, tile_z = lax.div(tile, 16), lax.rem(lax.div(tile, 2), 8)
    z = lax.rem(tile_z + column + 4 * upper, 8)
    copies = []
    for k in range(2):
        for u in range(2):
            line = 32 * u + 16 * lax.rem(tile_y + k, 2) + 8 * lax.div(z, 4)
            for h in range(2):
                copy = pltpu.make_async_copy(
                    est_ref.at[:, pl.ds(pl.multiple_of(line, 8), 8), pl.ds(128 * h, 128)],
                    lines_ref.at[k, u, h],
                    sem.at[k, u, h],
                )
                copy.start()
                copies.append(copy)
    for copy in copies:
        copy.wait()
    rows_ref = lines_ref.reshape(2, 2, 2, ROWS * 8, 128)
    for k, out_ref in enumerate((out0_ref, out1_ref)):
        for u in range(2):
            for h in range(2):
                for c in range(2):
                    rows = rows_ref[k, u, h, pl.ds(2 * lax.rem(z, 4) + c, ROWS, stride=8)]
                    out_ref[u, c, :, pl.ds(128 * h, 128)] = rows.astype(jnp.bfloat16)


def forward_kernel(
    place_ref, own_ref, other_ref, own_profile_ref, other_profile_ref, est0_ref, est1_ref,
    est2_ref, est3_ref, inverse_ref, e_ref,
):
    est_refs = (est0_ref, est1_ref, est2_ref, est3_ref)
    upper, column, tile = place_ref[0], place_ref[1], place_ref[2]
    tile_y, tile_z, core = lax.div(tile, 16), lax.rem(lax.div(tile, 2), 8), lax.rem(tile, 2)

    for r, est_ref in enumerate(est_refs):
        source = lax.rem(column + 4 - r, 4)
        for u in range(2):
            z = lax.rem(tile_z + 16 - source - 4 * lax.rem(upper + u, 2), 8)
            for c in range(2):
                for k in range(2):
                    slab = 16 * lax.rem(tile_y + k, 2) + 2 * z + lax.rem(core + c, 2)
                    base = pl.multiple_of(slab * ROWS + 8, 8)
                    e_ref[pl.ds(base, ROWS)] = est_ref[u, c, k].astype(jnp.float32)
    e_ref[pl.ds(0, 8)] = e_ref[pl.ds(TOTAL, 8)]
    e_ref[pl.ds(TOTAL + 8, 16)] = e_ref[pl.ds(8, 16)]
    row = lax.broadcasted_iota(jnp.int32, (1, 8, LENGTH), 1)

    for w in range(2):
        is_own = upper == w
        shift = jnp.where(is_own, own_ref[0], other_ref[0])
        offset = jnp.where(is_own, own_ref[1], other_ref[1])
        a, b = blend_of(column, w)
        skip = lax.div(8 + offset, 8)
        rest = 8 + offset - 8 * skip
        turn = lax.rem(8 - rest, 8)
        profile = jnp.where(is_own, own_profile_ref[...], other_profile_ref[...])
        matrix = blur_matrix(profile).astype(jnp.bfloat16)

        def blur(k, c, w=w, a=a, b=b, matrix=matrix, skip=skip, rest=rest, turn=turn, shift=shift):
            base = pl.multiple_of(k * (ROWS * GROUP), ROWS * GROUP)
            parts = []
            for q in range(GROUP):
                s = lax.rem(k * GROUP + q + shift, SLABS)
                start = pl.multiple_of(s * ROWS + 8 * skip, 8)
                wide = tile_rows(e_ref[pl.ds(start, ROWS + 16)], rest, turn, row)
                parts.append(a * wide[:ROWS] + b * wide[1 : ROWS + 1])
            warped = jnp.concatenate(parts, axis=0).astype(jnp.bfloat16)
            forward = jnp.dot(warped, matrix, preferred_element_type=jnp.float32)
            inverse_ref[w, pl.ds(base, ROWS * GROUP)] = 1.0 / forward
            return c

        lax.fori_loop(0, SLABS // GROUP, blur, 0)


def back_kernel(
    place_ref, own_ref, other_ref, own_profile_ref, other_profile_ref, image_ref, inverse_ref,
    out_ref, b_ref,
):
    upper, column = place_ref[0], place_ref[1]
    row = lax.broadcasted_iota(jnp.int32, (1, 8, LENGTH), 1)

    for w in range(2):
        profile = jnp.where(upper == w, own_profile_ref[...], other_profile_ref[...])
        matrix = blur_matrix(profile).astype(jnp.bfloat16)

        def blur(k, c, w=w, matrix=matrix):
            base = pl.multiple_of(k * (ROWS * GROUP), ROWS * GROUP)
            image = image_ref[pl.ds(w * SLABS + k * GROUP, GROUP)].reshape(ROWS * GROUP, LENGTH)
            ratios = image.astype(jnp.float32) * inverse_ref[w, pl.ds(base, ROWS * GROUP)]
            b_ref[w, pl.ds(base + 16, ROWS * GROUP)] = lax.dot_general(
                ratios.astype(jnp.bfloat16),
                matrix,
                (((1,), (1,)), ((), ())),
                preferred_element_type=jnp.float32,
            )
            return c

        lax.fori_loop(0, SLABS // GROUP, blur, 0)
        b_ref[w, pl.ds(0, 16)] = b_ref[w, pl.ds(TOTAL, 16)]
        b_ref[w, pl.ds(TOTAL + 16, 8)] = b_ref[w, pl.ds(16, 8)]

    views = []
    for w in range(2):
        is_own = upper == w
        shift = jnp.where(is_own, own_ref[0], other_ref[0])
        offset = jnp.where(is_own, own_ref[1], other_ref[1])
        skip = lax.div(8 - offset, 8)
        rest = 8 - offset - 8 * skip
        views.append((shift, skip, rest, lax.rem(8 - rest, 8), *blend_of(column, w)))

    def join(s, c):
        product = None
        for w, (shift, skip, rest, turn, a, b) in enumerate(views):
            t = lax.rem(s - shift + SLABS, SLABS)
            start = pl.multiple_of(t * ROWS + 8 * skip, 8)
            wide = b_ref[w, pl.ds(start, ROWS + 16)]
            blended = a * wide[8:] + b * wide[7 : ROWS + 15]
            correction = tile_rows(blended, rest, turn, row)
            product = correction if product is None else product * correction
        code = jnp.clip(jnp.log(product) * PAIR_SCALE, -32767.0, 32767.0)
        code = jnp.floor(code + 0.5).astype(jnp.int32).astype(jnp.int16)
        for g in range(4):
            out_ref[g, s] = code[8 * g : 8 * g + 8]
        return c

    lax.fori_loop(0, SLABS, join, 0)


def final_kernel(est_ref, code_ref, out_ref):
    for h in range(2):
        lines = pl.ds(32 * h, 32)
        logs = code_ref[h, 0].astype(jnp.int32).astype(jnp.float32) * (1.0 / TOTAL_SCALE)
        out_ref[:, lines] = est_ref[:, lines] * jnp.exp(logs)


def distance_route(k):
    route = []
    for v in range(8):
        for y in range(2):
            for z in range(8):
                for c in range(2):
                    target = 16 * ((y + k) % 2) + 2 * ((z + v) % 8) + c
                    route.append((32 * v + 16 * y + 2 * z + c, 32 * v + target))
    return route


VMEM = pl.BlockSpec(memory_space=pltpu.VMEM)
SMEM = pl.BlockSpec(memory_space=pltpu.SMEM)


def update(estimate, measured, blur_profile, view_offset, tile_shift):
    upper = lax.axis_index("upper")
    column = lax.axis_index("column")
    swap = [(0, 1), (1, 0)]
    moves = jnp.concatenate([tile_shift, view_offset])
    other_moves = lax.ppermute(moves, "upper", swap)
    other_profile = lax.ppermute(blur_profile, "upper", swap)

    tile = lax.axis_index("tile")
    core = tile % 2
    place = jnp.stack([upper, column, tile])
    chips = pl.pallas_call(
        pick_kernel,
        out_shape=[jax.ShapeDtypeStruct((2, 2, ROWS, LENGTH), jnp.bfloat16)] * 2,
        in_specs=[SMEM, pl.BlockSpec(memory_space=pl.ANY)],
        out_specs=[VMEM] * 2,
        scratch_shapes=[
            pltpu.VMEM((2, 2, 2, ROWS, 8, 128), jnp.float32),
            pltpu.SemaphoreType.DMA((2, 2, 2)),
        ],
        cost_estimate=pl.CostEstimate(flops=0, bytes_accessed=2 << 20, transcendentals=0),
        compiler_params=pltpu.CompilerParams(vmem_limit_bytes=125 << 19),
        name="pick_kernel",
    )(place, estimate)
    arrived = []
    for k, chip in enumerate(chips):
        arrived.append(lax.ppermute(chip, ("upper", "column", "tile"), distance_route(k)))
    image = measured[0].transpose(1, 0, 2)
    image_lines = lax.all_to_all(image, ("upper", "tile"), 0, 0, tiled=True)

    arrived = jnp.stack(arrived, axis=0)
    mine = lax.dynamic_index_in_dim(arrived, core, 2, keepdims=False)
    given = lax.dynamic_index_in_dim(arrived, 1 - core, 2, keepdims=False)
    given = lax.ppermute(given, "tile", [(i, i ^ 1) for i in range(32)])
    both = jnp.stack([mine, given])
    mine = lax.dynamic_index_in_dim(both, upper, 2, keepdims=False)
    given = lax.dynamic_index_in_dim(both, 1 - upper, 2, keepdims=False)
    given = lax.ppermute(given, "upper", swap)
    piece = jnp.stack([mine, given])
    est_lines = [piece]
    for d in (1, 2, 3):
        route = [(i, (i + d) % 4) for i in range(4)]
        est_lines.append(lax.ppermute(piece, "column", route))

    inverse = pl.pallas_call(
        forward_kernel,
        out_shape=jax.ShapeDtypeStruct((2, TOTAL, LENGTH), jnp.float32),
        in_specs=[SMEM] * 3 + [VMEM] * 6,
        out_specs=VMEM,
        scratch_shapes=[pltpu.VMEM((TOTAL + 24, LENGTH), jnp.float32)],
        cost_estimate=pl.CostEstimate(
            flops=4 * TOTAL * LENGTH * LENGTH, bytes_accessed=8 << 20, transcendentals=0
        ),
        compiler_params=pltpu.CompilerParams(vmem_limit_bytes=16 << 20),
        name="forward_kernel",
    )(place, moves, other_moves, blur_profile, other_profile, *est_lines)
    codes = pl.pallas_call(
        back_kernel,
        out_shape=jax.ShapeDtypeStruct((4, SLABS, 8, LENGTH), jnp.int16),
        in_specs=[SMEM] * 3 + [VMEM] * 4,
        out_specs=VMEM,
        scratch_shapes=[pltpu.VMEM((2, TOTAL + 24, LENGTH), jnp.float32)],
        compiler_params=pltpu.CompilerParams(vmem_limit_bytes=16 << 20),
        name="back_kernel",
    )(place, moves, other_moves, blur_profile, other_profile, image_lines, inverse)
    codes = lax.all_to_all(codes, "column", 0, 0, tiled=True)
    total = jnp.sum(codes.astype(jnp.int32), axis=0)
    logs = ((total + 2) >> 2).astype(jnp.int16)
    logs = lax.all_to_all(logs, "tile", 0, 0, tiled=True)
    logs = jnp.broadcast_to(logs.transpose(1, 0, 2)[None], (8, 8, 32, LENGTH))
    logs = lax.all_to_all(logs, ("upper", "column"), 0, 0, tiled=True)

    return pl.pallas_call(
        final_kernel,
        grid=(4,),
        out_shape=jax.ShapeDtypeStruct((32, 64, LENGTH), jnp.float32),
        in_specs=[
            pl.BlockSpec((8, 64, LENGTH), lambda g: (g, 0, 0)),
            pl.BlockSpec((2, 1, 8, 32, LENGTH), lambda g: (0, g, 0, 0, 0)),
        ],
        out_specs=pl.BlockSpec((8, 64, LENGTH), lambda g: (g, 0, 0)),
        compiler_params=pltpu.CompilerParams(vmem_limit_bytes=16 << 20),
        name="final_kernel",
    )(estimate, logs.reshape(2, 4, 8, 32, LENGTH))


def solution(mesh):
    fine = Mesh(mesh.devices.reshape(2, 4, 32), ("upper", "column", "tile"))
    view = ("upper", "column")
    placed = (P("tile"), P(view, "tile"), P(view), P(view), P(view))
    return jax.shard_map(update, mesh=fine, in_specs=placed, out_specs=P("tile"), check_vma=False)
```

profile of v0, /device:TPU:1, one launch (start us, length us, event | category | flops | bytes accessed | tf_op | source)
XLA Modules:
  0.0 126.5 jit_solution(10248332979956231677)
XLA Ops:
  0.0 2.8 %copy.11 = bf16[1,32,64,256]{3,1,2,0:T(8,128)(2,1)} copy(bf16[1,32,64,256]{3,2,1,0:T(8,128)(2,1)} %param.6) | data formatting | bytes 2097152 | tf_op args[1]
  2.8 0.0 copy-start.2
  2.8 13.3 %all-to-all-start = ((bf16[64,32,256]{2,1,0:T(8,128)(2,1)}), bf16[64,32,256]{2,1,0:T(8,128)(2,1)S(1)}, u32[]{:S(2)}, u32[]{:S(2)}) async-start(bf16[64,32,256]{2,1,0:T(8,128)(2,1)} %bitcast.21), calls=%async_computation | async-start | bytes 2097152 | tf_op jit(solution)/shard_map/all_to_all | solution.py:216
  16.1 0.7 pad_add_fusion.place_ref
  16.7 0.0 copy-start.1
  16.7 2.9 %pick_kernel.1 = (bf16[2,2,32,256]{3,2,1,0:T(8,128)(2,1)}, bf16[2,2,32,256]{3,2,1,0:T(8,128)(2,1)}) custom-call(s32[3]{0:T(128)} %pad_add_fusion.place_ref, f32[32,64,256]{2,1,0:T(8,128)} %est_ref.3), custom_call_target="tpu_custom_call" | custom-call | bytes 2097152 | tf_op jit(solution)/shard_map/pick_kernel/pallas_call | solution.py:199
  19.6 1.5 %collective-permute-start.2 = (bf16[2,2,32,256]{3,2,1,0:T(8,128)(2,1)}, bf16[2,2,32,256]{3,2,1,0:T(8,128)(2,1)S(1)}, u32[]{:S(2)}, u32[]{:S(2)}) collective-permute-start(bf16[2,2,32,256]{3,2,1,0:T(8,128)(2,1)} %get-tuple-element.7), channel_id=1, source_target_pairs={{0,0},{1,1},{2,2},{3,3},{4,4},{5,5},{6,6},{7,7},{8,8},{9,9},{10,10... | collective-permute-start | bytes 196616 | tf_op jit(solution)/shard_map/ppermute | solution.py:214
  21.1 2.9 %collective-permute-start.3 = (bf16[2,2,32,256]{3,2,1,0:T(8,128)(2,1)}, bf16[2,2,32,256]{3,2,1,0:T(8,128)(2,1)S(1)}, u32[]{:S(2)}, u32[]{:S(2)}) collective-permute-start(bf16[2,2,32,256]{3,2,1,0:T(8,128)(2,1)} %get-tuple-element.8), channel_id=1, source_target_pairs={{0,16},{1,17},{2,18},{3,19},{4,20},{5,21},{6,22},{7,23},{8,24},{9,... | collective-permute-start | bytes 196616 | tf_op jit(solution)/shard_map/ppermute | solution.py:214
  24.0 0.0 collective-permute-done.2
  24.0 3.1 %collective-permute-done.3 = bf16[2,2,32,256]{3,2,1,0:T(8,128)(2,1)S(1)} collective-permute-done((bf16[2,2,32,256]{3,2,1,0:T(8,128)(2,1)}, bf16[2,2,32,256]{3,2,1,0:T(8,128)(2,1)S(1)}, u32[]{:S(2)}, u32[]{:S(2)}) %collective-permute-start.3) | collective-permute-done | bytes 65568 | tf_op jit(solution)/shard_map/ppermute | solution.py:214
  27.1 1.8 %collective-permute-start.4 = (bf16[2,2,32,256]{3,2,1,0:T(8,128)(2,1)S(1)}, bf16[2,2,32,256]{3,2,1,0:T(8,128)(2,1)S(1)}, u32[]{:S(2)}, u32[]{:S(2)}) collective-permute-start(bf16[2,2,32,256]{3,2,1,0:T(8,128)(2,1)S(1)} %get-tuple-element.11), channel_id=1, source_target_pairs={{0,1},{1,0},{2,3},{3,2},{4,5},{5,4},{6,7},{7,6},{8,9},{9,8},{10,11... | collective-permute-start | bytes 196616 | tf_op jit(solution)/shard_map/ppermute | solution.py:221
  29.0 0.9 collective-permute-done.4
  29.9 25.1 %collective-permute-start.5 = (bf16[2,2,32,256]{3,2,1,0:T(8,128)(2,1)S(1)}, bf16[2,2,32,256]{3,2,1,0:T(8,128)(2,1)S(1)}, u32[]{:S(2)}, u32[]{:S(2)}) collective-permute-start(bf16[2,2,32,256]{3,2,1,0:T(8,128)(2,1)S(1)} %get-tuple-element.10), channel_id=1, source_target_pairs={{0,128},{128,0},{1,129},{129,1},{2,130},{130,2},{3,131},{131,3},{4... | collective-permute-start | bytes 196616 | tf_op jit(solution)/shard_map/ppermute | solution.py:225
  55.0 2.1 %collective-permute-done.5 = bf16[2,2,32,256]{3,2,1,0:T(8,128)(2,1)S(1)} collective-permute-done((bf16[2,2,32,256]{3,2,1,0:T(8,128)(2,1)S(1)}, bf16[2,2,32,256]{3,2,1,0:T(8,128)(2,1)S(1)}, u32[]{:S(2)}, u32[]{:S(2)}) %collective-permute-start.5) | collective-permute-done | bytes 65568 | tf_op jit(solution)/shard_map/ppermute | solution.py:225
  57.1 5.0 %collective-permute-start.8 = (bf16[2,2,2,32,256]{4,3,2,1,0:T(8,128)(2,1)S(1)}, bf16[2,2,2,32,256]{4,3,2,1,0:T(8,128)(2,1)S(1)}, u32[]{:S(2)}, u32[]{:S(2)}) collective-permute-start(bf16[2,2,2,32,256]{4,3,2,1,0:T(8,128)(2,1)S(1)} %pad_maximum_fusion.est0_ref), channel_id=1, source_target_pairs={{0,96},{32,0},{64,32},{96,64},{1,97},{33,1},{65,33},{97,65},{2,98}... | collective-permute-start | bytes 393224 | tf_op jit(solution)/shard_map/ppermute | solution.py:230
  62.1 0.0 collective-permute-start.7
  62.1 0.7 collective-permute-start.6
  62.7 0.0 copy-done.2
  62.8 0.5 collective-permute-start.1
  64.5 0.1 pad_add_fusion.1.own_ref
  64.6 1.0 collective-permute-start
  65.6 1.4 %collective-permute-done.other_ref = s32[2]{0:T(128)S(1)} collective-permute-done((s32[2]{0:T(128)S(1)}, s32[2]{0:T(128)S(1)}, u32[]{:S(2)}, u32[]{:S(2)}) %collective-permute-start) | collective-permute-done | bytes 40 | tf_op jit(solution)/shard_map/ppermute | solution.py:193
  67.0 0.0 collective-permute-done.1.other_profile_ref
  67.0 0.5 collective-permute-done.8.est3_ref
  67.5 0.0 collective-permute-done.7.est2_ref
  67.5 3.3 %collective-permute-done.6.est1_ref = bf16[2,2,2,32,256]{4,3,2,1,0:T(8,128)(2,1)S(1)} collective-permute-done((bf16[2,2,2,32,256]{4,3,2,1,0:T(8,128)(2,1)S(1)}, bf16[2,2,2,32,256]{4,3,2,1,0:T(8,128)(2,1)S(1)}, u32[]{:S(2)}, u32[]{:S(2)}) %collective-permute-start.6) | collective-permute-done | bytes 131104 | tf_op jit(solution)/shard_map/ppermute | solution.py:230
  70.8 0.0 copy-done.1
  70.8 3.9 %forward_kernel.1.inverse_ref = f32[2,1024,256]{2,1,0:T(8,128)S(1)} custom-call(s32[3]{0:T(128)S(1)} %copy-done.1, s32[2]{0:T(128)S(1)} %pad_add_fusion.1.own_ref, s32[2]{0:T(128)S(1)} %collective-permute-done.other_ref, f32[1,256]{1,0:T(1,128)S(1)} %copy-done.2, f32[1,256]{1,0:T(1,128)S(1)} %collective-permute-done.1.other_profile_ref, ...), custom_call_target="tpu_custom_call" | custom-call | flops 268435456 | bytes 8388608 | tf_op jit(solution)/shard_map/forward_kernel/pallas_call | solution.py:232
  74.6 0.0 all-to-all-done.image_ref
  74.7 5.7 %back_kernel.1 = s16[4,32,8,256]{3,2,1,0:T(8,128)(2,1)S(1)} custom-call(s32[3]{0:T(128)S(1)} %copy-done.1, s32[2]{0:T(128)S(1)} %pad_add_fusion.1.own_ref, s32[2]{0:T(128)S(1)} %collective-permute-done.other_ref, f32[1,256]{1,0:T(1,128)S(1)} %copy-done.2, f32[1,256]{1,0:T(1,128)S(1)} %collective-permute-done.1.other_profile_ref, ...), custom_call_target="tpu_custom_call" | custom-call | tf_op jit(solution)/shard_map/back_kernel/pallas_call | solution.py:244
  80.3 10.7 %all_to_all.20 = s16[4,32,8,256]{3,2,1,0:T(8,128)(2,1)S(1)} all-to-all(s16[4,32,8,256]{3,2,1,0:T(8,128)(2,1)S(1)} %back_kernel.1), channel_id=1, replica_groups=mesh['upper'=2,'column'=4,'tile'=32] {'column'}, dimensions={0} | all-to-all | bytes 1048576 | tf_op jit(solution)/shard_map/all_to_all | solution.py:253
  91.1 0.1 convert_reduce_fusion
  91.2 0.0 copy-start
  91.2 16.1 %all_to_all.21 = s16[32,8,256]{2,1,0:T(8,128)(2,1)S(1)} all-to-all(s16[32,8,256]{2,1,0:T(8,128)(2,1)S(1)} %shift-right-arithmetic_convert_fusion), channel_id=1, replica_groups=mesh['upper'=2,'column'=4,'tile'=32] {'tile'}, dimensions={0} | all-to-all | bytes 262144 | tf_op jit(solution)/shard_map/all_to_all | solution.py:256
  107.3 0.1 broadcast_in_dim.2
  107.5 17.0 %all_to_all.22 = s16[8,8,32,256]{3,2,1,0:T(8,128)(2,1)S(1)} all-to-all(s16[8,8,32,256]{3,2,1,0:T(8,128)(2,1)S(1)} %broadcast_in_dim.2), channel_id=1, replica_groups=mesh['upper'=2,'column'=4,'tile'=32] {'upper','column'}, dimensions={0} | all-to-all | bytes 2097152 | tf_op jit(solution)/shard_map/all_to_all | solution.py:258
  124.4 0.0 copy-done
  124.4 2.0 %final_kernel.1 = f32[32,64,256]{2,1,0:T(8,128)} custom-call(f32[32,64,256]{2,1,0:T(8,128)S(1)} %copy-done, s16[2,4,8,32,256]{4,3,2,1,0:T(8,128)(2,1)S(1)} %bitcast.22), custom_call_target="tpu_custom_call" | custom-call | tf_op jit(solution)/shard_map/final_kernel/pallas_call | solution.py:260
  (5 shorter events, 0.1 us)
Async XLA Ops:
  2.8 60.0 %copy-start.2 = (f32[1,256]{1,0:T(1,128)S(1)}, f32[1,256]{1,0:T(1,128)}, u32[]{:S(2)}) copy-start(f32[1,256]{1,0:T(1,128)} %own_profile_ref.3) | copy-start | bytes 3076
  2.8 71.9 %all-to-all-start = ((bf16[64,32,256]{2,1,0:T(8,128)(2,1)}), bf16[64,32,256]{2,1,0:T(8,128)(2,1)S(1)}, u32[]{:S(2)}, u32[]{:S(2)}) async-start(bf16[64,32,256]{2,1,0:T(8,128)(2,1)} %bitcast.21), calls=%async_computation | async-start | bytes 2097152 | tf_op jit(solution)/shard_map/all_to_all | solution.py:216
  16.7 54.1 %copy-start.1 = (s32[3]{0:T(128)S(1)}, s32[3]{0:T(128)}, u32[]{:S(2)}) copy-start(s32[3]{0:T(128)} %pad_add_fusion.place_ref) | copy-start | bytes 40
  19.6 4.4 %collective-permute-start.2 = (bf16[2,2,32,256]{3,2,1,0:T(8,128)(2,1)}, bf16[2,2,32,256]{3,2,1,0:T(8,128)(2,1)S(1)}, u32[]{:S(2)}, u32[]{:S(2)}) collective-permute-start(bf16[2,2,32,256]{3,2,1,0:T(8,128)(2,1)} %get-tuple-element.7), channel_id=1, source_target_pairs={{0,0},{1,1},{2,2},{3,3},{4,4},{5,5},{6,6},{7,7},{8,8},{9,9},{10,10... | collective-permute-start | bytes 196616 | tf_op jit(solution)/shard_map/ppermute | solution.py:214
  21.1 6.0 %collective-permute-start.3 = (bf16[2,2,32,256]{3,2,1,0:T(8,128)(2,1)}, bf16[2,2,32,256]{3,2,1,0:T(8,128)(2,1)S(1)}, u32[]{:S(2)}, u32[]{:S(2)}) collective-permute-start(bf16[2,2,32,256]{3,2,1,0:T(8,128)(2,1)} %get-tuple-element.8), channel_id=1, source_target_pairs={{0,16},{1,17},{2,18},{3,19},{4,20},{5,21},{6,22},{7,23},{8,24},{9,... | collective-permute-start | bytes 196616 | tf_op jit(solution)/shard_map/ppermute | solution.py:214
  27.1 2.7 %collective-permute-start.4 = (bf16[2,2,32,256]{3,2,1,0:T(8,128)(2,1)S(1)}, bf16[2,2,32,256]{3,2,1,0:T(8,128)(2,1)S(1)}, u32[]{:S(2)}, u32[]{:S(2)}) collective-permute-start(bf16[2,2,32,256]{3,2,1,0:T(8,128)(2,1)S(1)} %get-tuple-element.11), channel_id=1, source_target_pairs={{0,1},{1,0},{2,3},{3,2},{4,5},{5,4},{6,7},{7,6},{8,9},{9,8},{10,11... | collective-permute-start | bytes 196616 | tf_op jit(solution)/shard_map/ppermute | solution.py:221
  29.9 27.2 %collective-permute-start.5 = (bf16[2,2,32,256]{3,2,1,0:T(8,128)(2,1)S(1)}, bf16[2,2,32,256]{3,2,1,0:T(8,128)(2,1)S(1)}, u32[]{:S(2)}, u32[]{:S(2)}) collective-permute-start(bf16[2,2,32,256]{3,2,1,0:T(8,128)(2,1)S(1)} %get-tuple-element.10), channel_id=1, source_target_pairs={{0,128},{128,0},{1,129},{129,1},{2,130},{130,2},{3,131},{131,3},{4... | collective-permute-start | bytes 196616 | tf_op jit(solution)/shard_map/ppermute | solution.py:225
  57.1 10.4 %collective-permute-start.8 = (bf16[2,2,2,32,256]{4,3,2,1,0:T(8,128)(2,1)S(1)}, bf16[2,2,2,32,256]{4,3,2,1,0:T(8,128)(2,1)S(1)}, u32[]{:S(2)}, u32[]{:S(2)}) collective-permute-start(bf16[2,2,2,32,256]{4,3,2,1,0:T(8,128)(2,1)S(1)} %pad_maximum_fusion.est0_ref), channel_id=1, source_target_pairs={{0,96},{32,0},{64,32},{96,64},{1,97},{33,1},{65,33},{97,65},{2,98}... | collective-permute-start | bytes 393224 | tf_op jit(solution)/shard_map/ppermute | solution.py:230
  62.1 5.4 %collective-permute-start.7 = (bf16[2,2,2,32,256]{4,3,2,1,0:T(8,128)(2,1)S(1)}, bf16[2,2,2,32,256]{4,3,2,1,0:T(8,128)(2,1)S(1)}, u32[]{:S(2)}, u32[]{:S(2)}) collective-permute-start(bf16[2,2,2,32,256]{4,3,2,1,0:T(8,128)(2,1)S(1)} %pad_maximum_fusion.est0_ref), channel_id=1, source_target_pairs={{0,64},{32,96},{64,0},{96,32},{1,65},{33,97},{65,1},{97,33},{2,66}... | collective-permute-start | bytes 393224 | tf_op jit(solution)/shard_map/ppermute | solution.py:230
  62.1 8.7 %collective-permute-start.6 = (bf16[2,2,2,32,256]{4,3,2,1,0:T(8,128)(2,1)S(1)}, bf16[2,2,2,32,256]{4,3,2,1,0:T(8,128)(2,1)S(1)}, u32[]{:S(2)}, u32[]{:S(2)}) collective-permute-start(bf16[2,2,2,32,256]{4,3,2,1,0:T(8,128)(2,1)S(1)} %pad_maximum_fusion.est0_ref), channel_id=1, source_target_pairs={{0,32},{32,64},{64,96},{96,0},{1,33},{33,65},{65,97},{97,1},{2,34}... | collective-permute-start | bytes 393224 | tf_op jit(solution)/shard_map/ppermute | solution.py:230
  62.8 4.3 %collective-permute-start.1 = (f32[1,256]{1,0:T(1,128)S(1)}, f32[1,256]{1,0:T(1,128)S(1)}, u32[]{:S(2)}, u32[]{:S(2)}) collective-permute-start(f32[1,256]{1,0:T(1,128)S(1)} %copy-done.2), channel_id=1, source_target_pairs={{0,128},{128,0},{1,129},{129,1},{2,130},{130,2},{3,131},{131,3},{4... | collective-permute-start | bytes 3080 | tf_op jit(solution)/shard_map/ppermute | solution.py:194
  64.6 2.4 %collective-permute-start = (s32[2]{0:T(128)S(1)}, s32[2]{0:T(128)S(1)}, u32[]{:S(2)}, u32[]{:S(2)}) collective-permute-start(s32[2]{0:T(128)S(1)} %pad_add_fusion.1.own_ref), channel_id=1, source_target_pairs={{0,128},{128,0},{1,129},{129,1},{2,130},{130,2},{3,131},{131,3},{4... | collective-permute-start | bytes 32 | tf_op jit(solution)/shard_map/ppermute | solution.py:193
  91.2 33.2 %copy-start = (f32[32,64,256]{2,1,0:T(8,128)S(1)}, f32[32,64,256]{2,1,0:T(8,128)}, u32[]{:S(2)}) copy-start(f32[32,64,256]{2,1,0:T(8,128)} %est_ref.3) | copy-start | bytes 6291460
where the time goes:
time: 127 us; the launch traced here: 126 us
  starting transfers between devices  51.7 us (41%)
  blocking collectives  43.8 us (34%)
  Pallas kernels  14.5 us (11%)
  waiting for transfers between devices  11.3 us (9%)
  local copies, waits for them, and re-layouts  2.93 us (2%)
  between operations  1.4 us (1%)
    ppermute x1, starting transfers between devices, update(): given = lax.ppermute(given, 'upper', swap)  25.1 us
    all_to_all x1, blocking collectives, update(): logs = lax.all_to_all(logs, ('upper', 'column'), 0, 0, tiled=True)  17 us
    all_to_all x1, blocking collectives, update(): logs = lax.all_to_all(logs, 'tile', 0, 0, tiled=True)  16.1 us
    all_to_all x1, starting transfers between devices, update(): image_lines = lax.all_to_all(image, ('upper', 'tile'), 0, 0, tiled=True)  13.3 us
    all_to_all x1, blocking collectives, update(): codes = lax.all_to_all(codes, 'column', 0, 0, tiled=True)  10.7 us
    pallas_call x1, Pallas kernels, update(): pl.pallas_call(back_kernel, out_shape=jax.ShapeDtypeStruct((4, SLABS, 8,...  5.66 us
    ppermute x3, starting transfers between devices, update(): est_lines.append(lax.ppermute(piece, 'column', route))  5.66 us
    ppermute x2, starting transfers between devices, update(): lax.ppermute(chip, ('upper', 'column', 'tile'), distance_route(k))  4.36 us
  transfers between devices with their start and end apart: 10, of which 6 were waited for; matrix products, arithmetic and copies ran while one was open for 1% of the time, Pallas kernels for 5%

commit v1 on v0

--- a/solution.py
+++ b/solution.py
@@ -34,8 +34,13 @@
     return a, 1.0 - a
 
 
-def pick_kernel(place_ref, est_ref, out0_ref, out1_ref, lines_ref, sem):
-    upper, column, tile = place_ref[0], place_ref[1], place_ref[2]
+def place():
+    tile = lax.axis_index("tile")
+    return lax.axis_index("upper"), lax.axis_index("column"), tile
+
+
+def pick_kernel(est_ref, out0_ref, out1_ref, lines_ref, sem):
+    upper, column, tile = place()
     tile_y, tile_z = lax.div(tile, 16), lax.rem(lax.div(tile, 2), 8)
     z = lax.rem(tile_z + column + 4 * upper, 8)
     copies = []
@@ -62,11 +67,11 @@
 
 
 def forward_kernel(
-    place_ref, own_ref, other_ref, own_profile_ref, other_profile_ref, est0_ref, est1_ref,
+    shift_ref, offset_ref, other_ref, own_profile_ref, other_profile_ref, est0_ref, est1_ref,
     est2_ref, est3_ref, inverse_ref, e_ref,
 ):
     est_refs = (est0_ref, est1_ref, est2_ref, est3_ref)
-    upper, column, tile = place_ref[0], place_ref[1], place_ref[2]
+    upper, column, tile = place()
     tile_y, tile_z, core = lax.div(tile, 16), lax.rem(lax.div(tile, 2), 8), lax.rem(tile, 2)
 
     for r, est_ref in enumerate(est_refs):
@@ -84,13 +89,13 @@
 
     for w in range(2):
         is_own = upper == w
-        shift = jnp.where(is_own, own_ref[0], other_ref[0])
-        offset = jnp.where(is_own, own_ref[1], other_ref[1])
+        shift = jnp.where(is_own, shift_ref[0], other_ref[0, LENGTH].astype(jnp.int32))
+        offset = jnp.where(is_own, offset_ref[0], other_ref[0, LENGTH + 1].astype(jnp.int32))
         a, b = blend_of(column, w)
         skip = lax.div(8 + offset, 8)
         rest = 8 + offset - 8 * skip
         turn = lax.rem(8 - rest, 8)
-        profile = jnp.where(is_own, own_profile_ref[...], other_profile_ref[...])
+        profile = jnp.where(is_own, own_profile_ref[...], other_profile_ref[:, pl.ds(0, LENGTH)])
         matrix = blur_matrix(profile).astype(jnp.bfloat16)
 
         def blur(k, c, w=w, a=a, b=b, matrix=matrix, skip=skip, rest=rest, turn=turn, shift=shift):
@@ -110,14 +115,14 @@
 
 
 def back_kernel(
-    place_ref, own_ref, other_ref, own_profile_ref, other_profile_ref, image_ref, inverse_ref,
+    shift_ref, offset_ref, other_ref, own_profile_ref, other_profile_ref, image_ref, inverse_ref,
     out_ref, b_ref,
 ):
-    upper, column = place_ref[0], place_ref[1]
+    upper, column, _ = place()
     row = lax.broadcasted_iota(jnp.int32, (1, 8, LENGTH), 1)
 
     for w in range(2):
-        profile = jnp.where(upper == w, own_profile_ref[...], other_profile_ref[...])
+        profile = jnp.where(upper == w, own_profile_ref[...], other_profile_ref[:, pl.ds(0, LENGTH)])
         matrix = blur_matrix(profile).astype(jnp.bfloat16)
 
         def blur(k, c, w=w, matrix=matrix):
@@ -139,8 +144,8 @@
     views = []
     for w in range(2):
         is_own = upper == w
-        shift = jnp.where(is_own, own_ref[0], other_ref[0])
-        offset = jnp.where(is_own, own_ref[1], other_ref[1])
+        shift = jnp.where(is_own, shift_ref[0], other_ref[0, LENGTH].astype(jnp.int32))
+        offset = jnp.where(is_own, offset_ref[0], other_ref[0, LENGTH + 1].astype(jnp.int32))
         skip = lax.div(8 - offset, 8)
         rest = 8 - offset - 8 * skip
         views.append((shift, skip, rest, lax.rem(8 - rest, 8), *blend_of(column, w)))
@@ -157,7 +162,7 @@
         code = jnp.clip(jnp.log(product) * PAIR_SCALE, -32767.0, 32767.0)
         code = jnp.floor(code + 0.5).astype(jnp.int32).astype(jnp.int16)
         for g in range(4):
-            out_ref[g, s] = code[8 * g : 8 * g + 8]
+            out_ref[lax.rem(g - column + 4, 4), s] = code[8 * g : 8 * g + 8]
         return c
 
     lax.fori_loop(0, SLABS, join, 0)
@@ -187,19 +192,17 @@
 
 def update(estimate, measured, blur_profile, view_offset, tile_shift):
     upper = lax.axis_index("upper")
-    column = lax.axis_index("column")
     swap = [(0, 1), (1, 0)]
-    moves = jnp.concatenate([tile_shift, view_offset])
-    other_moves = lax.ppermute(moves, "upper", swap)
-    other_profile = lax.ppermute(blur_profile, "upper", swap)
+    moves = jnp.concatenate([tile_shift, view_offset]).astype(jnp.float32)
+    info = jnp.concatenate([blur_profile, jnp.pad(moves, (0, 126))[None]], axis=1)
+    other = lax.ppermute(info, "upper", swap)
 
     tile = lax.axis_index("tile")
     core = tile % 2
-    place = jnp.stack([upper, column, tile])
     chips = pl.pallas_call(
         pick_kernel,
         out_shape=[jax.ShapeDtypeStruct((2, 2, ROWS, LENGTH), jnp.bfloat16)] * 2,
-        in_specs=[SMEM, pl.BlockSpec(memory_space=pl.ANY)],
+        in_specs=[pl.BlockSpec(memory_space=pl.ANY)],
         out_specs=[VMEM] * 2,
         scratch_shapes=[
             pltpu.VMEM((2, 2, 2, ROWS, 8, 128), jnp.float32),
@@ -208,7 +211,7 @@
         cost_estimate=pl.CostEstimate(flops=0, bytes_accessed=2 << 20, transcendentals=0),
         compiler_params=pltpu.CompilerParams(vmem_limit_bytes=125 << 19),
         name="pick_kernel",
-    )(place, estimate)
+    )(estimate)
     arrived = []
     for k, chip in enumerate(chips):
         arrived.append(lax.ppermute(chip, ("upper", "column", "tile"), distance_route(k)))
@@ -240,7 +243,7 @@
         ),
         compiler_params=pltpu.CompilerParams(vmem_limit_bytes=16 << 20),
         name="forward_kernel",
-    )(place, moves, other_moves, blur_profile, other_profile, *est_lines)
+    )(tile_shift, view_offset, other, blur_profile, other, *est_lines)
     codes = pl.pallas_call(
         back_kernel,
         out_shape=jax.ShapeDtypeStruct((4, SLABS, 8, LENGTH), jnp.int16),
@@ -249,9 +252,11 @@
         scratch_shapes=[pltpu.VMEM((2, TOTAL + 24, LENGTH), jnp.float32)],
         compiler_params=pltpu.CompilerParams(vmem_limit_bytes=16 << 20),
         name="back_kernel",
-    )(place, moves, other_moves, blur_profile, other_profile, image_lines, inverse)
-    codes = lax.all_to_all(codes, "column", 0, 0, tiled=True)
-    total = jnp.sum(codes.astype(jnp.int32), axis=0)
+    )(tile_shift, view_offset, other, blur_profile, other, image_lines, inverse)
+    total = codes[0].astype(jnp.int32)
+    for d in (2, 1, 3):
+        route = [(i, (i + d) % 4) for i in range(4)]
+        total += lax.ppermute(codes[d], "column", route).astype(jnp.int32)
     logs = ((total + 2) >> 2).astype(jnp.int16)
     logs = lax.all_to_all(logs, "tile", 0, 0, tiled=True)
     logs = jnp.broadcast_to(logs.transpose(1, 0, 2)[None], (8, 8, 32, LENGTH))

time: 127 us -> 125 us (0.984)
  blocking collectives: 43.8 us -> 31.2 us
  waiting for transfers between devices: 11.3 us -> 21.4 us
  starting transfers between devices: 51.7 us -> 53.8 us
    all_to_all x1 -> x0, blocking collectives: 10.7 us -> none  [update(): codes = lax.all_to_all(codes, 'column', 0, 0, tiled=True)]
    ppermute x2 -> x4, waiting for transfers between devices: 1.42 us -> 9.85 us  [the longest x3 7.7 us: update(): total += lax.ppermute(codes[d], 'column', route).astype(jnp.int32)]
    ppermute x3, waiting for transfers between devices: 3.73 us -> 5.94 us  [update(): est_lines.append(lax.ppermute(piece, 'column', route))]
    all_to_all x1, blocking collectives: 16.1 us -> 14.2 us  [update(): logs = lax.all_to_all(logs, 'tile', 0, 0, tiled=True)]
    ppermute x1, starting transfers between devices: 25.1 us -> 26.9 us  [update(): given = lax.ppermute(given, 'upper', swap)]
    unnamed x7 -> x5, local copies, waits for them, and re-layouts: 2.79 us -> 2.78 us
  transfers between devices with their start and end apart: 10 -> 12, of which waited for: 6 -> 7; matrix products, arithmetic and copies ran while one was open for 1% -> 0% of each run, Pallas kernels for 5% -> 5%
where the time goes in v1:
time: 125 us
  starting transfers between devices  53.8 us (43%)
  blocking collectives  31.2 us (25%)
  waiting for transfers between devices  21.4 us (17%)
  Pallas kernels  13.7 us (11%)
  local copies, waits for them, and re-layouts  2.96 us (2%)
  between operations  1.41 us (1%)
    ppermute x1, starting transfers between devices, update(): given = lax.ppermute(given, 'upper', swap)  26.9 us
    all_to_all x1, blocking collectives, update(): logs = lax.all_to_all(logs, ('upper', 'column'), 0, 0, tiled=True)  17 us
    all_to_all x1, blocking collectives, update(): logs = lax.all_to_all(logs, 'tile', 0, 0, tiled=True)  14.2 us
    all_to_all x1, starting transfers between devices, update(): image_lines = lax.all_to_all(image, ('upper', 'tile'), 0, 0, tiled=True)  13.3 us
    ppermute x3, waiting for transfers between devices, update(): total += lax.ppermute(codes[d], 'column', route).astype(jnp.int32)  7.7 us
    ppermute x3, waiting for transfers between devices, update(): est_lines.append(lax.ppermute(piece, 'column', route))  5.94 us
    ppermute x3, starting transfers between devices, update(): est_lines.append(lax.ppermute(piece, 'column', route))  5.83 us
    pallas_call x1, Pallas kernels, update(): pl.pallas_call(back_kernel, out_shape=jax.ShapeDtypeStruct((4, SLABS, 8,...  5.64 us
  transfers between devices with their start and end apart: 12, of which 7 were waited for; matrix products, arithmetic and copies ran while one was open for 0% of the time, Pallas kernels for 5%

profile of v1, /device:TPU:1, one launch (start us, length us, event | category | flops | bytes accessed | tf_op | source)
XLA Modules:
  0.0 124.6 jit_solution(5112249101352157218)
XLA Ops:
  0.0 2.8 %copy.11 = bf16[1,32,64,256]{3,1,2,0:T(8,128)(2,1)} copy(bf16[1,32,64,256]{3,2,1,0:T(8,128)(2,1)} %param.6) | data formatting | bytes 2097152 | tf_op args[1]
  2.8 0.0 copy-start.1
  2.8 13.3 %all-to-all-start = ((bf16[64,32,256]{2,1,0:T(8,128)(2,1)}), bf16[64,32,256]{2,1,0:T(8,128)(2,1)S(1)}, u32[]{:S(2)}, u32[]{:S(2)}) async-start(bf16[64,32,256]{2,1,0:T(8,128)(2,1)} %bitcast.31), calls=%async_computation | async-start | bytes 2097152 | tf_op jit(solution)/shard_map/all_to_all | solution.py:219
  16.1 2.1 %pick_kernel.1 = (bf16[2,2,32,256]{3,2,1,0:T(8,128)(2,1)}, bf16[2,2,32,256]{3,2,1,0:T(8,128)(2,1)}) custom-call(f32[32,64,256]{2,1,0:T(8,128)} %est_ref.3), custom_call_target="tpu_custom_call" | custom-call | bytes 2097152 | tf_op jit(solution)/shard_map/pick_kernel/pallas_call | solution.py:202
  18.2 1.5 %collective-permute-start.1 = (bf16[2,2,32,256]{3,2,1,0:T(8,128)(2,1)}, bf16[2,2,32,256]{3,2,1,0:T(8,128)(2,1)S(1)}, u32[]{:S(2)}, u32[]{:S(2)}) collective-permute-start(bf16[2,2,32,256]{3,2,1,0:T(8,128)(2,1)} %get-tuple-element.7), channel_id=1, source_target_pairs={{0,0},{1,1},{2,2},{3,3},{4,4},{5,5},{6,6},{7,7},{8,8},{9,9},{10,10... | collective-permute-start | bytes 196616 | tf_op jit(solution)/shard_map/ppermute | solution.py:217
  19.7 2.9 %collective-permute-start.2 = (bf16[2,2,32,256]{3,2,1,0:T(8,128)(2,1)}, bf16[2,2,32,256]{3,2,1,0:T(8,128)(2,1)S(1)}, u32[]{:S(2)}, u32[]{:S(2)}) collective-permute-start(bf16[2,2,32,256]{3,2,1,0:T(8,128)(2,1)} %get-tuple-element.8), channel_id=1, source_target_pairs={{0,16},{1,17},{2,18},{3,19},{4,20},{5,21},{6,22},{7,23},{8,24},{9,... | collective-permute-start | bytes 196616 | tf_op jit(solution)/shard_map/ppermute | solution.py:217
  22.5 0.0 collective-permute-done.1
  22.5 3.2 %collective-permute-done.2 = bf16[2,2,32,256]{3,2,1,0:T(8,128)(2,1)S(1)} collective-permute-done((bf16[2,2,32,256]{3,2,1,0:T(8,128)(2,1)}, bf16[2,2,32,256]{3,2,1,0:T(8,128)(2,1)S(1)}, u32[]{:S(2)}, u32[]{:S(2)}) %collective-permute-start.2) | collective-permute-done | bytes 65568 | tf_op jit(solution)/shard_map/ppermute | solution.py:217
  25.8 1.4 %collective-permute-start.3 = (bf16[2,2,32,256]{3,2,1,0:T(8,128)(2,1)S(1)}, bf16[2,2,32,256]{3,2,1,0:T(8,128)(2,1)S(1)}, u32[]{:S(2)}, u32[]{:S(2)}) collective-permute-start(bf16[2,2,32,256]{3,2,1,0:T(8,128)(2,1)S(1)} %get-tuple-element.14), channel_id=1, source_target_pairs={{0,1},{1,0},{2,3},{3,2},{4,5},{5,4},{6,7},{7,6},{8,9},{9,8},{10,11... | collective-permute-start | bytes 196616 | tf_op jit(solution)/shard_map/ppermute | solution.py:224
  28.5 0.0 collective-permute-done.3
  28.5 26.9 %collective-permute-start.4 = (bf16[2,2,32,256]{3,2,1,0:T(8,128)(2,1)S(1)}, bf16[2,2,32,256]{3,2,1,0:T(8,128)(2,1)S(1)}, u32[]{:S(2)}, u32[]{:S(2)}) collective-permute-start(bf16[2,2,32,256]{3,2,1,0:T(8,128)(2,1)S(1)} %get-tuple-element.13), channel_id=1, source_target_pairs={{0,128},{128,0},{1,129},{129,1},{2,130},{130,2},{3,131},{131,3},{4... | collective-permute-start | bytes 196616 | tf_op jit(solution)/shard_map/ppermute | solution.py:228
  55.4 0.1 add_convert_fusion
  55.5 2.4 %collective-permute-done.4 = bf16[2,2,32,256]{3,2,1,0:T(8,128)(2,1)S(1)} collective-permute-done((bf16[2,2,32,256]{3,2,1,0:T(8,128)(2,1)S(1)}, bf16[2,2,32,256]{3,2,1,0:T(8,128)(2,1)S(1)}, u32[]{:S(2)}, u32[]{:S(2)}) %collective-permute-start.4) | collective-permute-done | bytes 65568 | tf_op jit(solution)/shard_map/ppermute | solution.py:228
  57.8 5.2 %collective-permute-start.7 = (bf16[2,2,2,32,256]{4,3,2,1,0:T(8,128)(2,1)S(1)}, bf16[2,2,2,32,256]{4,3,2,1,0:T(8,128)(2,1)S(1)}, u32[]{:S(2)}, u32[]{:S(2)}) collective-permute-start(bf16[2,2,2,32,256]{4,3,2,1,0:T(8,128)(2,1)S(1)} %pad_maximum_fusion.est0_ref), channel_id=1, source_target_pairs={{0,96},{32,0},{64,32},{96,64},{1,97},{33,1},{65,33},{97,65},{2,98}... | collective-permute-start | bytes 393224 | tf_op jit(solution)/shard_map/ppermute | solution.py:233
  63.0 0.0 collective-permute-start.6
  63.0 0.7 collective-permute-start.5
  63.7 0.0 copy-done.1
  63.7 0.4 collective-permute-start
  64.1 2.1 %collective-permute-done.other_ref.other_profile_ref = f32[1,384]{1,0:T(1,128)S(1)} collective-permute-done((f32[1,384]{1,0:T(1,128)S(1)}, f32[1,384]{1,0:T(1,128)S(1)}, u32[]{:S(2)}, u32[]{:S(2)}) %collective-permute-start) | collective-permute-done | bytes 1568 | tf_op jit(solution)/shard_map/ppermute | solution.py:198
  66.2 2.4 %collective-permute-done.7.est3_ref = bf16[2,2,2,32,256]{4,3,2,1,0:T(8,128)(2,1)S(1)} collective-permute-done((bf16[2,2,2,32,256]{4,3,2,1,0:T(8,128)(2,1)S(1)}, bf16[2,2,2,32,256]{4,3,2,1,0:T(8,128)(2,1)S(1)}, u32[]{:S(2)}, u32[]{:S(2)}) %collective-permute-start.7) | collective-permute-done | bytes 131104 | tf_op jit(solution)/shard_map/ppermute | solution.py:233
  68.6 0.0 collective-permute-done.6.est2_ref
  68.6 3.5 %collective-permute-done.5.est1_ref = bf16[2,2,2,32,256]{4,3,2,1,0:T(8,128)(2,1)S(1)} collective-permute-done((bf16[2,2,2,32,256]{4,3,2,1,0:T(8,128)(2,1)S(1)}, bf16[2,2,2,32,256]{4,3,2,1,0:T(8,128)(2,1)S(1)}, u32[]{:S(2)}, u32[]{:S(2)}) %collective-permute-start.5) | collective-permute-done | bytes 131104 | tf_op jit(solution)/shard_map/ppermute | solution.py:233
  72.2 3.9 %forward_kernel.1.inverse_ref = f32[2,1024,256]{2,1,0:T(8,128)S(1)} custom-call(s32[1]{0:T(128)S(6)} %copy.13.shift_ref, s32[1]{0:T(128)S(6)} %copy.12.offset_ref, f32[1,384]{1,0:T(1,128)S(1)} %collective-permute-done.other_ref.other_profile_ref, f32[1,256]{1,0:T(1,128)S(1)} %copy-done.1, f32[1,384]{1,0:T(1,128)S(1)} %collective-permute-done.other_ref.other_profile_ref, ...), custom_call_target="tpu_custom_call" | custom-call | flops 268435456 | bytes 8388608 | tf_op jit(solution)/shard_map/forward_kernel/pallas_call | solution.py:235
  76.0 0.0 all-to-all-done.image_ref
  76.0 5.6 %back_kernel.1 = s16[4,32,8,256]{3,2,1,0:T(8,128)(2,1)S(1)} custom-call(s32[1]{0:T(128)S(6)} %copy.13.shift_ref, s32[1]{0:T(128)S(6)} %copy.12.offset_ref, f32[1,384]{1,0:T(1,128)S(1)} %collective-permute-done.other_ref.other_profile_ref, f32[1,256]{1,0:T(1,128)S(1)} %copy-done.1, f32[1,384]{1,0:T(1,128)S(1)} %collective-permute-done.other_ref.other_profile_ref, ...), custom_call_target="tpu_custom_call" | custom-call | tf_op jit(solution)/shard_map/back_kernel/pallas_call | solution.py:247
  81.7 0.1 collective-permute-start.8
  81.8 0.2 collective-permute-start.10
  82.0 0.0 copy-start
  82.0 1.3 %collective-permute-start.9 = (s16[32,8,256]{2,1,0:T(8,128)(2,1)S(1)}, s16[32,8,256]{2,1,0:T(8,128)(2,1)S(1)}, u32[]{:S(2)}, u32[]{:S(2)}) collective-permute-start(s16[32,8,256]{2,1,0:T(8,128)(2,1)S(1)} %get-tuple-element.11), channel_id=1, source_target_pairs={{0,32},{32,64},{64,96},{96,0},{1,33},{33,65},{65,97},{97,1},{2,34}... | collective-permute-start | bytes 393224 | tf_op jit(solution)/shard_map/ppermute | solution.py:259
  83.4 4.2 %collective-permute-done.8 = s16[32,8,256]{2,1,0:T(8,128)(2,1)S(1)} collective-permute-done((s16[32,8,256]{2,1,0:T(8,128)(2,1)S(1)}, s16[32,8,256]{2,1,0:T(8,128)(2,1)S(1)}, u32[]{:S(2)}, u32[]{:S(2)}) %collective-permute-start.8) | collective-permute-done | bytes 131104 | tf_op jit(solution)/shard_map/ppermute | solution.py:259
  87.6 0.0 collective-permute-done.10
  87.6 3.5 %collective-permute-done.9 = s16[32,8,256]{2,1,0:T(8,128)(2,1)S(1)} collective-permute-done((s16[32,8,256]{2,1,0:T(8,128)(2,1)S(1)}, s16[32,8,256]{2,1,0:T(8,128)(2,1)S(1)}, u32[]{:S(2)}, u32[]{:S(2)}) %collective-permute-start.9) | collective-permute-done | bytes 131104 | tf_op jit(solution)/shard_map/ppermute | solution.py:259
  91.1 0.2 fusion.4
  91.2 14.2 %all_to_all.15 = s16[32,8,256]{2,1,0:T(8,128)(2,1)S(1)} all-to-all(s16[32,8,256]{2,1,0:T(8,128)(2,1)S(1)} %fusion.4), channel_id=1, replica_groups=mesh['upper'=2,'column'=4,'tile'=32] {'tile'}, dimensions={0} | all-to-all | bytes 262144 | tf_op jit(solution)/shard_map/all_to_all | solution.py:261
  105.4 0.1 broadcast_in_dim.10
  105.6 17.0 %all_to_all.16 = s16[8,8,32,256]{3,2,1,0:T(8,128)(2,1)S(1)} all-to-all(s16[8,8,32,256]{3,2,1,0:T(8,128)(2,1)S(1)} %broadcast_in_dim.10), channel_id=1, replica_groups=mesh['upper'=2,'column'=4,'tile'=32] {'upper','column'}, dimensions={0} | all-to-all | bytes 2097152 | tf_op jit(solution)/shard_map/all_to_all | solution.py:263
  122.6 0.0 copy-done
  122.6 2.0 %final_kernel.1 = f32[32,64,256]{2,1,0:T(8,128)} custom-call(f32[32,64,256]{2,1,0:T(8,128)S(1)} %copy-done, s16[2,4,8,32,256]{4,3,2,1,0:T(8,128)(2,1)S(1)} %bitcast.32), custom_call_target="tpu_custom_call" | custom-call | tf_op jit(solution)/shard_map/final_kernel/pallas_call | solution.py:265
  (7 shorter events, 0.1 us)
Async XLA Ops:
  2.8 60.9 %copy-start.1 = (f32[1,256]{1,0:T(1,128)S(1)}, f32[1,256]{1,0:T(1,128)}, u32[]{:S(2)}) copy-start(f32[1,256]{1,0:T(1,128)} %own_profile_ref.3) | copy-start | bytes 3076
  2.8 73.3 %all-to-all-start = ((bf16[64,32,256]{2,1,0:T(8,128)(2,1)}), bf16[64,32,256]{2,1,0:T(8,128)(2,1)S(1)}, u32[]{:S(2)}, u32[]{:S(2)}) async-start(bf16[64,32,256]{2,1,0:T(8,128)(2,1)} %bitcast.31), calls=%async_computation | async-start | bytes 2097152 | tf_op jit(solution)/shard_map/all_to_all | solution.py:219
  18.2 4.4 %collective-permute-start.1 = (bf16[2,2,32,256]{3,2,1,0:T(8,128)(2,1)}, bf16[2,2,32,256]{3,2,1,0:T(8,128)(2,1)S(1)}, u32[]{:S(2)}, u32[]{:S(2)}) collective-permute-start(bf16[2,2,32,256]{3,2,1,0:T(8,128)(2,1)} %get-tuple-element.7), channel_id=1, source_target_pairs={{0,0},{1,1},{2,2},{3,3},{4,4},{5,5},{6,6},{7,7},{8,8},{9,9},{10,10... | collective-permute-start | bytes 196616 | tf_op jit(solution)/shard_map/ppermute | solution.py:217
  19.7 6.1 %collective-permute-start.2 = (bf16[2,2,32,256]{3,2,1,0:T(8,128)(2,1)}, bf16[2,2,32,256]{3,2,1,0:T(8,128)(2,1)S(1)}, u32[]{:S(2)}, u32[]{:S(2)}) collective-permute-start(bf16[2,2,32,256]{3,2,1,0:T(8,128)(2,1)} %get-tuple-element.8), channel_id=1, source_target_pairs={{0,16},{1,17},{2,18},{3,19},{4,20},{5,21},{6,22},{7,23},{8,24},{9,... | collective-permute-start | bytes 196616 | tf_op jit(solution)/shard_map/ppermute | solution.py:217
  25.8 2.7 %collective-permute-start.3 = (bf16[2,2,32,256]{3,2,1,0:T(8,128)(2,1)S(1)}, bf16[2,2,32,256]{3,2,1,0:T(8,128)(2,1)S(1)}, u32[]{:S(2)}, u32[]{:S(2)}) collective-permute-start(bf16[2,2,32,256]{3,2,1,0:T(8,128)(2,1)S(1)} %get-tuple-element.14), channel_id=1, source_target_pairs={{0,1},{1,0},{2,3},{3,2},{4,5},{5,4},{6,7},{7,6},{8,9},{9,8},{10,11... | collective-permute-start | bytes 196616 | tf_op jit(solution)/shard_map/ppermute | solution.py:224
  28.5 29.3 %collective-permute-start.4 = (bf16[2,2,32,256]{3,2,1,0:T(8,128)(2,1)S(1)}, bf16[2,2,32,256]{3,2,1,0:T(8,128)(2,1)S(1)}, u32[]{:S(2)}, u32[]{:S(2)}) collective-permute-start(bf16[2,2,32,256]{3,2,1,0:T(8,128)(2,1)S(1)} %get-tuple-element.13), channel_id=1, source_target_pairs={{0,128},{128,0},{1,129},{129,1},{2,130},{130,2},{3,131},{131,3},{4... | collective-permute-start | bytes 196616 | tf_op jit(solution)/shard_map/ppermute | solution.py:228
  57.8 10.8 %collective-permute-start.7 = (bf16[2,2,2,32,256]{4,3,2,1,0:T(8,128)(2,1)S(1)}, bf16[2,2,2,32,256]{4,3,2,1,0:T(8,128)(2,1)S(1)}, u32[]{:S(2)}, u32[]{:S(2)}) collective-permute-start(bf16[2,2,2,32,256]{4,3,2,1,0:T(8,128)(2,1)S(1)} %pad_maximum_fusion.est0_ref), channel_id=1, source_target_pairs={{0,96},{32,0},{64,32},{96,64},{1,97},{33,1},{65,33},{97,65},{2,98}... | collective-permute-start | bytes 393224 | tf_op jit(solution)/shard_map/ppermute | solution.py:233
  63.0 5.6 %collective-permute-start.6 = (bf16[2,2,2,32,256]{4,3,2,1,0:T(8,128)(2,1)S(1)}, bf16[2,2,2,32,256]{4,3,2,1,0:T(8,128)(2,1)S(1)}, u32[]{:S(2)}, u32[]{:S(2)}) collective-permute-start(bf16[2,2,2,32,256]{4,3,2,1,0:T(8,128)(2,1)S(1)} %pad_maximum_fusion.est0_ref), channel_id=1, source_target_pairs={{0,64},{32,96},{64,0},{96,32},{1,65},{33,97},{65,1},{97,33},{2,66}... | collective-permute-start | bytes 393224 | tf_op jit(solution)/shard_map/ppermute | solution.py:233
  63.0 9.1 %collective-permute-start.5 = (bf16[2,2,2,32,256]{4,3,2,1,0:T(8,128)(2,1)S(1)}, bf16[2,2,2,32,256]{4,3,2,1,0:T(8,128)(2,1)S(1)}, u32[]{:S(2)}, u32[]{:S(2)}) collective-permute-start(bf16[2,2,2,32,256]{4,3,2,1,0:T(8,128)(2,1)S(1)} %pad_maximum_fusion.est0_ref), channel_id=1, source_target_pairs={{0,32},{32,64},{64,96},{96,0},{1,33},{33,65},{65,97},{97,1},{2,34}... | collective-permute-start | bytes 393224 | tf_op jit(solution)/shard_map/ppermute | solution.py:233
  63.7 2.5 %collective-permute-start = (f32[1,384]{1,0:T(1,128)S(1)}, f32[1,384]{1,0:T(1,128)S(1)}, u32[]{:S(2)}, u32[]{:S(2)}) collective-permute-start(f32[1,384]{1,0:T(1,128)S(1)} %pad_maximum_fusion.1), channel_id=1, source_target_pairs={{0,128},{128,0},{1,129},{129,1},{2,130},{130,2},{3,131},{131,3},{4... | collective-permute-start | bytes 4616 | tf_op jit(solution)/shard_map/ppermute | solution.py:198
  81.7 5.9 %collective-permute-start.8 = (s16[32,8,256]{2,1,0:T(8,128)(2,1)S(1)}, s16[32,8,256]{2,1,0:T(8,128)(2,1)S(1)}, u32[]{:S(2)}, u32[]{:S(2)}) collective-permute-start(s16[32,8,256]{2,1,0:T(8,128)(2,1)S(1)} %get-tuple-element.9), channel_id=1, source_target_pairs={{0,64},{32,96},{64,0},{96,32},{1,65},{33,97},{65,1},{97,33},{2,66}... | collective-permute-start | bytes 393224 | tf_op jit(solution)/shard_map/ppermute | solution.py:259
  81.8 5.8 %collective-permute-start.10 = (s16[32,8,256]{2,1,0:T(8,128)(2,1)S(1)}, s16[32,8,256]{2,1,0:T(8,128)(2,1)S(1)}, u32[]{:S(2)}, u32[]{:S(2)}) collective-permute-start(s16[32,8,256]{2,1,0:T(8,128)(2,1)S(1)} %get-tuple-element.10), channel_id=1, source_target_pairs={{0,96},{32,0},{64,32},{96,64},{1,97},{33,1},{65,33},{97,65},{2,98}... | collective-permute-start | bytes 393224 | tf_op jit(solution)/shard_map/ppermute | solution.py:259
  82.0 40.5 %copy-start = (f32[32,64,256]{2,1,0:T(8,128)S(1)}, f32[32,64,256]{2,1,0:T(8,128)}, u32[]{:S(2)}) copy-start(f32[32,64,256]{2,1,0:T(8,128)} %est_ref.3) | copy-start | bytes 6291460
  82.0 9.0 %collective-permute-start.9 = (s16[32,8,256]{2,1,0:T(8,128)(2,1)S(1)}, s16[32,8,256]{2,1,0:T(8,128)(2,1)S(1)}, u32[]{:S(2)}, u32[]{:S(2)}) collective-permute-start(s16[32,8,256]{2,1,0:T(8,128)(2,1)S(1)} %get-tuple-element.11), channel_id=1, source_target_pairs={{0,32},{32,64},{64,96},{96,0},{1,33},{33,65},{65,97},{97,1},{2,34}... | collective-permute-start | bytes 393224 | tf_op jit(solution)/shard_map/ppermute | solution.py:259

commit v2 on v1

--- a/solution.py
+++ b/solution.py
@@ -39,7 +39,7 @@
     return lax.axis_index("upper"), lax.axis_index("column"), tile
 
 
-def pick_kernel(est_ref, out0_ref, out1_ref, lines_ref, sem):
+def pick_kernel(est_ref, out_ref, lines_ref, sem):
     upper, column, tile = place()
     tile_y, tile_z = lax.div(tile, 16), lax.rem(lax.div(tile, 2), 8)
     z = lax.rem(tile_z + column + 4 * upper, 8)
@@ -55,15 +55,14 @@
                 )
                 copy.start()
                 copies.append(copy)
-    for copy in copies:
-        copy.wait()
     rows_ref = lines_ref.reshape(2, 2, 2, ROWS * 8, 128)
-    for k, out_ref in enumerate((out0_ref, out1_ref)):
+    for k in range(2):
         for u in range(2):
             for h in range(2):
+                copies[4 * k + 2 * u + h].wait()
                 for c in range(2):
                     rows = rows_ref[k, u, h, pl.ds(2 * lax.rem(z, 4) + c, ROWS, stride=8)]
-                    out_ref[u, c, :, pl.ds(128 * h, 128)] = rows.astype(jnp.bfloat16)
+                    out_ref[c, k, u, :, pl.ds(128 * h, 128)] = rows.astype(jnp.bfloat16)
 
 
 def forward_kernel(
@@ -82,7 +81,7 @@
                 for k in range(2):
                     slab = 16 * lax.rem(tile_y + k, 2) + 2 * z + lax.rem(core + c, 2)
                     base = pl.multiple_of(slab * ROWS + 8, 8)
-                    e_ref[pl.ds(base, ROWS)] = est_ref[u, c, k].astype(jnp.float32)
+                    e_ref[pl.ds(base, ROWS)] = est_ref[u, k, c].astype(jnp.float32)
     e_ref[pl.ds(0, 8)] = e_ref[pl.ds(TOTAL, 8)]
     e_ref[pl.ds(TOTAL + 8, 16)] = e_ref[pl.ds(8, 16)]
     row = lax.broadcasted_iota(jnp.int32, (1, 8, LENGTH), 1)
@@ -175,15 +174,21 @@
         out_ref[:, lines] = est_ref[:, lines] * jnp.exp(logs)
 
 
-def distance_route(k):
+def distance_route():
     route = []
     for v in range(8):
         for y in range(2):
             for z in range(8):
                 for c in range(2):
-                    target = 16 * ((y + k) % 2) + 2 * ((z + v) % 8) + c
+                    target = 16 * y + 2 * ((z + v) % 8) + c
                     route.append((32 * v + 16 * y + 2 * z + c, 32 * v + target))
     return route
+
+
+def swap_halves(block, axis, route, keep):
+    mine = lax.dynamic_index_in_dim(block, keep, 0, keepdims=False)
+    given = lax.dynamic_index_in_dim(block, 1 - keep, 0, keepdims=False)
+    return mine, lax.ppermute(given, axis, route)
 
 
 VMEM = pl.BlockSpec(memory_space=pltpu.VMEM)
@@ -198,12 +203,11 @@
     other = lax.ppermute(info, "upper", swap)
 
     tile = lax.axis_index("tile")
-    core = tile % 2
-    chips = pl.pallas_call(
+    chip = pl.pallas_call(
         pick_kernel,
-        out_shape=[jax.ShapeDtypeStruct((2, 2, ROWS, LENGTH), jnp.bfloat16)] * 2,
+        out_shape=jax.ShapeDtypeStruct((2, 2, 2, ROWS, LENGTH), jnp.bfloat16),
         in_specs=[pl.BlockSpec(memory_space=pl.ANY)],
-        out_specs=[VMEM] * 2,
+        out_specs=VMEM,
         scratch_shapes=[
             pltpu.VMEM((2, 2, 2, ROWS, 8, 128), jnp.float32),
             pltpu.SemaphoreType.DMA((2, 2, 2)),
@@ -212,21 +216,17 @@
         compiler_params=pltpu.CompilerParams(vmem_limit_bytes=125 << 19),
         name="pick_kernel",
     )(estimate)
-    arrived = []
-    for k, chip in enumerate(chips):
-        arrived.append(lax.ppermute(chip, ("upper", "column", "tile"), distance_route(k)))
+    block = lax.ppermute(chip, ("upper", "column", "tile"), distance_route())
     image = measured[0].transpose(1, 0, 2)
     image_lines = lax.all_to_all(image, ("upper", "tile"), 0, 0, tiled=True)
 
-    arrived = jnp.stack(arrived, axis=0)
-    mine = lax.dynamic_index_in_dim(arrived, core, 2, keepdims=False)
-    given = lax.dynamic_index_in_dim(arrived, 1 - core, 2, keepdims=False)
-    given = lax.ppermute(given, "tile", [(i, i ^ 1) for i in range(32)])
-    both = jnp.stack([mine, given])
-    mine = lax.dynamic_index_in_dim(both, upper, 2, keepdims=False)
-    given = lax.dynamic_index_in_dim(both, 1 - upper, 2, keepdims=False)
-    given = lax.ppermute(given, "upper", swap)
-    piece = jnp.stack([mine, given])
+    pair = swap_halves(block, "tile", [(i, i ^ 1) for i in range(32)], tile % 2)
+    block = jnp.stack(pair, axis=2)
+    mine, given = block[0], block[1]
+    given = lax.ppermute(given, "tile", [(i, i ^ 16) for i in range(32)])
+    block = jnp.stack([mine, given], axis=1)
+    pair = swap_halves(block, "upper", swap, upper)
+    piece = jnp.stack(pair)
     est_lines = [piece]
     for d in (1, 2, 3):
         route = [(i, (i + d) % 4) for i in range(4)]

time: 125 us -> 128 us (1.024)
  blocking collectives: 31.2 us -> 38.5 us
  waiting for transfers between devices: 21.4 us -> 14.7 us
  starting transfers between devices: 53.8 us -> 56.3 us
    all_to_all x1, blocking collectives: 14.2 us -> 21.5 us  [update(): logs = lax.all_to_all(logs, 'tile', 0, 0, tiled=True)]
    ppermute x4, starting transfers between devices: 32.6 us -> 36 us  [the longest x2 31.5 us: swap_halves(): return (mine, lax.ppermute(given, axis, route))]
    ppermute x3, waiting for transfers between devices: 7.7 us -> 4.91 us  [update(): total += lax.ppermute(codes[d], 'column', route).astype(jnp.int32)]
    ppermute x3, waiting for transfers between devices: 5.94 us -> 3.23 us  [update(): est_lines.append(lax.ppermute(piece, 'column', route))]
    ppermute x4, waiting for transfers between devices: 5.59 us -> 4.17 us  [the longest x2 2.48 us: swap_halves(): return (mine, lax.ppermute(given, axis, route))]
  transfers between devices with their start and end apart: 12 -> 12, of which waited for: 7 -> 9; matrix products, arithmetic and copies ran while one was open for 0% -> 0% of each run, Pallas kernels for 5% -> 5%
where the time goes in v2:
time: 128 us
  starting transfers between devices  56.3 us (44%)
  blocking collectives  38.5 us (30%)
  waiting for transfers between devices  14.7 us (11%)
  Pallas kernels  13.6 us (11%)
  local copies, waits for them, and re-layouts  2.97 us (2%)
  between operations  1.41 us (1%)
    ppermute x2, starting transfers between devices, swap_halves(): return (mine, lax.ppermute(given, axis, route))  31.5 us
    all_to_all x1, blocking collectives, update(): logs = lax.all_to_all(logs, 'tile', 0, 0, tiled=True)  21.5 us
    all_to_all x1, blocking collectives, update(): logs = lax.all_to_all(logs, ('upper', 'column'), 0, 0, tiled=True)  17 us
    all_to_all x1, starting transfers between devices, update(): image_lines = lax.all_to_all(image, ('upper', 'tile'), 0, 0, tiled=True)  13.1 us
    pallas_call x1, Pallas kernels, update(): pl.pallas_call(back_kernel, out_shape=jax.ShapeDtypeStruct((4, SLABS, 8,...  5.65 us
    ppermute x3, starting transfers between devices, update(): est_lines.append(lax.ppermute(piece, 'column', route))  5.19 us
    ppermute x3, waiting for transfers between devices, update(): total += lax.ppermute(codes[d], 'column', route).astype(jnp.int32)  4.91 us
    pallas_call x1, Pallas kernels, update(): pl.pallas_call(forward_kernel, out_shape=jax.ShapeDtypeStruct((2, TOTAL,...  3.87 us
  transfers between devices with their start and end apart: 12, of which 9 were waited for; matrix products, arithmetic and copies ran while one was open for 0% of the time, Pallas kernels for 5%

profile of v2, /device:TPU:1, one launch (start us, length us, event | category | flops | bytes accessed | tf_op | source)
XLA Modules:
  0.0 127.8 jit_solution(799405767174174796)
XLA Ops:
  0.0 2.8 %copy.10 = bf16[1,32,64,256]{3,1,2,0:T(8,128)(2,1)} copy(bf16[1,32,64,256]{3,2,1,0:T(8,128)(2,1)} %param.6) | data formatting | bytes 2097152 | tf_op args[1]
  2.8 13.1 %all-to-all-start = ((bf16[64,32,256]{2,1,0:T(8,128)(2,1)}), bf16[64,32,256]{2,1,0:T(8,128)(2,1)S(1)}, u32[]{:S(2)}, u32[]{:S(2)}) async-start(bf16[64,32,256]{2,1,0:T(8,128)(2,1)} %bitcast.34), calls=%async_computation | async-start | bytes 2097152 | tf_op jit(solution)/shard_map/all_to_all | solution.py:221
  15.9 0.0 copy-start.1
  15.9 2.1 %pick_kernel.1 = bf16[2,2,2,32,256]{4,3,2,1,0:T(8,128)(2,1)} custom-call(f32[32,64,256]{2,1,0:T(8,128)} %est_ref.3), custom_call_target="tpu_custom_call" | custom-call | bytes 2097152 | tf_op jit(solution)/shard_map/pick_kernel/pallas_call | solution.py:206
  18.0 1.6 %collective-permute-start.1 = (bf16[2,2,2,32,256]{4,3,2,1,0:T(8,128)(2,1)}, bf16[2,2,2,32,256]{4,3,2,1,0:T(8,128)(2,1)S(1)}, u32[]{:S(2)}, u32[]{:S(2)}) collective-permute-start(bf16[2,2,2,32,256]{4,3,2,1,0:T(8,128)(2,1)} %pick_kernel.1), channel_id=1, source_target_pairs={{0,0},{1,1},{2,2},{3,3},{4,4},{5,5},{6,6},{7,7},{8,8},{9,9},{10,10... | collective-permute-start | bytes 393224 | tf_op jit(solution)/shard_map/ppermute | solution.py:219
  19.6 0.0 collective-permute-done.1
  19.6 0.5 collective-permute-start.2
  20.1 0.9 collective-permute-done.2
  21.1 2.9 %collective-permute-start.3 = (bf16[2,2,32,256]{3,2,1,0:T(8,128)(2,1)S(1)}, bf16[2,2,32,256]{3,2,1,0:T(8,128)(2,1)S(1)}, u32[]{:S(2)}, u32[]{:S(2)}) collective-permute-start(bf16[2,2,32,256]{3,2,1,0:T(8,128)(2,1)S(1)} %get-tuple-element.10), channel_id=1, source_target_pairs={{0,16},{1,17},{2,18},{3,19},{4,20},{5,21},{6,22},{7,23},{8,24},{9,... | collective-permute-start | bytes 196616 | tf_op jit(solution)/shard_map/ppermute | solution.py:226
  25.2 1.7 %collective-permute-done.3 = bf16[2,2,32,256]{3,2,1,0:T(8,128)(2,1)S(1)} collective-permute-done((bf16[2,2,32,256]{3,2,1,0:T(8,128)(2,1)S(1)}, bf16[2,2,32,256]{3,2,1,0:T(8,128)(2,1)S(1)}, u32[]{:S(2)}, u32[]{:S(2)}) %collective-permute-start.3) | collective-permute-done | bytes 65568 | tf_op jit(solution)/shard_map/ppermute | solution.py:226
  26.9 31.0 %collective-permute-start.4 = (bf16[2,2,32,256]{3,2,1,0:T(8,128)(2,1)S(1)}, bf16[2,2,32,256]{3,2,1,0:T(8,128)(2,1)S(1)}, u32[]{:S(2)}, u32[]{:S(2)}) collective-permute-start(bf16[2,2,32,256]{3,2,1,0:T(8,128)(2,1)S(1)} %get-tuple-element.9), channel_id=1, source_target_pairs={{0,128},{128,0},{1,129},{129,1},{2,130},{130,2},{3,131},{131,3},{4... | collective-permute-start | bytes 196616 | tf_op jit(solution)/shard_map/ppermute | solution.py:191
  57.9 0.1 add_convert_fusion
  58.0 1.6 %collective-permute-done.4 = bf16[2,2,32,256]{3,2,1,0:T(8,128)(2,1)S(1)} collective-permute-done((bf16[2,2,32,256]{3,2,1,0:T(8,128)(2,1)S(1)}, bf16[2,2,32,256]{3,2,1,0:T(8,128)(2,1)S(1)}, u32[]{:S(2)}, u32[]{:S(2)}) %collective-permute-start.4) | collective-permute-done | bytes 65568 | tf_op jit(solution)/shard_map/ppermute | solution.py:191
  59.6 4.5 %collective-permute-start.7 = (bf16[2,2,2,32,256]{4,3,2,1,0:T(8,128)(2,1)S(1)}, bf16[2,2,2,32,256]{4,3,2,1,0:T(8,128)(2,1)S(1)}, u32[]{:S(2)}, u32[]{:S(2)}) collective-permute-start(bf16[2,2,2,32,256]{4,3,2,1,0:T(8,128)(2,1)S(1)} %pad_maximum_fusion.est0_ref), channel_id=1, source_target_pairs={{0,96},{32,0},{64,32},{96,64},{1,97},{33,1},{65,33},{97,65},{2,98}... | collective-permute-start | bytes 393224 | tf_op jit(solution)/shard_map/ppermute | solution.py:233
  64.1 0.0 collective-permute-start.6
  64.1 0.7 collective-permute-start.5
  64.8 0.0 copy-done.1
  64.8 0.1 collective-permute-start
  64.9 2.4 %collective-permute-done.other_ref.other_profile_ref = f32[1,384]{1,0:T(1,128)S(1)} collective-permute-done((f32[1,384]{1,0:T(1,128)S(1)}, f32[1,384]{1,0:T(1,128)S(1)}, u32[]{:S(2)}, u32[]{:S(2)}) %collective-permute-start) | collective-permute-done | bytes 1568 | tf_op jit(solution)/shard_map/ppermute | solution.py:203
  67.3 0.1 collective-permute-done.7.est3_ref
  67.4 2.1 %collective-permute-done.6.est2_ref = bf16[2,2,2,32,256]{4,3,2,1,0:T(8,128)(2,1)S(1)} collective-permute-done((bf16[2,2,2,32,256]{4,3,2,1,0:T(8,128)(2,1)S(1)}, bf16[2,2,2,32,256]{4,3,2,1,0:T(8,128)(2,1)S(1)}, u32[]{:S(2)}, u32[]{:S(2)}) %collective-permute-start.6) | collective-permute-done | bytes 131104 | tf_op jit(solution)/shard_map/ppermute | solution.py:233
  69.5 1.0 collective-permute-done.5.est1_ref
  70.6 3.9 %forward_kernel.1.inverse_ref = f32[2,1024,256]{2,1,0:T(8,128)S(1)} custom-call(s32[1]{0:T(128)S(6)} %copy.12.shift_ref, s32[1]{0:T(128)S(6)} %copy.11.offset_ref, f32[1,384]{1,0:T(1,128)S(1)} %collective-permute-done.other_ref.other_profile_ref, f32[1,256]{1,0:T(1,128)S(1)} %copy-done.1, f32[1,384]{1,0:T(1,128)S(1)} %collective-permute-done.other_ref.other_profile_ref, ...), custom_call_target="tpu_custom_call" | custom-call | flops 268435456 | bytes 8388608 | tf_op jit(solution)/shard_map/forward_kernel/pallas_call | solution.py:235
  74.4 0.0 all-to-all-done.image_ref
  74.4 5.6 %back_kernel.1 = s16[4,32,8,256]{3,2,1,0:T(8,128)(2,1)S(1)} custom-call(s32[1]{0:T(128)S(6)} %copy.12.shift_ref, s32[1]{0:T(128)S(6)} %copy.11.offset_ref, f32[1,384]{1,0:T(1,128)S(1)} %collective-permute-done.other_ref.other_profile_ref, f32[1,256]{1,0:T(1,128)S(1)} %copy-done.1, f32[1,384]{1,0:T(1,128)S(1)} %collective-permute-done.other_ref.other_profile_ref, ...), custom_call_target="tpu_custom_call" | custom-call | tf_op jit(solution)/shard_map/back_kernel/pallas_call | solution.py:247
  80.1 0.4 collective-permute-start.8
  80.6 0.8 collective-permute-start.10
  81.4 0.0 copy-start
  81.4 0.6 collective-permute-start.9
  82.0 3.6 %collective-permute-done.8 = s16[32,8,256]{2,1,0:T(8,128)(2,1)S(1)} collective-permute-done((s16[32,8,256]{2,1,0:T(8,128)(2,1)S(1)}, s16[32,8,256]{2,1,0:T(8,128)(2,1)S(1)}, u32[]{:S(2)}, u32[]{:S(2)}) %collective-permute-start.8) | collective-permute-done | bytes 131104 | tf_op jit(solution)/shard_map/ppermute | solution.py:259
  85.6 0.0 collective-permute-done.10
  85.6 1.3 %collective-permute-done.9 = s16[32,8,256]{2,1,0:T(8,128)(2,1)S(1)} collective-permute-done((s16[32,8,256]{2,1,0:T(8,128)(2,1)S(1)}, s16[32,8,256]{2,1,0:T(8,128)(2,1)S(1)}, u32[]{:S(2)}, u32[]{:S(2)}) %collective-permute-start.9) | collective-permute-done | bytes 131104 | tf_op jit(solution)/shard_map/ppermute | solution.py:259
  86.9 0.2 fusion.4
  87.1 21.5 %all_to_all.15 = s16[32,8,256]{2,1,0:T(8,128)(2,1)S(1)} all-to-all(s16[32,8,256]{2,1,0:T(8,128)(2,1)S(1)} %fusion.4), channel_id=1, replica_groups=mesh['upper'=2,'column'=4,'tile'=32] {'tile'}, dimensions={0} | all-to-all | bytes 262144 | tf_op jit(solution)/shard_map/all_to_all | solution.py:261
  108.7 0.1 broadcast_in_dim.10
  108.8 17.0 %all_to_all.16 = s16[8,8,32,256]{3,2,1,0:T(8,128)(2,1)S(1)} all-to-all(s16[8,8,32,256]{3,2,1,0:T(8,128)(2,1)S(1)} %broadcast_in_dim.10), channel_id=1, replica_groups=mesh['upper'=2,'column'=4,'tile'=32] {'upper','column'}, dimensions={0} | all-to-all | bytes 2097152 | tf_op jit(solution)/shard_map/all_to_all | solution.py:263
  125.8 0.0 copy-done
  125.8 2.1 %final_kernel.1 = f32[32,64,256]{2,1,0:T(8,128)} custom-call(f32[32,64,256]{2,1,0:T(8,128)S(1)} %copy-done, s16[2,4,8,32,256]{4,3,2,1,0:T(8,128)(2,1)S(1)} %bitcast.35), custom_call_target="tpu_custom_call" | custom-call | tf_op jit(solution)/shard_map/final_kernel/pallas_call | solution.py:265
  (8 shorter events, 0.1 us)
Async XLA Ops:
  2.8 71.7 %all-to-all-start = ((bf16[64,32,256]{2,1,0:T(8,128)(2,1)}), bf16[64,32,256]{2,1,0:T(8,128)(2,1)S(1)}, u32[]{:S(2)}, u32[]{:S(2)}) async-start(bf16[64,32,256]{2,1,0:T(8,128)(2,1)} %bitcast.34), calls=%async_computation | async-start | bytes 2097152 | tf_op jit(solution)/shard_map/all_to_all | solution.py:221
  15.9 48.9 %copy-start.1 = (f32[1,256]{1,0:T(1,128)S(1)}, f32[1,256]{1,0:T(1,128)}, u32[]{:S(2)}) copy-start(f32[1,256]{1,0:T(1,128)} %own_profile_ref.3) | copy-start | bytes 3076
  18.0 1.6 %collective-permute-start.1 = (bf16[2,2,2,32,256]{4,3,2,1,0:T(8,128)(2,1)}, bf16[2,2,2,32,256]{4,3,2,1,0:T(8,128)(2,1)S(1)}, u32[]{:S(2)}, u32[]{:S(2)}) collective-permute-start(bf16[2,2,2,32,256]{4,3,2,1,0:T(8,128)(2,1)} %pick_kernel.1), channel_id=1, source_target_pairs={{0,0},{1,1},{2,2},{3,3},{4,4},{5,5},{6,6},{7,7},{8,8},{9,9},{10,10... | collective-permute-start | bytes 393224 | tf_op jit(solution)/shard_map/ppermute | solution.py:219
  19.6 1.4 %collective-permute-start.2 = (bf16[2,2,32,256]{3,2,1,0:T(8,128)(2,1)S(1)}, bf16[2,2,32,256]{3,2,1,0:T(8,128)(2,1)S(1)}, u32[]{:S(2)}, u32[]{:S(2)}) collective-permute-start(bf16[2,2,32,256]{3,2,1,0:T(8,128)(2,1)S(1)} %get-tuple-element.12), channel_id=1, source_target_pairs={{0,1},{1,0},{2,3},{3,2},{4,5},{5,4},{6,7},{7,6},{8,9},{9,8},{10,11... | collective-permute-start | bytes 196616 | tf_op jit(solution)/shard_map/ppermute | solution.py:191
  21.1 5.9 %collective-permute-start.3 = (bf16[2,2,32,256]{3,2,1,0:T(8,128)(2,1)S(1)}, bf16[2,2,32,256]{3,2,1,0:T(8,128)(2,1)S(1)}, u32[]{:S(2)}, u32[]{:S(2)}) collective-permute-start(bf16[2,2,32,256]{3,2,1,0:T(8,128)(2,1)S(1)} %get-tuple-element.10), channel_id=1, source_target_pairs={{0,16},{1,17},{2,18},{3,19},{4,20},{5,21},{6,22},{7,23},{8,24},{9,... | collective-permute-start | bytes 196616 | tf_op jit(solution)/shard_map/ppermute | solution.py:226
  26.9 32.6 %collective-permute-start.4 = (bf16[2,2,32,256]{3,2,1,0:T(8,128)(2,1)S(1)}, bf16[2,2,32,256]{3,2,1,0:T(8,128)(2,1)S(1)}, u32[]{:S(2)}, u32[]{:S(2)}) collective-permute-start(bf16[2,2,32,256]{3,2,1,0:T(8,128)(2,1)S(1)} %get-tuple-element.9), channel_id=1, source_target_pairs={{0,128},{128,0},{1,129},{129,1},{2,130},{130,2},{3,131},{131,3},{4... | collective-permute-start | bytes 196616 | tf_op jit(solution)/shard_map/ppermute | solution.py:191
  59.6 7.8 %collective-permute-start.7 = (bf16[2,2,2,32,256]{4,3,2,1,0:T(8,128)(2,1)S(1)}, bf16[2,2,2,32,256]{4,3,2,1,0:T(8,128)(2,1)S(1)}, u32[]{:S(2)}, u32[]{:S(2)}) collective-permute-start(bf16[2,2,2,32,256]{4,3,2,1,0:T(8,128)(2,1)S(1)} %pad_maximum_fusion.est0_ref), channel_id=1, source_target_pairs={{0,96},{32,0},{64,32},{96,64},{1,97},{33,1},{65,33},{97,65},{2,98}... | collective-permute-start | bytes 393224 | tf_op jit(solution)/shard_map/ppermute | solution.py:233
  64.1 5.4 %collective-permute-start.6 = (bf16[2,2,2,32,256]{4,3,2,1,0:T(8,128)(2,1)S(1)}, bf16[2,2,2,32,256]{4,3,2,1,0:T(8,128)(2,1)S(1)}, u32[]{:S(2)}, u32[]{:S(2)}) collective-permute-start(bf16[2,2,2,32,256]{4,3,2,1,0:T(8,128)(2,1)S(1)} %pad_maximum_fusion.est0_ref), channel_id=1, source_target_pairs={{0,64},{32,96},{64,0},{96,32},{1,65},{33,97},{65,1},{97,33},{2,66}... | collective-permute-start | bytes 393224 | tf_op jit(solution)/shard_map/ppermute | solution.py:233
  64.1 6.4 %collective-permute-start.5 = (bf16[2,2,2,32,256]{4,3,2,1,0:T(8,128)(2,1)S(1)}, bf16[2,2,2,32,256]{4,3,2,1,0:T(8,128)(2,1)S(1)}, u32[]{:S(2)}, u32[]{:S(2)}) collective-permute-start(bf16[2,2,2,32,256]{4,3,2,1,0:T(8,128)(2,1)S(1)} %pad_maximum_fusion.est0_ref), channel_id=1, source_target_pairs={{0,32},{32,64},{64,96},{96,0},{1,33},{33,65},{65,97},{97,1},{2,34}... | collective-permute-start | bytes 393224 | tf_op jit(solution)/shard_map/ppermute | solution.py:233
  64.8 2.5 %collective-permute-start = (f32[1,384]{1,0:T(1,128)S(1)}, f32[1,384]{1,0:T(1,128)S(1)}, u32[]{:S(2)}, u32[]{:S(2)}) collective-permute-start(f32[1,384]{1,0:T(1,128)S(1)} %pad_maximum_fusion.2), channel_id=1, source_target_pairs={{0,128},{128,0},{1,129},{129,1},{2,130},{130,2},{3,131},{131,3},{4... | collective-permute-start | bytes 4616 | tf_op jit(solution)/shard_map/ppermute | solution.py:203
  80.1 5.5 %collective-permute-start.8 = (s16[32,8,256]{2,1,0:T(8,128)(2,1)S(1)}, s16[32,8,256]{2,1,0:T(8,128)(2,1)S(1)}, u32[]{:S(2)}, u32[]{:S(2)}) collective-permute-start(s16[32,8,256]{2,1,0:T(8,128)(2,1)S(1)} %get-tuple-element.5), channel_id=1, source_target_pairs={{0,64},{32,96},{64,0},{96,32},{1,65},{33,97},{65,1},{97,33},{2,66}... | collective-permute-start | bytes 393224 | tf_op jit(solution)/shard_map/ppermute | solution.py:259
  80.6 5.0 %collective-permute-start.10 = (s16[32,8,256]{2,1,0:T(8,128)(2,1)S(1)}, s16[32,8,256]{2,1,0:T(8,128)(2,1)S(1)}, u32[]{:S(2)}, u32[]{:S(2)}) collective-permute-start(s16[32,8,256]{2,1,0:T(8,128)(2,1)S(1)} %get-tuple-element.6), channel_id=1, source_target_pairs={{0,96},{32,0},{64,32},{96,64},{1,97},{33,1},{65,33},{97,65},{2,98}... | collective-permute-start | bytes 393224 | tf_op jit(solution)/shard_map/ppermute | solution.py:259
  81.4 44.4 %copy-start = (f32[32,64,256]{2,1,0:T(8,128)S(1)}, f32[32,64,256]{2,1,0:T(8,128)}, u32[]{:S(2)}) copy-start(f32[32,64,256]{2,1,0:T(8,128)} %est_ref.3) | copy-start | bytes 6291460
  81.4 5.5 %collective-permute-start.9 = (s16[32,8,256]{2,1,0:T(8,128)(2,1)S(1)}, s16[32,8,256]{2,1,0:T(8,128)(2,1)S(1)}, u32[]{:S(2)}, u32[]{:S(2)}) collective-permute-start(s16[32,8,256]{2,1,0:T(8,128)(2,1)S(1)} %get-tuple-element.7), channel_id=1, source_target_pairs={{0,32},{32,64},{64,96},{96,0},{1,33},{33,65},{65,97},{97,1},{2,34}... | collective-permute-start | bytes 393224 | tf_op jit(solution)/shard_map/ppermute | solution.py:259

commit v3 on v2

--- a/solution.py
+++ b/solution.py
@@ -10,7 +10,7 @@
 TOTAL_SCALE = PAIR_SCALE / 4.0
 SLABS, ROWS, LENGTH = 32, 32, 256
 TOTAL = SLABS * ROWS
-GROUP = 4
+GROUP = 8
 
 
 def blur_matrix(profile):
@@ -115,30 +115,37 @@
 
 def back_kernel(
     shift_ref, offset_ref, other_ref, own_profile_ref, other_profile_ref, image_ref, inverse_ref,
-    out_ref, b_ref,
+    out_ref, b_ref, matrix_ref,
 ):
     upper, column, _ = place()
     row = lax.broadcasted_iota(jnp.int32, (1, 8, LENGTH), 1)
 
     for w in range(2):
         profile = jnp.where(upper == w, own_profile_ref[...], other_profile_ref[:, pl.ds(0, LENGTH)])
-        matrix = blur_matrix(profile).astype(jnp.bfloat16)
-
-        def blur(k, c, w=w, matrix=matrix):
+        matrix_ref[w] = blur_matrix(profile).astype(jnp.bfloat16)
+        a, b = blend_of(column, w)
+
+        def blur(k, c, w=w, a=a, b=b):
             base = pl.multiple_of(k * (ROWS * GROUP), ROWS * GROUP)
+            edge = pl.multiple_of(lax.rem(base + TOTAL - 8, TOTAL), 8)
+            slab = w * SLABS + lax.rem(k * GROUP + SLABS - 1, SLABS)
             image = image_ref[pl.ds(w * SLABS + k * GROUP, GROUP)].reshape(ROWS * GROUP, LENGTH)
             ratios = image.astype(jnp.float32) * inverse_ref[w, pl.ds(base, ROWS * GROUP)]
-            b_ref[w, pl.ds(base + 16, ROWS * GROUP)] = lax.dot_general(
-                ratios.astype(jnp.bfloat16),
-                matrix,
+            before = image_ref[slab, pl.ds(ROWS - 8, 8)].astype(jnp.float32)
+            before = before * inverse_ref[w, pl.ds(edge, 8)]
+            wide = jnp.concatenate([before, ratios], axis=0)
+            blended = a * ratios + b * wide[7 : ROWS * GROUP + 7]
+            b_ref[w, pl.ds(base + 8, ROWS * GROUP)] = lax.dot_general(
+                blended.astype(jnp.bfloat16),
+                matrix_ref[w],
                 (((1,), (1,)), ((), ())),
                 preferred_element_type=jnp.float32,
             )
             return c
 
         lax.fori_loop(0, SLABS // GROUP, blur, 0)
-        b_ref[w, pl.ds(0, 16)] = b_ref[w, pl.ds(TOTAL, 16)]
-        b_ref[w, pl.ds(TOTAL + 16, 8)] = b_ref[w, pl.ds(16, 8)]
+        b_ref[w, pl.ds(0, 8)] = b_ref[w, pl.ds(TOTAL, 8)]
+        b_ref[w, pl.ds(TOTAL + 8, 8)] = b_ref[w, pl.ds(8, 8)]
 
     views = []
     for w in range(2):
@@ -147,24 +154,25 @@
         offset = jnp.where(is_own, offset_ref[0], other_ref[0, LENGTH + 1].astype(jnp.int32))
         skip = lax.div(8 - offset, 8)
         rest = 8 - offset - 8 * skip
-        views.append((shift, skip, rest, lax.rem(8 - rest, 8), *blend_of(column, w)))
-
-    def join(s, c):
+        views.append((shift, skip, rest, lax.rem(8 - rest, 8)))
+
+    def join(k, c):
+        for q in range(4):
+            join_slab(4 * k + q)
+        return c
+
+    def join_slab(s):
         product = None
-        for w, (shift, skip, rest, turn, a, b) in enumerate(views):
+        for w, (shift, skip, rest, turn) in enumerate(views):
             t = lax.rem(s - shift + SLABS, SLABS)
             start = pl.multiple_of(t * ROWS + 8 * skip, 8)
-            wide = b_ref[w, pl.ds(start, ROWS + 16)]
-            blended = a * wide[8:] + b * wide[7 : ROWS + 15]
-            correction = tile_rows(blended, rest, turn, row)
+            correction = tile_rows(b_ref[w, pl.ds(start, ROWS + 8)], rest, turn, row)
             product = correction if product is None else product * correction
-        code = jnp.clip(jnp.log(product) * PAIR_SCALE, -32767.0, 32767.0)
-        code = jnp.floor(code + 0.5).astype(jnp.int32).astype(jnp.int16)
+        code = jnp.round(jnp.log(product) * PAIR_SCALE).astype(jnp.int32).astype(jnp.int16)
         for g in range(4):
             out_ref[lax.rem(g - column + 4, 4), s] = code[8 * g : 8 * g + 8]
-        return c
-
-    lax.fori_loop(0, SLABS, join, 0)
+
+    lax.fori_loop(0, SLABS // 4, join, 0)
 
 
 def final_kernel(est_ref, code_ref, out_ref):
@@ -222,11 +230,12 @@
 
     pair = swap_halves(block, "tile", [(i, i ^ 1) for i in range(32)], tile % 2)
     block = jnp.stack(pair, axis=2)
-    mine, given = block[0], block[1]
-    given = lax.ppermute(given, "tile", [(i, i ^ 16) for i in range(32)])
-    block = jnp.stack([mine, given], axis=1)
-    pair = swap_halves(block, "upper", swap, upper)
-    piece = jnp.stack(pair)
+    own_line = lax.dynamic_index_in_dim(block, upper, 1, keepdims=False)
+    other_line = lax.dynamic_index_in_dim(block, 1 - upper, 1, keepdims=False)
+    far = lax.ppermute(other_line[1], ("upper", "tile"), [(i, i ^ 48) for i in range(64)])
+    across = lax.ppermute(own_line[1], "tile", [(i, i ^ 16) for i in range(32)])
+    beside = lax.ppermute(other_line[0], "upper", swap)
+    piece = jnp.stack([own_line[0], across, beside, far]).reshape(2, 2, 2, ROWS, LENGTH)
     est_lines = [piece]
     for d in (1, 2, 3):
         route = [(i, (i + d) % 4) for i in range(4)]
@@ -249,7 +258,10 @@
         out_shape=jax.ShapeDtypeStruct((4, SLABS, 8, LENGTH), jnp.int16),
         in_specs=[SMEM] * 3 + [VMEM] * 4,
         out_specs=VMEM,
-        scratch_shapes=[pltpu.VMEM((2, TOTAL + 24, LENGTH), jnp.float32)],
+        scratch_shapes=[
+            pltpu.VMEM((2, TOTAL + 16, LENGTH), jnp.float32),
+            pltpu.VMEM((2, LENGTH, LENGTH), jnp.bfloat16),
+        ],
         compiler_params=pltpu.CompilerParams(vmem_limit_bytes=16 << 20),
         name="back_kernel",
     )(tile_shift, view_offset, other, blur_profile, other, image_lines, inverse)

time: 128 us -> 123 us (0.961)
  blocking collectives: 38.5 us -> 32.7 us
  waiting for transfers between devices: 14.7 us -> 18.4 us
  Pallas kernels: 13.6 us -> 10.1 us
    ppermute x1 -> x3, starting transfers between devices: 2.89 us -> 34.7 us  [the longest x1 31.2 us: update(): beside = lax.ppermute(other_line[0], 'upper', swap)]
    ppermute x2 -> x1, starting transfers between devices: 31.5 us -> 0.54 us  [swap_halves(): return (mine, lax.ppermute(given, axis, route))]
    all_to_all x1, blocking collectives: 21.5 us -> 15.7 us  [update(): logs = lax.all_to_all(logs, 'tile', 0, 0, tiled=True)]
    ppermute x2 -> x1, waiting for transfers between devices: 2.48 us -> 0.01 us  [swap_halves(): return (mine, lax.ppermute(given, axis, route))]
    ppermute x3, waiting for transfers between devices: 4.91 us -> 7.31 us  [update(): total += lax.ppermute(codes[d], 'column', route).astype(jnp.int32)]
    pallas_call x1, Pallas kernels: 5.65 us -> 3.25 us  [update(): pl.pallas_call(back_kernel, out_shape=jax.ShapeDtypeStruct((4, SLABS, 8,...]
    ppermute x3, waiting for transfers between devices: 3.23 us -> 5.54 us  [update(): est_lines.append(lax.ppermute(piece, 'column', route))]
    ppermute x1 -> x3, waiting for transfers between devices: 1.69 us -> 3.31 us  [the longest x1 2.11 us: update(): lax.ppermute(other_line[1], ('upper', 'tile'), [(i, i ^ 48) for i in rang...]
  transfers between devices with their start and end apart: 12 -> 13, of which waited for: 9 -> 8; matrix products, arithmetic and copies ran while one was open for 0% -> 0% of each run, Pallas kernels for 5% -> 4%
where the time goes in v3:
time: 123 us; the launch traced here: 122 us
  starting transfers between devices  56.5 us (46%)
  blocking collectives  32.7 us (27%)
  waiting for transfers between devices  18.4 us (15%)
  Pallas kernels  10.1 us (8%)
  local copies, waits for them, and re-layouts  2.98 us (2%)
  between operations  1.44 us (1%)
    ppermute x1, starting transfers between devices, update(): beside = lax.ppermute(other_line[0], 'upper', swap)  31.2 us
    all_to_all x1, blocking collectives, update(): logs = lax.all_to_all(logs, ('upper', 'column'), 0, 0, tiled=True)  17 us
    all_to_all x1, blocking collectives, update(): logs = lax.all_to_all(logs, 'tile', 0, 0, tiled=True)  15.7 us
    all_to_all x1, starting transfers between devices, update(): image_lines = lax.all_to_all(image, ('upper', 'tile'), 0, 0, tiled=True)  13.1 us
    ppermute x3, waiting for transfers between devices, update(): total += lax.ppermute(codes[d], 'column', route).astype(jnp.int32)  7.31 us
    ppermute x3, waiting for transfers between devices, update(): est_lines.append(lax.ppermute(piece, 'column', route))  5.54 us
    ppermute x3, starting transfers between devices, update(): est_lines.append(lax.ppermute(piece, 'column', route))  4.75 us
    pallas_call x1, Pallas kernels, update(): pl.pallas_call(back_kernel, out_shape=jax.ShapeDtypeStruct((4, SLABS, 8,...  3.25 us
  transfers between devices with their start and end apart: 13, of which 8 were waited for; matrix products, arithmetic and copies ran while one was open for 0% of the time, Pallas kernels for 4%

profile of v3, /device:TPU:1, one launch (start us, length us, event | category | flops | bytes accessed | tf_op | source)
XLA Modules:
  0.0 122.4 jit_solution(11063887281619790160)
XLA Ops:
  0.0 2.8 %copy.9 = bf16[1,32,64,256]{3,1,2,0:T(8,128)(2,1)} copy(bf16[1,32,64,256]{3,2,1,0:T(8,128)(2,1)} %param.6) | data formatting | bytes 2097152 | tf_op args[1]
  2.8 13.1 %all-to-all-start = ((bf16[64,32,256]{2,1,0:T(8,128)(2,1)}), bf16[64,32,256]{2,1,0:T(8,128)(2,1)S(1)}, u32[]{:S(2)}, u32[]{:S(2)}) async-start(bf16[64,32,256]{2,1,0:T(8,128)(2,1)} %bitcast.36), calls=%async_computation | async-start | bytes 2097152 | tf_op jit(solution)/shard_map/all_to_all | solution.py:229
  15.9 0.0 copy-start.1
  15.9 2.0 %pick_kernel.1 = bf16[2,2,2,32,256]{4,3,2,1,0:T(8,128)(2,1)} custom-call(f32[32,64,256]{2,1,0:T(8,128)} %est_ref.3), custom_call_target="tpu_custom_call" | custom-call | bytes 2097152 | tf_op jit(solution)/shard_map/pick_kernel/pallas_call | solution.py:214
  18.0 1.6 %collective-permute-start.1 = (bf16[2,2,2,32,256]{4,3,2,1,0:T(8,128)(2,1)}, bf16[2,2,2,32,256]{4,3,2,1,0:T(8,128)(2,1)S(1)}, u32[]{:S(2)}, u32[]{:S(2)}) collective-permute-start(bf16[2,2,2,32,256]{4,3,2,1,0:T(8,128)(2,1)} %pick_kernel.1), channel_id=1, source_target_pairs={{0,0},{1,1},{2,2},{3,3},{4,4},{5,5},{6,6},{7,7},{8,8},{9,9},{10,10... | collective-permute-start | bytes 393224 | tf_op jit(solution)/shard_map/ppermute | solution.py:227
  19.6 0.0 collective-permute-done.1
  19.6 0.5 collective-permute-start.2
  21.4 0.0 collective-permute-done.2
  21.5 2.9 %collective-permute-start.3 = (bf16[2,32,256]{2,1,0:T(8,128)(2,1)S(1)}, bf16[2,32,256]{2,1,0:T(8,128)(2,1)S(1)}, u32[]{:S(2)}, u32[]{:S(2)}) collective-permute-start(bf16[2,32,256]{2,1,0:T(8,128)(2,1)S(1)} %get-tuple-element.13), channel_id=1, source_target_pairs={{0,16},{1,17},{2,18},{3,19},{4,20},{5,21},{6,22},{7,23},{8,24},{9,... | collective-permute-start | bytes 98312 | tf_op jit(solution)/shard_map/ppermute | solution.py:236
  24.4 31.2 %collective-permute-start.4 = (bf16[2,32,256]{2,1,0:T(8,128)(2,1)S(1)}, bf16[2,32,256]{2,1,0:T(8,128)(2,1)S(1)}, u32[]{:S(2)}, u32[]{:S(2)}) collective-permute-start(bf16[2,32,256]{2,1,0:T(8,128)(2,1)S(1)} %get-tuple-element.14), channel_id=1, source_target_pairs={{0,128},{128,0},{1,129},{129,1},{2,130},{130,2},{3,131},{131,3},{4... | collective-permute-start | bytes 98312 | tf_op jit(solution)/shard_map/ppermute | solution.py:237
  55.5 0.6 collective-permute-start.5
  56.1 0.1 add_convert_fusion
  56.2 0.0 collective-permute-done.3
  56.2 1.2 collective-permute-done.4
  57.4 2.1 %collective-permute-done.5 = bf16[2,32,256]{2,1,0:T(8,128)(2,1)S(1)} collective-permute-done((bf16[2,32,256]{2,1,0:T(8,128)(2,1)S(1)}, bf16[2,32,256]{2,1,0:T(8,128)(2,1)S(1)}, u32[]{:S(2)}, u32[]{:S(2)}) %collective-permute-start.5) | collective-permute-done | bytes 32800 | tf_op jit(solution)/shard_map/ppermute | solution.py:235
  59.5 4.1 %collective-permute-start.8 = (bf16[2,2,2,32,256]{4,3,2,1,0:T(8,128)(2,1)S(1)}, bf16[2,2,2,32,256]{4,3,2,1,0:T(8,128)(2,1)S(1)}, u32[]{:S(2)}, u32[]{:S(2)}) collective-permute-start(bf16[2,2,2,32,256]{4,3,2,1,0:T(8,128)(2,1)S(1)} %bitcast.38), channel_id=1, source_target_pairs={{0,96},{32,0},{64,32},{96,64},{1,97},{33,1},{65,33},{97,65},{2,98}... | collective-permute-start | bytes 393224 | tf_op jit(solution)/shard_map/ppermute | solution.py:242
  63.6 0.0 collective-permute-start.7
  63.6 0.7 collective-permute-start.6
  64.3 0.0 copy-done.1
  64.3 0.2 collective-permute-start
  64.6 2.3 %collective-permute-done.other_ref.other_profile_ref = f32[1,384]{1,0:T(1,128)S(1)} collective-permute-done((f32[1,384]{1,0:T(1,128)S(1)}, f32[1,384]{1,0:T(1,128)S(1)}, u32[]{:S(2)}, u32[]{:S(2)}) %collective-permute-start) | collective-permute-done | bytes 1568 | tf_op jit(solution)/shard_map/ppermute | solution.py:211
  66.8 1.9 %collective-permute-done.8.est3_ref = bf16[2,2,2,32,256]{4,3,2,1,0:T(8,128)(2,1)S(1)} collective-permute-done((bf16[2,2,2,32,256]{4,3,2,1,0:T(8,128)(2,1)S(1)}, bf16[2,2,2,32,256]{4,3,2,1,0:T(8,128)(2,1)S(1)}, u32[]{:S(2)}, u32[]{:S(2)}) %collective-permute-start.8) | collective-permute-done | bytes 131104 | tf_op jit(solution)/shard_map/ppermute | solution.py:242
  68.7 0.3 collective-permute-done.7.est2_ref
  69.0 3.3 %collective-permute-done.6.est1_ref = bf16[2,2,2,32,256]{4,3,2,1,0:T(8,128)(2,1)S(1)} collective-permute-done((bf16[2,2,2,32,256]{4,3,2,1,0:T(8,128)(2,1)S(1)}, bf16[2,2,2,32,256]{4,3,2,1,0:T(8,128)(2,1)S(1)}, u32[]{:S(2)}, u32[]{:S(2)}) %collective-permute-start.6) | collective-permute-done | bytes 131104 | tf_op jit(solution)/shard_map/ppermute | solution.py:242
  72.4 2.7 %forward_kernel.1.inverse_ref = f32[2,1024,256]{2,1,0:T(8,128)S(1)} custom-call(s32[1]{0:T(128)S(6)} %copy.11.shift_ref, s32[1]{0:T(128)S(6)} %copy.10.offset_ref, f32[1,384]{1,0:T(1,128)S(1)} %collective-permute-done.other_ref.other_profile_ref, f32[1,256]{1,0:T(1,128)S(1)} %copy-done.1, f32[1,384]{1,0:T(1,128)S(1)} %collective-permute-done.other_ref.other_profile_ref, ...), custom_call_target="tpu_custom_call" | custom-call | flops 268435456 | bytes 8388608 | tf_op jit(solution)/shard_map/forward_kernel/pallas_call | solution.py:244
  75.1 0.0 all-to-all-done.image_ref
  75.1 3.3 %back_kernel.1 = s16[4,32,8,256]{3,2,1,0:T(8,128)(2,1)S(1)} custom-call(s32[1]{0:T(128)S(6)} %copy.11.shift_ref, s32[1]{0:T(128)S(6)} %copy.10.offset_ref, f32[1,384]{1,0:T(1,128)S(1)} %collective-permute-done.other_ref.other_profile_ref, f32[1,256]{1,0:T(1,128)S(1)} %copy-done.1, f32[1,384]{1,0:T(1,128)S(1)} %collective-permute-done.other_ref.other_profile_ref, ...), custom_call_target="tpu_custom_call" | custom-call | tf_op jit(solution)/shard_map/back_kernel/pallas_call | solution.py:256
  78.4 0.1 collective-permute-start.9
  78.5 0.1 collective-permute-start.11
  78.6 0.0 copy-start
  78.6 1.4 %collective-permute-start.10 = (s16[32,8,256]{2,1,0:T(8,128)(2,1)S(1)}, s16[32,8,256]{2,1,0:T(8,128)(2,1)S(1)}, u32[]{:S(2)}, u32[]{:S(2)}) collective-permute-start(s16[32,8,256]{2,1,0:T(8,128)(2,1)S(1)} %get-tuple-element.7), channel_id=1, source_target_pairs={{0,32},{32,64},{64,96},{96,0},{1,33},{33,65},{65,97},{97,1},{2,34}... | collective-permute-start | bytes 393224 | tf_op jit(solution)/shard_map/ppermute | solution.py:271
  80.0 3.9 %collective-permute-done.9 = s16[32,8,256]{2,1,0:T(8,128)(2,1)S(1)} collective-permute-done((s16[32,8,256]{2,1,0:T(8,128)(2,1)S(1)}, s16[32,8,256]{2,1,0:T(8,128)(2,1)S(1)}, u32[]{:S(2)}, u32[]{:S(2)}) %collective-permute-start.9) | collective-permute-done | bytes 131104 | tf_op jit(solution)/shard_map/ppermute | solution.py:271
  83.9 0.0 collective-permute-done.11
  83.9 3.4 %collective-permute-done.10 = s16[32,8,256]{2,1,0:T(8,128)(2,1)S(1)} collective-permute-done((s16[32,8,256]{2,1,0:T(8,128)(2,1)S(1)}, s16[32,8,256]{2,1,0:T(8,128)(2,1)S(1)}, u32[]{:S(2)}, u32[]{:S(2)}) %collective-permute-start.10) | collective-permute-done | bytes 131104 | tf_op jit(solution)/shard_map/ppermute | solution.py:271
  87.4 0.2 fusion.4
  87.5 15.7 %all_to_all.15 = s16[32,8,256]{2,1,0:T(8,128)(2,1)S(1)} all-to-all(s16[32,8,256]{2,1,0:T(8,128)(2,1)S(1)} %fusion.4), channel_id=1, replica_groups=mesh['upper'=2,'column'=4,'tile'=32] {'tile'}, dimensions={0} | all-to-all | bytes 262144 | tf_op jit(solution)/shard_map/all_to_all | solution.py:273
  103.2 0.1 broadcast_in_dim.10
  103.4 17.0 %all_to_all.16 = s16[8,8,32,256]{3,2,1,0:T(8,128)(2,1)S(1)} all-to-all(s16[8,8,32,256]{3,2,1,0:T(8,128)(2,1)S(1)} %broadcast_in_dim.10), channel_id=1, replica_groups=mesh['upper'=2,'column'=4,'tile'=32] {'upper','column'}, dimensions={0} | all-to-all | bytes 2097152 | tf_op jit(solution)/shard_map/all_to_all | solution.py:275
  120.4 0.0 copy-done
  120.4 2.1 %final_kernel.1 = f32[32,64,256]{2,1,0:T(8,128)} custom-call(f32[32,64,256]{2,1,0:T(8,128)S(1)} %copy-done, s16[2,4,8,32,256]{4,3,2,1,0:T(8,128)(2,1)S(1)} %bitcast.37), custom_call_target="tpu_custom_call" | custom-call | tf_op jit(solution)/shard_map/final_kernel/pallas_call | solution.py:277
  (9 shorter events, 0.1 us)
Async XLA Ops:
  2.8 72.3 %all-to-all-start = ((bf16[64,32,256]{2,1,0:T(8,128)(2,1)}), bf16[64,32,256]{2,1,0:T(8,128)(2,1)S(1)}, u32[]{:S(2)}, u32[]{:S(2)}) async-start(bf16[64,32,256]{2,1,0:T(8,128)(2,1)} %bitcast.36), calls=%async_computation | async-start | bytes 2097152 | tf_op jit(solution)/shard_map/all_to_all | solution.py:229
  15.9 48.4 %copy-start.1 = (f32[1,256]{1,0:T(1,128)S(1)}, f32[1,256]{1,0:T(1,128)}, u32[]{:S(2)}) copy-start(f32[1,256]{1,0:T(1,128)} %own_profile_ref.3) | copy-start | bytes 3076
  18.0 1.6 %collective-permute-start.1 = (bf16[2,2,2,32,256]{4,3,2,1,0:T(8,128)(2,1)}, bf16[2,2,2,32,256]{4,3,2,1,0:T(8,128)(2,1)S(1)}, u32[]{:S(2)}, u32[]{:S(2)}) collective-permute-start(bf16[2,2,2,32,256]{4,3,2,1,0:T(8,128)(2,1)} %pick_kernel.1), channel_id=1, source_target_pairs={{0,0},{1,1},{2,2},{3,3},{4,4},{5,5},{6,6},{7,7},{8,8},{9,9},{10,10... | collective-permute-start | bytes 393224 | tf_op jit(solution)/shard_map/ppermute | solution.py:227
  19.6 1.8 %collective-permute-start.2 = (bf16[2,2,32,256]{3,2,1,0:T(8,128)(2,1)S(1)}, bf16[2,2,32,256]{3,2,1,0:T(8,128)(2,1)S(1)}, u32[]{:S(2)}, u32[]{:S(2)}) collective-permute-start(bf16[2,2,32,256]{3,2,1,0:T(8,128)(2,1)S(1)} %get-tuple-element.10), channel_id=1, source_target_pairs={{0,1},{1,0},{2,3},{3,2},{4,5},{5,4},{6,7},{7,6},{8,9},{9,8},{10,11... | collective-permute-start | bytes 196616 | tf_op jit(solution)/shard_map/ppermute | solution.py:199
  21.5 34.7 %collective-permute-start.3 = (bf16[2,32,256]{2,1,0:T(8,128)(2,1)S(1)}, bf16[2,32,256]{2,1,0:T(8,128)(2,1)S(1)}, u32[]{:S(2)}, u32[]{:S(2)}) collective-permute-start(bf16[2,32,256]{2,1,0:T(8,128)(2,1)S(1)} %get-tuple-element.13), channel_id=1, source_target_pairs={{0,16},{1,17},{2,18},{3,19},{4,20},{5,21},{6,22},{7,23},{8,24},{9,... | collective-permute-start | bytes 98312 | tf_op jit(solution)/shard_map/ppermute | solution.py:236
  24.4 33.0 %collective-permute-start.4 = (bf16[2,32,256]{2,1,0:T(8,128)(2,1)S(1)}, bf16[2,32,256]{2,1,0:T(8,128)(2,1)S(1)}, u32[]{:S(2)}, u32[]{:S(2)}) collective-permute-start(bf16[2,32,256]{2,1,0:T(8,128)(2,1)S(1)} %get-tuple-element.14), channel_id=1, source_target_pairs={{0,128},{128,0},{1,129},{129,1},{2,130},{130,2},{3,131},{131,3},{4... | collective-permute-start | bytes 98312 | tf_op jit(solution)/shard_map/ppermute | solution.py:237
  55.5 4.0 %collective-permute-start.5 = (bf16[2,32,256]{2,1,0:T(8,128)(2,1)S(1)}, bf16[2,32,256]{2,1,0:T(8,128)(2,1)S(1)}, u32[]{:S(2)}, u32[]{:S(2)}) collective-permute-start(bf16[2,32,256]{2,1,0:T(8,128)(2,1)S(1)} %get-tuple-element.15), channel_id=1, source_target_pairs={{0,144},{1,145},{2,146},{3,147},{4,148},{5,149},{6,150},{7,151},{8... | collective-permute-start | bytes 98312 | tf_op jit(solution)/shard_map/ppermute | solution.py:235
  59.5 9.2 %collective-permute-start.8 = (bf16[2,2,2,32,256]{4,3,2,1,0:T(8,128)(2,1)S(1)}, bf16[2,2,2,32,256]{4,3,2,1,0:T(8,128)(2,1)S(1)}, u32[]{:S(2)}, u32[]{:S(2)}) collective-permute-start(bf16[2,2,2,32,256]{4,3,2,1,0:T(8,128)(2,1)S(1)} %bitcast.38), channel_id=1, source_target_pairs={{0,96},{32,0},{64,32},{96,64},{1,97},{33,1},{65,33},{97,65},{2,98}... | collective-permute-start | bytes 393224 | tf_op jit(solution)/shard_map/ppermute | solution.py:242
  63.6 5.4 %collective-permute-start.7 = (bf16[2,2,2,32,256]{4,3,2,1,0:T(8,128)(2,1)S(1)}, bf16[2,2,2,32,256]{4,3,2,1,0:T(8,128)(2,1)S(1)}, u32[]{:S(2)}, u32[]{:S(2)}) collective-permute-start(bf16[2,2,2,32,256]{4,3,2,1,0:T(8,128)(2,1)S(1)} %bitcast.39), channel_id=1, source_target_pairs={{0,64},{32,96},{64,0},{96,32},{1,65},{33,97},{65,1},{97,33},{2,66}... | collective-permute-start | bytes 393224 | tf_op jit(solution)/shard_map/ppermute | solution.py:242
  63.6 8.8 %collective-permute-start.6 = (bf16[2,2,2,32,256]{4,3,2,1,0:T(8,128)(2,1)S(1)}, bf16[2,2,2,32,256]{4,3,2,1,0:T(8,128)(2,1)S(1)}, u32[]{:S(2)}, u32[]{:S(2)}) collective-permute-start(bf16[2,2,2,32,256]{4,3,2,1,0:T(8,128)(2,1)S(1)} %bitcast.40), channel_id=1, source_target_pairs={{0,32},{32,64},{64,96},{96,0},{1,33},{33,65},{65,97},{97,1},{2,34}... | collective-permute-start | bytes 393224 | tf_op jit(solution)/shard_map/ppermute | solution.py:242
  64.3 2.5 %collective-permute-start = (f32[1,384]{1,0:T(1,128)S(1)}, f32[1,384]{1,0:T(1,128)S(1)}, u32[]{:S(2)}, u32[]{:S(2)}) collective-permute-start(f32[1,384]{1,0:T(1,128)S(1)} %pad_maximum_fusion.1), channel_id=1, source_target_pairs={{0,128},{128,0},{1,129},{129,1},{2,130},{130,2},{3,131},{131,3},{4... | collective-permute-start | bytes 4616 | tf_op jit(solution)/shard_map/ppermute | solution.py:211
  78.4 5.5 %collective-permute-start.9 = (s16[32,8,256]{2,1,0:T(8,128)(2,1)S(1)}, s16[32,8,256]{2,1,0:T(8,128)(2,1)S(1)}, u32[]{:S(2)}, u32[]{:S(2)}) collective-permute-start(s16[32,8,256]{2,1,0:T(8,128)(2,1)S(1)} %get-tuple-element.5), channel_id=1, source_target_pairs={{0,64},{32,96},{64,0},{96,32},{1,65},{33,97},{65,1},{97,33},{2,66}... | collective-permute-start | bytes 393224 | tf_op jit(solution)/shard_map/ppermute | solution.py:271
  78.5 5.4 %collective-permute-start.11 = (s16[32,8,256]{2,1,0:T(8,128)(2,1)S(1)}, s16[32,8,256]{2,1,0:T(8,128)(2,1)S(1)}, u32[]{:S(2)}, u32[]{:S(2)}) collective-permute-start(s16[32,8,256]{2,1,0:T(8,128)(2,1)S(1)} %get-tuple-element.6), channel_id=1, source_target_pairs={{0,96},{32,0},{64,32},{96,64},{1,97},{33,1},{65,33},{97,65},{2,98}... | collective-permute-start | bytes 393224 | tf_op jit(solution)/shard_map/ppermute | solution.py:271
  78.6 41.8 %copy-start = (f32[32,64,256]{2,1,0:T(8,128)S(1)}, f32[32,64,256]{2,1,0:T(8,128)}, u32[]{:S(2)}) copy-start(f32[32,64,256]{2,1,0:T(8,128)} %est_ref.3) | copy-start | bytes 6291460
  78.6 8.8 %collective-permute-start.10 = (s16[32,8,256]{2,1,0:T(8,128)(2,1)S(1)}, s16[32,8,256]{2,1,0:T(8,128)(2,1)S(1)}, u32[]{:S(2)}, u32[]{:S(2)}) collective-permute-start(s16[32,8,256]{2,1,0:T(8,128)(2,1)S(1)} %get-tuple-element.7), channel_id=1, source_target_pairs={{0,32},{32,64},{64,96},{96,0},{1,33},{33,65},{65,97},{97,1},{2,34}... | collective-permute-start | bytes 393224 | tf_op jit(solution)/shard_map/ppermute | solution.py:271

commit v4 on v3

--- a/solution.py
+++ b/solution.py
@@ -1,3 +1,5 @@
+import functools
+
 import jax
 import jax.numpy as jnp
 from jax import lax
@@ -105,8 +107,11 @@
                 start = pl.multiple_of(s * ROWS + 8 * skip, 8)
                 wide = tile_rows(e_ref[pl.ds(start, ROWS + 16)], rest, turn, row)
                 parts.append(a * wide[:ROWS] + b * wide[1 : ROWS + 1])
-            warped = jnp.concatenate(parts, axis=0).astype(jnp.bfloat16)
-            forward = jnp.dot(warped, matrix, preferred_element_type=jnp.float32)
+            warped = jnp.concatenate(parts, axis=0)
+            high = warped.astype(jnp.bfloat16)
+            low = (warped - high.astype(jnp.float32)).astype(jnp.bfloat16)
+            forward = jnp.dot(high, matrix, preferred_element_type=jnp.float32)
+            forward += jnp.dot(low, matrix, preferred_element_type=jnp.float32)
             inverse_ref[w, pl.ds(base, ROWS * GROUP)] = 1.0 / forward
             return c
 
@@ -175,11 +180,88 @@
     lax.fori_loop(0, SLABS // 4, join, 0)
 
 
-def final_kernel(est_ref, code_ref, out_ref):
-    for h in range(2):
-        lines = pl.ds(32 * h, 32)
-        logs = code_ref[h, 0].astype(jnp.int32).astype(jnp.float32) * (1.0 / TOTAL_SCALE)
-        out_ref[:, lines] = est_ref[:, lines] * jnp.exp(logs)
+def part_of(u, d):
+    upper, column, _ = place()
+    rows = pl.ds(pl.multiple_of(8 * lax.rem(column - d + 4, 4), 8), 8)
+    lines = pl.ds(pl.multiple_of(32 * lax.rem(upper + u, 2), 32), 32)
+    return rows, lines
+
+
+def apply_codes(code_ref, est_ref, part_ref):
+    logs = code_ref[...].astype(jnp.int32).astype(jnp.float32) * (1.0 / TOTAL_SCALE)
+    part_ref[...] = est_ref[...] * jnp.exp(logs)
+
+
+def first_kernel(places, later, est_ref, *refs):
+    count = len(places)
+    codes, (out_ref, rest_ref, parts_ref, in_sem, out_sem) = refs[:count], refs[count:]
+    loads, stores = [], []
+    for p, (u, d) in enumerate(places + later):
+        rows, lines = part_of(u, d)
+        target = parts_ref.at[p] if p < count else rest_ref.at[p - count]
+        load = pltpu.make_async_copy(est_ref.at[rows, lines], target, in_sem.at[p])
+        load.start()
+        loads.append(load)
+    for p, (u, d) in enumerate(places):
+        rows, lines = part_of(u, d)
+        loads[p].wait()
+        apply_codes(codes[p], parts_ref.at[p], parts_ref.at[count + p])
+        store = pltpu.make_async_copy(
+            parts_ref.at[count + p], out_ref.at[rows, lines], out_sem.at[p]
+        )
+        store.start()
+        stores.append(store)
+    for copy in loads[count:] + stores:
+        copy.wait()
+
+
+def last_kernel(places, est_ref, *refs):
+    count = len(places)
+    codes, (out_ref, parts_ref, sem) = refs[:count], refs[count + 1 :]
+    stores = []
+    for p, (u, d) in enumerate(places):
+        rows, lines = part_of(u, d)
+        apply_codes(codes[p], est_ref.at[p], parts_ref.at[p])
+        store = pltpu.make_async_copy(parts_ref.at[p], out_ref.at[rows, lines], sem.at[p])
+        store.start()
+        stores.append(store)
+    for store in stores:
+        store.wait()
+
+
+def finish(places, estimate, pieces, early):
+    whole = jax.ShapeDtypeStruct((32, 64, LENGTH), jnp.float32)
+    part = (8, 32, LENGTH)
+    late = len(places) - early
+    first, rest = pl.pallas_call(
+        functools.partial(first_kernel, places[:early], places[early:]),
+        out_shape=(whole, jax.ShapeDtypeStruct((late, *part), jnp.float32)),
+        in_specs=[ANY] + [VMEM] * early,
+        out_specs=(ANY, VMEM),
+        scratch_shapes=[
+            pltpu.VMEM((2 * early, *part), jnp.float32),
+            pltpu.SemaphoreType.DMA((early + late,)),
+            pltpu.SemaphoreType.DMA((early,)),
+        ],
+        cost_estimate=pl.CostEstimate(
+            flops=early << 17, bytes_accessed=early << 19, transcendentals=early << 16
+        ),
+        compiler_params=pltpu.CompilerParams(vmem_limit_bytes=32 << 19),
+        name="first_kernel",
+    )(estimate, *pieces[:early])
+    return pl.pallas_call(
+        functools.partial(last_kernel, places[early:]),
+        out_shape=whole,
+        in_specs=[VMEM] * (1 + late) + [ANY],
+        out_specs=ANY,
+        scratch_shapes=[
+            pltpu.VMEM((late, *part), jnp.float32),
+            pltpu.SemaphoreType.DMA((late,)),
+        ],
+        input_output_aliases={1 + late: 0},
+        compiler_params=pltpu.CompilerParams(vmem_limit_bytes=16 << 20),
+        name="last_kernel",
+    )(rest, *pieces[early:], first)
 
 
 def distance_route():
@@ -201,6 +283,7 @@
 
 VMEM = pl.BlockSpec(memory_space=pltpu.VMEM)
 SMEM = pl.BlockSpec(memory_space=pltpu.SMEM)
+ANY = pl.BlockSpec(memory_space=pl.ANY)
 
 
 def update(estimate, measured, blur_profile, view_offset, tile_shift):
@@ -271,21 +354,13 @@
         total += lax.ppermute(codes[d], "column", route).astype(jnp.int32)
     logs = ((total + 2) >> 2).astype(jnp.int16)
     logs = lax.all_to_all(logs, "tile", 0, 0, tiled=True)
-    logs = jnp.broadcast_to(logs.transpose(1, 0, 2)[None], (8, 8, 32, LENGTH))
-    logs = lax.all_to_all(logs, ("upper", "column"), 0, 0, tiled=True)
-
-    return pl.pallas_call(
-        final_kernel,
-        grid=(4,),
-        out_shape=jax.ShapeDtypeStruct((32, 64, LENGTH), jnp.float32),
-        in_specs=[
-            pl.BlockSpec((8, 64, LENGTH), lambda g: (g, 0, 0)),
-            pl.BlockSpec((2, 1, 8, 32, LENGTH), lambda g: (0, g, 0, 0, 0)),
-        ],
-        out_specs=pl.BlockSpec((8, 64, LENGTH), lambda g: (g, 0, 0)),
-        compiler_params=pltpu.CompilerParams(vmem_limit_bytes=16 << 20),
-        name="final_kernel",
-    )(estimate, logs.reshape(2, 4, 8, 32, LENGTH))
+    logs = logs.transpose(1, 0, 2)
+    places = [(0, 0), (1, 2), (0, 2), (1, 1), (1, 3), (0, 1), (0, 3), (1, 0)]
+    pieces = [logs]
+    for u, d in places[1:]:
+        route = [(i, 4 * ((i // 4 + u) % 2) + (i + d) % 4) for i in range(8)]
+        pieces.append(lax.ppermute(logs, ("upper", "column"), route))
+    return finish(places, estimate, pieces, 6)
 
 
 def solution(mesh):

time: 123 us -> 125 us (1.016)
  the two profiles are of different devices: /device:TPU:1 before, /device:TPU:6 now
where the time goes in v4:
time: 125 us
  waiting for transfers between devices  51.5 us (41%)
  starting transfers between devices  41.8 us (33%)
  blocking collectives  16 us (13%)
  Pallas kernels  10.6 us (8%)
  local copies, waits for them, and re-layouts  2.87 us (2%)
  between operations  1.66 us (1%)
    ppermute x1, waiting for transfers between devices, update(): block = lax.ppermute(chip, ('upper', 'column', 'tile'), distance_route())  28.8 us
    all_to_all x1, blocking collectives, update(): logs = lax.all_to_all(logs, 'tile', 0, 0, tiled=True)  16 us
    all_to_all x1, starting transfers between devices, update(): image_lines = lax.all_to_all(image, ('upper', 'tile'), 0, 0, tiled=True)  12.1 us
    ppermute x7, starting transfers between devices, update(): pieces.append(lax.ppermute(logs, ('upper', 'column'), route))  11.9 us
    ppermute x7, waiting for transfers between devices, update(): pieces.append(lax.ppermute(logs, ('upper', 'column'), route))  8.76 us
    ppermute x1, starting transfers between devices, update(): block = lax.ppermute(chip, ('upper', 'column', 'tile'), distance_route())  5.28 us
    ppermute x3, waiting for transfers between devices, update(): total += lax.ppermute(codes[d], 'column', route).astype(jnp.int32)  4.7 us
    ppermute x3, starting transfers between devices, update(): total += lax.ppermute(codes[d], 'column', route).astype(jnp.int32)  4.16 us
  transfers between devices with their start and end apart: 20, of which 12 were waited for; matrix products, arithmetic and copies ran while one was open for 0% of the time, Pallas kernels for 5%

profile of v4, /device:TPU:6, one launch (start us, length us, event | category | flops | bytes accessed | tf_op | source)
XLA Modules:
  0.0 124.7 jit_solution(15896308033673249978)
XLA Ops:
  0.0 2.8 %copy.16 = bf16[1,32,64,256]{3,1,2,0:T(8,128)(2,1)} copy(bf16[1,32,64,256]{3,2,1,0:T(8,128)(2,1)} %param.6) | data formatting | bytes 2097152 | tf_op args[1]
  2.8 12.1 %all-to-all-start = ((bf16[64,32,256]{2,1,0:T(8,128)(2,1)}), bf16[64,32,256]{2,1,0:T(8,128)(2,1)S(1)}, u32[]{:S(2)}, u32[]{:S(2)}) async-start(bf16[64,32,256]{2,1,0:T(8,128)(2,1)} %bitcast.36), calls=%async_computation | async-start | bytes 2097152 | tf_op jit(solution)/shard_map/all_to_all | solution.py:312
  14.9 0.0 copy-start.1
  14.9 2.1 %pick_kernel.1 = bf16[2,2,2,32,256]{4,3,2,1,0:T(8,128)(2,1)} custom-call(f32[32,64,256]{2,1,0:T(8,128)} %est_ref.3), custom_call_target="tpu_custom_call" | custom-call | bytes 2097152 | tf_op jit(solution)/shard_map/pick_kernel/pallas_call | solution.py:297
  17.0 5.3 %collective-permute-start.1 = (bf16[2,2,2,32,256]{4,3,2,1,0:T(8,128)(2,1)}, bf16[2,2,2,32,256]{4,3,2,1,0:T(8,128)(2,1)S(1)}, u32[]{:S(2)}, u32[]{:S(2)}) collective-permute-start(bf16[2,2,2,32,256]{4,3,2,1,0:T(8,128)(2,1)} %pick_kernel.1), channel_id=1, source_target_pairs={{0,0},{1,1},{2,2},{3,3},{4,4},{5,5},{6,6},{7,7},{8,8},{9,9},{10,10... | collective-permute-start | bytes 393224 | tf_op jit(solution)/shard_map/ppermute | solution.py:310
  22.3 28.8 %collective-permute-done.1 = bf16[2,2,2,32,256]{4,3,2,1,0:T(8,128)(2,1)S(1)} collective-permute-done((bf16[2,2,2,32,256]{4,3,2,1,0:T(8,128)(2,1)}, bf16[2,2,2,32,256]{4,3,2,1,0:T(8,128)(2,1)S(1)}, u32[]{:S(2)}, u32[]{:S(2)}) %collective-permute-start.1) | collective-permute-done | bytes 131104 | tf_op jit(solution)/shard_map/ppermute | solution.py:310
  51.1 0.1 collective-permute-start.2
  52.5 0.0 collective-permute-done.2
  52.6 3.2 %collective-permute-start.3 = (bf16[2,32,256]{2,1,0:T(8,128)(2,1)S(1)}, bf16[2,32,256]{2,1,0:T(8,128)(2,1)S(1)}, u32[]{:S(2)}, u32[]{:S(2)}) collective-permute-start(bf16[2,32,256]{2,1,0:T(8,128)(2,1)S(1)} %get-tuple-element.17), channel_id=1, source_target_pairs={{0,16},{1,17},{2,18},{3,19},{4,20},{5,21},{6,22},{7,23},{8,24},{9,... | collective-permute-start | bytes 98312 | tf_op jit(solution)/shard_map/ppermute | solution.py:319
  55.8 0.0 collective-permute-start.4
  55.8 1.0 collective-permute-start.5
  56.8 0.1 add_convert_fusion
  56.8 1.5 %collective-permute-done.3 = bf16[2,32,256]{2,1,0:T(8,128)(2,1)S(1)} collective-permute-done((bf16[2,32,256]{2,1,0:T(8,128)(2,1)S(1)}, bf16[2,32,256]{2,1,0:T(8,128)(2,1)S(1)}, u32[]{:S(2)}, u32[]{:S(2)}) %collective-permute-start.3) | collective-permute-done | bytes 32800 | tf_op jit(solution)/shard_map/ppermute | solution.py:319
  58.3 1.4 %collective-permute-done.4 = bf16[2,32,256]{2,1,0:T(8,128)(2,1)S(1)} collective-permute-done((bf16[2,32,256]{2,1,0:T(8,128)(2,1)S(1)}, bf16[2,32,256]{2,1,0:T(8,128)(2,1)S(1)}, u32[]{:S(2)}, u32[]{:S(2)}) %collective-permute-start.4) | collective-permute-done | bytes 32800 | tf_op jit(solution)/shard_map/ppermute | solution.py:320
  59.7 1.3 %collective-permute-done.5 = bf16[2,32,256]{2,1,0:T(8,128)(2,1)S(1)} collective-permute-done((bf16[2,32,256]{2,1,0:T(8,128)(2,1)S(1)}, bf16[2,32,256]{2,1,0:T(8,128)(2,1)S(1)}, u32[]{:S(2)}, u32[]{:S(2)}) %collective-permute-start.5) | collective-permute-done | bytes 32800 | tf_op jit(solution)/shard_map/ppermute | solution.py:318
  61.0 0.1 collective-permute-start.8
  61.1 0.7 collective-permute-start.7
  61.8 2.5 %collective-permute-start.6 = (bf16[2,2,2,32,256]{4,3,2,1,0:T(8,128)(2,1)S(1)}, bf16[2,2,2,32,256]{4,3,2,1,0:T(8,128)(2,1)S(1)}, u32[]{:S(2)}, u32[]{:S(2)}) collective-permute-start(bf16[2,2,2,32,256]{4,3,2,1,0:T(8,128)(2,1)S(1)} %bitcast.48), channel_id=1, source_target_pairs={{0,32},{32,64},{64,96},{96,0},{1,33},{33,65},{65,97},{97,1},{2,34}... | collective-permute-start | bytes 393224 | tf_op jit(solution)/shard_map/ppermute | solution.py:325
  64.3 0.8 collective-permute-start
  65.2 2.9 %collective-permute-done.other_ref.other_profile_ref = f32[1,384]{1,0:T(1,128)S(1)} collective-permute-done((f32[1,384]{1,0:T(1,128)S(1)}, f32[1,384]{1,0:T(1,128)S(1)}, u32[]{:S(2)}, u32[]{:S(2)}) %collective-permute-start) | collective-permute-done | bytes 1568 | tf_op jit(solution)/shard_map/ppermute | solution.py:294
  68.0 1.6 %collective-permute-done.8.est3_ref = bf16[2,2,2,32,256]{4,3,2,1,0:T(8,128)(2,1)S(1)} collective-permute-done((bf16[2,2,2,32,256]{4,3,2,1,0:T(8,128)(2,1)S(1)}, bf16[2,2,2,32,256]{4,3,2,1,0:T(8,128)(2,1)S(1)}, u32[]{:S(2)}, u32[]{:S(2)}) %collective-permute-start.8) | collective-permute-done | bytes 131104 | tf_op jit(solution)/shard_map/ppermute | solution.py:325
  69.6 0.6 collective-permute-done.6.est1_ref
  70.2 3.0 %forward_kernel.1.inverse_ref = f32[2,1024,256]{2,1,0:T(8,128)S(1)} custom-call(s32[1]{0:T(128)S(6)} %copy.20.shift_ref, s32[1]{0:T(128)S(6)} %copy.19.offset_ref, f32[1,384]{1,0:T(1,128)S(1)} %collective-permute-done.other_ref.other_profile_ref, f32[1,256]{1,0:T(1,128)S(1)} %copy-done.1, f32[1,384]{1,0:T(1,128)S(1)} %collective-permute-done.other_ref.other_profile_ref, ...), custom_call_target="tpu_custom_call" | custom-call | flops 268435456 | bytes 8388608 | tf_op jit(solution)/shard_map/forward_kernel/pallas_call | solution.py:327
  73.2 0.0 all-to-all-done.image_ref
  73.2 0.0 copy-start
  73.2 3.2 %back_kernel.1 = s16[4,32,8,256]{3,2,1,0:T(8,128)(2,1)S(1)} custom-call(s32[1]{0:T(128)S(6)} %copy.20.shift_ref, s32[1]{0:T(128)S(6)} %copy.19.offset_ref, f32[1,384]{1,0:T(1,128)S(1)} %collective-permute-done.other_ref.other_profile_ref, f32[1,256]{1,0:T(1,128)S(1)} %copy-done.1, f32[1,384]{1,0:T(1,128)S(1)} %collective-permute-done.other_ref.other_profile_ref, ...), custom_call_target="tpu_custom_call" | custom-call | tf_op jit(solution)/shard_map/back_kernel/pallas_call | solution.py:339
  76.5 0.9 collective-permute-start.9
  77.4 2.4 %collective-permute-start.11 = (s16[32,8,256]{2,1,0:T(8,128)(2,1)S(1)}, s16[32,8,256]{2,1,0:T(8,128)(2,1)S(1)}, u32[]{:S(2)}, u32[]{:S(2)}) collective-permute-start(s16[32,8,256]{2,1,0:T(8,128)(2,1)S(1)} %get-tuple-element.10), channel_id=1, source_target_pairs={{0,96},{32,0},{64,32},{96,64},{1,97},{33,1},{65,33},{97,65},{2,98}... | collective-permute-start | bytes 393224 | tf_op jit(solution)/shard_map/ppermute | solution.py:354
  79.7 0.9 collective-permute-start.10
  80.6 2.9 %collective-permute-done.9 = s16[32,8,256]{2,1,0:T(8,128)(2,1)S(1)} collective-permute-done((s16[32,8,256]{2,1,0:T(8,128)(2,1)S(1)}, s16[32,8,256]{2,1,0:T(8,128)(2,1)S(1)}, u32[]{:S(2)}, u32[]{:S(2)}) %collective-permute-start.9) | collective-permute-done | bytes 131104 | tf_op jit(solution)/shard_map/ppermute | solution.py:354
  83.5 1.2 %collective-permute-done.11 = s16[32,8,256]{2,1,0:T(8,128)(2,1)S(1)} collective-permute-done((s16[32,8,256]{2,1,0:T(8,128)(2,1)S(1)}, s16[32,8,256]{2,1,0:T(8,128)(2,1)S(1)}, u32[]{:S(2)}, u32[]{:S(2)}) %collective-permute-start.11) | collective-permute-done | bytes 131104 | tf_op jit(solution)/shard_map/ppermute | solution.py:354
  84.8 0.5 collective-permute-done.10
  85.3 0.2 fusion.4
  85.5 16.0 %all_to_all.10 = s16[32,8,256]{2,1,0:T(8,128)(2,1)S(1)} all-to-all(s16[32,8,256]{2,1,0:T(8,128)(2,1)S(1)} %fusion.4), channel_id=1, replica_groups=mesh['upper'=2,'column'=4,'tile'=32] {'tile'}, dimensions={0} | all-to-all | bytes 262144 | tf_op jit(solution)/shard_map/all_to_all | solution.py:356
  101.5 2.8 %collective-permute-start.16 = (s16[8,32,256]{2,1,0:T(8,128)(2,1)S(1)}, s16[8,32,256]{2,1,0:T(8,128)(2,1)S(1)}, u32[]{:S(2)}, u32[]{:S(2)}) collective-permute-start(s16[8,32,256]{2,1,0:T(8,128)(2,1)S(1)} %bitcast.38), channel_id=1, source_target_pairs={{0,32},{32,64},{64,96},{96,0},{128,160},{160,192},{192,224},{224,1... | collective-permute-start | bytes 393224 | tf_op jit(solution)/shard_map/ppermute | solution.py:362
  104.2 0.0 collective-permute-start.15
  104.2 4.1 %collective-permute-start.14 = (s16[8,32,256]{2,1,0:T(8,128)(2,1)S(1)}, s16[8,32,256]{2,1,0:T(8,128)(2,1)S(1)}, u32[]{:S(2)}, u32[]{:S(2)}) collective-permute-start(s16[8,32,256]{2,1,0:T(8,128)(2,1)S(1)} %bitcast.40), channel_id=1, source_target_pairs={{0,160},{32,192},{64,224},{96,128},{128,32},{160,64},{192,96},{224... | collective-permute-start | bytes 393224 | tf_op jit(solution)/shard_map/ppermute | solution.py:362
  108.3 0.0 collective-permute-start.13
  108.3 2.9 %collective-permute-start.12 = (s16[8,32,256]{2,1,0:T(8,128)(2,1)S(1)}, s16[8,32,256]{2,1,0:T(8,128)(2,1)S(1)}, u32[]{:S(2)}, u32[]{:S(2)}) collective-permute-start(s16[8,32,256]{2,1,0:T(8,128)(2,1)S(1)} %bitcast.42), channel_id=1, source_target_pairs={{0,192},{32,224},{64,128},{96,160},{128,64},{160,96},{192,0},{224,... | collective-permute-start | bytes 393224 | tf_op jit(solution)/shard_map/ppermute | solution.py:362
  111.3 0.0 collective-permute-done.16.refs_5_
  111.3 2.1 %collective-permute-start.18 = (s16[8,32,256]{2,1,0:T(8,128)(2,1)S(1)}, s16[8,32,256]{2,1,0:T(8,128)(2,1)S(1)}, u32[]{:S(2)}, u32[]{:S(2)}) collective-permute-start(s16[8,32,256]{2,1,0:T(8,128)(2,1)S(1)} %bitcast.43), channel_id=1, source_target_pairs={{0,128},{32,160},{64,192},{96,224},{128,0},{160,32},{192,64},{224,... | collective-permute-start | bytes 393224 | tf_op jit(solution)/shard_map/ppermute | solution.py:362
  113.3 4.1 %collective-permute-done.15.refs_4_ = s16[8,32,256]{2,1,0:T(8,128)(2,1)S(1)} collective-permute-done((s16[8,32,256]{2,1,0:T(8,128)(2,1)S(1)}, s16[8,32,256]{2,1,0:T(8,128)(2,1)S(1)}, u32[]{:S(2)}, u32[]{:S(2)}) %collective-permute-start.15) | collective-permute-done | bytes 131104 | tf_op jit(solution)/shard_map/ppermute | solution.py:362
  117.5 0.0 collective-permute-done.14.refs_3_
  117.5 0.0 collective-permute-done.13.refs_2_
  117.5 0.0 collective-permute-done.12.refs_1_
  117.5 1.5 %first_kernel.1 = (f32[32,64,256]{2,1,0:T(8,128)}, f32[2,8,32,256]{3,2,1,0:T(8,128)S(1)}) custom-call(f32[32,64,256]{2,1,0:T(8,128)S(1)} %copy-done, s16[8,32,256]{2,1,0:T(8,128)(2,1)S(1)} %bitcast.45, s16[8,32,256]{2,1,0:T(8,128)(2,1)S(1)} %collective-permute-done.12.refs_1_, s16[8,32,256]{2,1,0:T(8,128)(2,1)S(1)} %collective-permute-done.13.refs_2_, ...), custom_call_target="tpu_custom_call" | custom-call | flops 786432 | bytes 3145728 | tf_op jit(solution)/shard_map/first_kernel/pallas_call | solution.py:236
  119.0 4.6 %collective-permute-done.17.refs_0_ = s16[8,32,256]{2,1,0:T(8,128)(2,1)S(1)} collective-permute-done((s16[8,32,256]{2,1,0:T(8,128)(2,1)S(1)}, s16[8,32,256]{2,1,0:T(8,128)(2,1)S(1)}, u32[]{:S(2)}, u32[]{:S(2)}) %collective-permute-start.17) | collective-permute-done | bytes 131104 | tf_op jit(solution)/shard_map/ppermute | solution.py:362
  123.6 0.9 last_kernel.1
  (14 shorter events, 0.1 us)
Async XLA Ops:
  2.8 70.4 %all-to-all-start = ((bf16[64,32,256]{2,1,0:T(8,128)(2,1)}), bf16[64,32,256]{2,1,0:T(8,128)(2,1)S(1)}, u32[]{:S(2)}, u32[]{:S(2)}) async-start(bf16[64,32,256]{2,1,0:T(8,128)(2,1)} %bitcast.36), calls=%async_computation | async-start | bytes 2097152 | tf_op jit(solution)/shard_map/all_to_all | solution.py:312
  14.9 49.4 %copy-start.1 = (f32[1,256]{1,0:T(1,128)S(1)}, f32[1,256]{1,0:T(1,128)}, u32[]{:S(2)}) copy-start(f32[1,256]{1,0:T(1,128)} %own_profile_ref.3) | copy-start | bytes 3076
  17.0 34.1 %collective-permute-start.1 = (bf16[2,2,2,32,256]{4,3,2,1,0:T(8,128)(2,1)}, bf16[2,2,2,32,256]{4,3,2,1,0:T(8,128)(2,1)S(1)}, u32[]{:S(2)}, u32[]{:S(2)}) collective-permute-start(bf16[2,2,2,32,256]{4,3,2,1,0:T(8,128)(2,1)} %pick_kernel.1), channel_id=1, source_target_pairs={{0,0},{1,1},{2,2},{3,3},{4,4},{5,5},{6,6},{7,7},{8,8},{9,9},{10,10... | collective-permute-start | bytes 393224 | tf_op jit(solution)/shard_map/ppermute | solution.py:310
  51.1 1.4 %collective-permute-start.2 = (bf16[2,2,32,256]{3,2,1,0:T(8,128)(2,1)S(1)}, bf16[2,2,32,256]{3,2,1,0:T(8,128)(2,1)S(1)}, u32[]{:S(2)}, u32[]{:S(2)}) collective-permute-start(bf16[2,2,32,256]{3,2,1,0:T(8,128)(2,1)S(1)} %get-tuple-element.14), channel_id=1, source_target_pairs={{0,1},{1,0},{2,3},{3,2},{4,5},{5,4},{6,7},{7,6},{8,9},{9,8},{10,11... | collective-permute-start | bytes 196616 | tf_op jit(solution)/shard_map/ppermute | solution.py:281
  52.6 5.7 %collective-permute-start.3 = (bf16[2,32,256]{2,1,0:T(8,128)(2,1)S(1)}, bf16[2,32,256]{2,1,0:T(8,128)(2,1)S(1)}, u32[]{:S(2)}, u32[]{:S(2)}) collective-permute-start(bf16[2,32,256]{2,1,0:T(8,128)(2,1)S(1)} %get-tuple-element.17), channel_id=1, source_target_pairs={{0,16},{1,17},{2,18},{3,19},{4,20},{5,21},{6,22},{7,23},{8,24},{9,... | collective-permute-start | bytes 98312 | tf_op jit(solution)/shard_map/ppermute | solution.py:319
  55.8 3.9 %collective-permute-start.4 = (bf16[2,32,256]{2,1,0:T(8,128)(2,1)S(1)}, bf16[2,32,256]{2,1,0:T(8,128)(2,1)S(1)}, u32[]{:S(2)}, u32[]{:S(2)}) collective-permute-start(bf16[2,32,256]{2,1,0:T(8,128)(2,1)S(1)} %get-tuple-element.18), channel_id=1, source_target_pairs={{0,128},{128,0},{1,129},{129,1},{2,130},{130,2},{3,131},{131,3},{4... | collective-permute-start | bytes 98312 | tf_op jit(solution)/shard_map/ppermute | solution.py:320
  55.8 5.2 %collective-permute-start.5 = (bf16[2,32,256]{2,1,0:T(8,128)(2,1)S(1)}, bf16[2,32,256]{2,1,0:T(8,128)(2,1)S(1)}, u32[]{:S(2)}, u32[]{:S(2)}) collective-permute-start(bf16[2,32,256]{2,1,0:T(8,128)(2,1)S(1)} %get-tuple-element.19), channel_id=1, source_target_pairs={{0,144},{1,145},{2,146},{3,147},{4,148},{5,149},{6,150},{7,151},{8... | collective-permute-start | bytes 98312 | tf_op jit(solution)/shard_map/ppermute | solution.py:318
  61.0 8.6 %collective-permute-start.8 = (bf16[2,2,2,32,256]{4,3,2,1,0:T(8,128)(2,1)S(1)}, bf16[2,2,2,32,256]{4,3,2,1,0:T(8,128)(2,1)S(1)}, u32[]{:S(2)}, u32[]{:S(2)}) collective-permute-start(bf16[2,2,2,32,256]{4,3,2,1,0:T(8,128)(2,1)S(1)} %bitcast.46), channel_id=1, source_target_pairs={{0,96},{32,0},{64,32},{96,64},{1,97},{33,1},{65,33},{97,65},{2,98}... | collective-permute-start | bytes 393224 | tf_op jit(solution)/shard_map/ppermute | solution.py:325
  61.1 8.5 %collective-permute-start.7 = (bf16[2,2,2,32,256]{4,3,2,1,0:T(8,128)(2,1)S(1)}, bf16[2,2,2,32,256]{4,3,2,1,0:T(8,128)(2,1)S(1)}, u32[]{:S(2)}, u32[]{:S(2)}) collective-permute-start(bf16[2,2,2,32,256]{4,3,2,1,0:T(8,128)(2,1)S(1)} %bitcast.47), channel_id=1, source_target_pairs={{0,64},{32,96},{64,0},{96,32},{1,65},{33,97},{65,1},{97,33},{2,66}... | collective-permute-start | bytes 393224 | tf_op jit(solution)/shard_map/ppermute | solution.py:325
  61.8 8.4 %collective-permute-start.6 = (bf16[2,2,2,32,256]{4,3,2,1,0:T(8,128)(2,1)S(1)}, bf16[2,2,2,32,256]{4,3,2,1,0:T(8,128)(2,1)S(1)}, u32[]{:S(2)}, u32[]{:S(2)}) collective-permute-start(bf16[2,2,2,32,256]{4,3,2,1,0:T(8,128)(2,1)S(1)} %bitcast.48), channel_id=1, source_target_pairs={{0,32},{32,64},{64,96},{96,0},{1,33},{33,65},{65,97},{97,1},{2,34}... | collective-permute-start | bytes 393224 | tf_op jit(solution)/shard_map/ppermute | solution.py:325
  64.3 3.7 %collective-permute-start = (f32[1,384]{1,0:T(1,128)S(1)}, f32[1,384]{1,0:T(1,128)S(1)}, u32[]{:S(2)}, u32[]{:S(2)}) collective-permute-start(f32[1,384]{1,0:T(1,128)S(1)} %pad_maximum_fusion.1), channel_id=1, source_target_pairs={{0,128},{128,0},{1,129},{129,1},{2,130},{130,2},{3,131},{131,3},{4... | collective-permute-start | bytes 4616 | tf_op jit(solution)/shard_map/ppermute | solution.py:294
  73.2 44.3 %copy-start = (f32[32,64,256]{2,1,0:T(8,128)S(1)}, f32[32,64,256]{2,1,0:T(8,128)}, u32[]{:S(2)}) copy-start(f32[32,64,256]{2,1,0:T(8,128)} %est_ref.3) | copy-start | bytes 6291460
  76.5 7.1 %collective-permute-start.9 = (s16[32,8,256]{2,1,0:T(8,128)(2,1)S(1)}, s16[32,8,256]{2,1,0:T(8,128)(2,1)S(1)}, u32[]{:S(2)}, u32[]{:S(2)}) collective-permute-start(s16[32,8,256]{2,1,0:T(8,128)(2,1)S(1)} %get-tuple-element.9), channel_id=1, source_target_pairs={{0,64},{32,96},{64,0},{96,32},{1,65},{33,97},{65,1},{97,33},{2,66}... | collective-permute-start | bytes 393224 | tf_op jit(solution)/shard_map/ppermute | solution.py:354
  77.4 7.4 %collective-permute-start.11 = (s16[32,8,256]{2,1,0:T(8,128)(2,1)S(1)}, s16[32,8,256]{2,1,0:T(8,128)(2,1)S(1)}, u32[]{:S(2)}, u32[]{:S(2)}) collective-permute-start(s16[32,8,256]{2,1,0:T(8,128)(2,1)S(1)} %get-tuple-element.10), channel_id=1, source_target_pairs={{0,96},{32,0},{64,32},{96,64},{1,97},{33,1},{65,33},{97,65},{2,98}... | collective-permute-start | bytes 393224 | tf_op jit(solution)/shard_map/ppermute | solution.py:354
  79.7 5.6 %collective-permute-start.10 = (s16[32,8,256]{2,1,0:T(8,128)(2,1)S(1)}, s16[32,8,256]{2,1,0:T(8,128)(2,1)S(1)}, u32[]{:S(2)}, u32[]{:S(2)}) collective-permute-start(s16[32,8,256]{2,1,0:T(8,128)(2,1)S(1)} %get-tuple-element.11), channel_id=1, source_target_pairs={{0,32},{32,64},{64,96},{96,0},{1,33},{33,65},{65,97},{97,1},{2,34}... | collective-permute-start | bytes 393224 | tf_op jit(solution)/shard_map/ppermute | solution.py:354
  101.5 9.8 %collective-permute-start.16 = (s16[8,32,256]{2,1,0:T(8,128)(2,1)S(1)}, s16[8,32,256]{2,1,0:T(8,128)(2,1)S(1)}, u32[]{:S(2)}, u32[]{:S(2)}) collective-permute-start(s16[8,32,256]{2,1,0:T(8,128)(2,1)S(1)} %bitcast.38), channel_id=1, source_target_pairs={{0,32},{32,64},{64,96},{96,0},{128,160},{160,192},{192,224},{224,1... | collective-permute-start | bytes 393224 | tf_op jit(solution)/shard_map/ppermute | solution.py:362
  104.2 13.3 %collective-permute-start.15 = (s16[8,32,256]{2,1,0:T(8,128)(2,1)S(1)}, s16[8,32,256]{2,1,0:T(8,128)(2,1)S(1)}, u32[]{:S(2)}, u32[]{:S(2)}) collective-permute-start(s16[8,32,256]{2,1,0:T(8,128)(2,1)S(1)} %bitcast.39), channel_id=1, source_target_pairs={{0,224},{32,128},{64,160},{96,192},{128,96},{160,0},{192,32},{224,... | collective-permute-start | bytes 393224 | tf_op jit(solution)/shard_map/ppermute | solution.py:362
  104.2 13.3 %collective-permute-start.14 = (s16[8,32,256]{2,1,0:T(8,128)(2,1)S(1)}, s16[8,32,256]{2,1,0:T(8,128)(2,1)S(1)}, u32[]{:S(2)}, u32[]{:S(2)}) collective-permute-start(s16[8,32,256]{2,1,0:T(8,128)(2,1)S(1)} %bitcast.40), channel_id=1, source_target_pairs={{0,160},{32,192},{64,224},{96,128},{128,32},{160,64},{192,96},{224... | collective-permute-start | bytes 393224 | tf_op jit(solution)/shard_map/ppermute | solution.py:362
  108.3 9.1 %collective-permute-start.13 = (s16[8,32,256]{2,1,0:T(8,128)(2,1)S(1)}, s16[8,32,256]{2,1,0:T(8,128)(2,1)S(1)}, u32[]{:S(2)}, u32[]{:S(2)}) collective-permute-start(s16[8,32,256]{2,1,0:T(8,128)(2,1)S(1)} %bitcast.41), channel_id=1, source_target_pairs={{0,64},{32,96},{64,0},{96,32},{128,192},{160,224},{192,128},{224,1... | collective-permute-start | bytes 393224 | tf_op jit(solution)/shard_map/ppermute | solution.py:362
  108.3 9.1 %collective-permute-start.12 = (s16[8,32,256]{2,1,0:T(8,128)(2,1)S(1)}, s16[8,32,256]{2,1,0:T(8,128)(2,1)S(1)}, u32[]{:S(2)}, u32[]{:S(2)}) collective-permute-start(s16[8,32,256]{2,1,0:T(8,128)(2,1)S(1)} %bitcast.42), channel_id=1, source_target_pairs={{0,192},{32,224},{64,128},{96,160},{128,64},{160,96},{192,0},{224,... | collective-permute-start | bytes 393224 | tf_op jit(solution)/shard_map/ppermute | solution.py:362
  111.3 7.7 %collective-permute-start.18 = (s16[8,32,256]{2,1,0:T(8,128)(2,1)S(1)}, s16[8,32,256]{2,1,0:T(8,128)(2,1)S(1)}, u32[]{:S(2)}, u32[]{:S(2)}) collective-permute-start(s16[8,32,256]{2,1,0:T(8,128)(2,1)S(1)} %bitcast.43), channel_id=1, source_target_pairs={{0,128},{32,160},{64,192},{96,224},{128,0},{160,32},{192,64},{224,... | collective-permute-start | bytes 393224 | tf_op jit(solution)/shard_map/ppermute | solution.py:362
  117.5 6.2 %collective-permute-start.17 = (s16[8,32,256]{2,1,0:T(8,128)(2,1)S(1)}, s16[8,32,256]{2,1,0:T(8,128)(2,1)S(1)}, u32[]{:S(2)}, u32[]{:S(2)}) collective-permute-start(s16[8,32,256]{2,1,0:T(8,128)(2,1)S(1)} %bitcast.44), channel_id=1, source_target_pairs={{0,96},{32,0},{64,32},{96,64},{128,224},{160,128},{192,160},{224,1... | collective-permute-start | bytes 393224 | tf_op jit(solution)/shard_map/ppermute | solution.py:362

commit v5 on v4

--- a/solution.py
+++ b/solution.py
@@ -215,13 +215,13 @@
         copy.wait()
 
 
-def last_kernel(places, est_ref, *refs):
+def later_kernel(places, skip, est_ref, *refs):
     count = len(places)
     codes, (out_ref, parts_ref, sem) = refs[:count], refs[count + 1 :]
     stores = []
     for p, (u, d) in enumerate(places):
         rows, lines = part_of(u, d)
-        apply_codes(codes[p], est_ref.at[p], parts_ref.at[p])
+        apply_codes(codes[p], est_ref.at[skip + p], parts_ref.at[p])
         store = pltpu.make_async_copy(parts_ref.at[p], out_ref.at[rows, lines], sem.at[p])
         store.start()
         stores.append(store)
@@ -229,11 +229,17 @@
         store.wait()
 
 
-def finish(places, estimate, pieces, early):
+def finish(places, estimate, pieces, early, middle):
     whole = jax.ShapeDtypeStruct((32, 64, LENGTH), jnp.float32)
     part = (8, 32, LENGTH)
     late = len(places) - early
-    first, rest = pl.pallas_call(
+
+    def cost(count):
+        return pl.CostEstimate(
+            flops=count << 17, bytes_accessed=count << 19, transcendentals=count << 16
+        )
+
+    result, rest = pl.pallas_call(
         functools.partial(first_kernel, places[:early], places[early:]),
         out_shape=(whole, jax.ShapeDtypeStruct((late, *part), jnp.float32)),
         in_specs=[ANY] + [VMEM] * early,
@@ -243,25 +249,27 @@
             pltpu.SemaphoreType.DMA((early + late,)),
             pltpu.SemaphoreType.DMA((early,)),
         ],
-        cost_estimate=pl.CostEstimate(
-            flops=early << 17, bytes_accessed=early << 19, transcendentals=early << 16
-        ),
-        compiler_params=pltpu.CompilerParams(vmem_limit_bytes=32 << 19),
+        cost_estimate=cost(early),
+        compiler_params=pltpu.CompilerParams(vmem_limit_bytes=16 << 20),
         name="first_kernel",
     )(estimate, *pieces[:early])
-    return pl.pallas_call(
-        functools.partial(last_kernel, places[early:]),
-        out_shape=whole,
-        in_specs=[VMEM] * (1 + late) + [ANY],
-        out_specs=ANY,
-        scratch_shapes=[
-            pltpu.VMEM((late, *part), jnp.float32),
-            pltpu.SemaphoreType.DMA((late,)),
-        ],
-        input_output_aliases={1 + late: 0},
-        compiler_params=pltpu.CompilerParams(vmem_limit_bytes=16 << 20),
-        name="last_kernel",
-    )(rest, *pieces[early:], first)
+    for start, stop in ((early, early + middle), (early + middle, len(places))):
+        count = stop - start
+        result = pl.pallas_call(
+            functools.partial(later_kernel, places[start:stop], start - early),
+            out_shape=whole,
+            in_specs=[VMEM] * (1 + count) + [ANY],
+            out_specs=ANY,
+            scratch_shapes=[
+                pltpu.VMEM((count, *part), jnp.float32),
+                pltpu.SemaphoreType.DMA((count,)),
+            ],
+            input_output_aliases={1 + count: 0},
+            cost_estimate=cost(count),
+            compiler_params=pltpu.CompilerParams(vmem_limit_bytes=16 << 20),
+            name="later_kernel",
+        )(rest, *pieces[start:stop], result)
+    return result
 
 
 def distance_route():
@@ -351,7 +359,8 @@
     total = codes[0].astype(jnp.int32)
     for d in (2, 1, 3):
         route = [(i, (i + d) % 4) for i in range(4)]
-        total += lax.ppermute(codes[d], "column", route).astype(jnp.int32)
+        arrived = lax.ppermute(codes[d], "column", route)
+        total += arrived.astype(jnp.int32)
     logs = ((total + 2) >> 2).astype(jnp.int16)
     logs = lax.all_to_all(logs, "tile", 0, 0, tiled=True)
     logs = logs.transpose(1, 0, 2)
@@ -360,7 +369,7 @@
     for u, d in places[1:]:
         route = [(i, 4 * ((i // 4 + u) % 2) + (i + d) % 4) for i in range(8)]
         pieces.append(lax.ppermute(logs, ("upper", "column"), route))
-    return finish(places, estimate, pieces, 6)
+    return finish(places, estimate, pieces, 4, 2)
 
 
 def solution(mesh):

time: 125 us -> 119 us (0.952)
  the two profiles are of different devices: /device:TPU:6 before, /device:TPU:1 now
where the time goes in v5:
time: 119 us
  starting transfers between devices  69.5 us (58%)
  waiting for transfers between devices  17.6 us (15%)
  blocking collectives  16 us (13%)
  Pallas kernels  11.3 us (9%)
  local copies, waits for them, and re-layouts  2.87 us (2%)
  between operations  1.64 us (1%)
    ppermute x1, starting transfers between devices, update(): beside = lax.ppermute(other_line[0], 'upper', swap)  32.2 us
    all_to_all x1, blocking collectives, update(): logs = lax.all_to_all(logs, 'tile', 0, 0, tiled=True)  16 us
    all_to_all x1, starting transfers between devices, update(): image_lines = lax.all_to_all(image, ('upper', 'tile'), 0, 0, tiled=True)  13.1 us
    ppermute x7, starting transfers between devices, update(): pieces.append(lax.ppermute(logs, ('upper', 'column'), route))  10.5 us
    ppermute x3, waiting for transfers between devices, update(): arrived = lax.ppermute(codes[d], 'column', route)  6.35 us
    ppermute x3, starting transfers between devices, update(): est_lines.append(lax.ppermute(piece, 'column', route))  5.92 us
    ppermute x7, waiting for transfers between devices, update(): pieces.append(lax.ppermute(logs, ('upper', 'column'), route))  3.39 us
    pallas_call x1, Pallas kernels, update(): pl.pallas_call(back_kernel, out_shape=jax.ShapeDtypeStruct((4, SLABS, 8,...  3.26 us
  transfers between devices with their start and end apart: 20, of which 11 were waited for; matrix products, arithmetic and copies ran while one was open for 0% of the time, Pallas kernels for 6%

profile of v5, /device:TPU:1, one launch (start us, length us, event | category | flops | bytes accessed | tf_op | source)
XLA Modules:
  0.0 119.2 jit_solution(8650741003245826465)
XLA Ops:
  0.0 2.8 %copy.17 = bf16[1,32,64,256]{3,1,2,0:T(8,128)(2,1)} copy(bf16[1,32,64,256]{3,2,1,0:T(8,128)(2,1)} %param.6) | data formatting | bytes 2097152 | tf_op args[1]
  2.8 13.1 %all-to-all-start = ((bf16[64,32,256]{2,1,0:T(8,128)(2,1)}), bf16[64,32,256]{2,1,0:T(8,128)(2,1)S(1)}, u32[]{:S(2)}, u32[]{:S(2)}) async-start(bf16[64,32,256]{2,1,0:T(8,128)(2,1)} %bitcast.36), calls=%async_computation | async-start | bytes 2097152 | tf_op jit(solution)/shard_map/all_to_all | solution.py:320
  15.9 0.0 copy-start.1
  15.9 2.1 %pick_kernel.1 = bf16[2,2,2,32,256]{4,3,2,1,0:T(8,128)(2,1)} custom-call(f32[32,64,256]{2,1,0:T(8,128)} %est_ref.3), custom_call_target="tpu_custom_call" | custom-call | bytes 2097152 | tf_op jit(solution)/shard_map/pick_kernel/pallas_call | solution.py:305
  18.0 1.6 %collective-permute-start.1 = (bf16[2,2,2,32,256]{4,3,2,1,0:T(8,128)(2,1)}, bf16[2,2,2,32,256]{4,3,2,1,0:T(8,128)(2,1)S(1)}, u32[]{:S(2)}, u32[]{:S(2)}) collective-permute-start(bf16[2,2,2,32,256]{4,3,2,1,0:T(8,128)(2,1)} %pick_kernel.1), channel_id=1, source_target_pairs={{0,0},{1,1},{2,2},{3,3},{4,4},{5,5},{6,6},{7,7},{8,8},{9,9},{10,10... | collective-permute-start | bytes 393224 | tf_op jit(solution)/shard_map/ppermute | solution.py:318
  19.6 0.0 collective-permute-done.1
  19.6 0.5 collective-permute-start.2
  21.4 0.0 collective-permute-done.2
  21.5 32.2 %collective-permute-start.4 = (bf16[2,32,256]{2,1,0:T(8,128)(2,1)S(1)}, bf16[2,32,256]{2,1,0:T(8,128)(2,1)S(1)}, u32[]{:S(2)}, u32[]{:S(2)}) collective-permute-start(bf16[2,32,256]{2,1,0:T(8,128)(2,1)S(1)} %get-tuple-element.18), channel_id=1, source_target_pairs={{0,128},{128,0},{1,129},{129,1},{2,130},{130,2},{3,131},{131,3},{4... | collective-permute-start | bytes 98312 | tf_op jit(solution)/shard_map/ppermute | solution.py:328
  53.6 1.4 %collective-permute-start.5 = (bf16[2,32,256]{2,1,0:T(8,128)(2,1)S(1)}, bf16[2,32,256]{2,1,0:T(8,128)(2,1)S(1)}, u32[]{:S(2)}, u32[]{:S(2)}) collective-permute-start(bf16[2,32,256]{2,1,0:T(8,128)(2,1)S(1)} %get-tuple-element.19), channel_id=1, source_target_pairs={{0,144},{1,145},{2,146},{3,147},{4,148},{5,149},{6,150},{7,151},{8... | collective-permute-start | bytes 98312 | tf_op jit(solution)/shard_map/ppermute | solution.py:326
  55.1 1.2 collective-permute-start.3
  56.2 0.1 add_convert_fusion
  56.3 0.0 collective-permute-done.4
  56.3 1.3 %collective-permute-done.5 = bf16[2,32,256]{2,1,0:T(8,128)(2,1)S(1)} collective-permute-done((bf16[2,32,256]{2,1,0:T(8,128)(2,1)S(1)}, bf16[2,32,256]{2,1,0:T(8,128)(2,1)S(1)}, u32[]{:S(2)}, u32[]{:S(2)}) %collective-permute-start.5) | collective-permute-done | bytes 32800 | tf_op jit(solution)/shard_map/ppermute | solution.py:326
  57.6 1.7 %collective-permute-done.3 = bf16[2,32,256]{2,1,0:T(8,128)(2,1)S(1)} collective-permute-done((bf16[2,32,256]{2,1,0:T(8,128)(2,1)S(1)}, bf16[2,32,256]{2,1,0:T(8,128)(2,1)S(1)}, u32[]{:S(2)}, u32[]{:S(2)}) %collective-permute-start.3) | collective-permute-done | bytes 32800 | tf_op jit(solution)/shard_map/ppermute | solution.py:327
  59.4 0.1 collective-permute-start.6
  59.5 5.8 %collective-permute-start.7 = (bf16[2,2,2,32,256]{4,3,2,1,0:T(8,128)(2,1)S(1)}, bf16[2,2,2,32,256]{4,3,2,1,0:T(8,128)(2,1)S(1)}, u32[]{:S(2)}, u32[]{:S(2)}) collective-permute-start(bf16[2,2,2,32,256]{4,3,2,1,0:T(8,128)(2,1)S(1)} %bitcast.47), channel_id=1, source_target_pairs={{0,64},{32,96},{64,0},{96,32},{1,65},{33,97},{65,1},{97,33},{2,66}... | collective-permute-start | bytes 393224 | tf_op jit(solution)/shard_map/ppermute | solution.py:333
  65.3 0.0 collective-permute-start.8
  65.3 0.1 collective-permute-start
  65.4 2.7 %collective-permute-done.other_ref.other_profile_ref = f32[1,384]{1,0:T(1,128)S(1)} collective-permute-done((f32[1,384]{1,0:T(1,128)S(1)}, f32[1,384]{1,0:T(1,128)S(1)}, u32[]{:S(2)}, u32[]{:S(2)}) %collective-permute-start) | collective-permute-done | bytes 1568 | tf_op jit(solution)/shard_map/ppermute | solution.py:302
  68.1 0.0 collective-permute-done.6.est1_ref
  68.1 1.5 %collective-permute-done.7.est2_ref = bf16[2,2,2,32,256]{4,3,2,1,0:T(8,128)(2,1)S(1)} collective-permute-done((bf16[2,2,2,32,256]{4,3,2,1,0:T(8,128)(2,1)S(1)}, bf16[2,2,2,32,256]{4,3,2,1,0:T(8,128)(2,1)S(1)}, u32[]{:S(2)}, u32[]{:S(2)}) %collective-permute-start.7) | collective-permute-done | bytes 131104 | tf_op jit(solution)/shard_map/ppermute | solution.py:333
  69.7 0.6 collective-permute-done.8.est3_ref
  70.3 3.0 %forward_kernel.1.inverse_ref = f32[2,1024,256]{2,1,0:T(8,128)S(1)} custom-call(s32[1]{0:T(128)S(6)} %copy.22.shift_ref, s32[1]{0:T(128)S(6)} %copy.21.offset_ref, f32[1,384]{1,0:T(1,128)S(1)} %collective-permute-done.other_ref.other_profile_ref, f32[1,256]{1,0:T(1,128)S(1)} %copy-done.1, f32[1,384]{1,0:T(1,128)S(1)} %collective-permute-done.other_ref.other_profile_ref, ...), custom_call_target="tpu_custom_call" | custom-call | flops 268435456 | bytes 8388608 | tf_op jit(solution)/shard_map/forward_kernel/pallas_call | solution.py:335
  73.3 0.0 all-to-all-done.image_ref
  73.3 0.0 copy-start
  73.3 3.3 %back_kernel.1 = s16[4,32,8,256]{3,2,1,0:T(8,128)(2,1)S(1)} custom-call(s32[1]{0:T(128)S(6)} %copy.22.shift_ref, s32[1]{0:T(128)S(6)} %copy.21.offset_ref, f32[1,384]{1,0:T(1,128)S(1)} %collective-permute-done.other_ref.other_profile_ref, f32[1,256]{1,0:T(1,128)S(1)} %copy-done.1, f32[1,384]{1,0:T(1,128)S(1)} %collective-permute-done.other_ref.other_profile_ref, ...), custom_call_target="tpu_custom_call" | custom-call | tf_op jit(solution)/shard_map/back_kernel/pallas_call | solution.py:347
  76.6 0.1 collective-permute-start.10
  76.7 2.7 %collective-permute-start.11 = (s16[32,8,256]{2,1,0:T(8,128)(2,1)S(1)}, s16[32,8,256]{2,1,0:T(8,128)(2,1)S(1)}, u32[]{:S(2)}, u32[]{:S(2)}) collective-permute-start(s16[32,8,256]{2,1,0:T(8,128)(2,1)S(1)} %get-tuple-element.10), channel_id=1, source_target_pairs={{0,96},{32,0},{64,32},{96,64},{1,97},{33,1},{65,33},{97,65},{2,98}... | collective-permute-start | bytes 393224 | tf_op jit(solution)/shard_map/ppermute | solution.py:362
  79.3 0.2 collective-permute-start.9
  79.6 2.1 %collective-permute-done.10 = s16[32,8,256]{2,1,0:T(8,128)(2,1)S(1)} collective-permute-done((s16[32,8,256]{2,1,0:T(8,128)(2,1)S(1)}, s16[32,8,256]{2,1,0:T(8,128)(2,1)S(1)}, u32[]{:S(2)}, u32[]{:S(2)}) %collective-permute-start.10) | collective-permute-done | bytes 131104 | tf_op jit(solution)/shard_map/ppermute | solution.py:362
  81.7 1.0 collective-permute-done.11
  82.7 3.3 %collective-permute-done.9 = s16[32,8,256]{2,1,0:T(8,128)(2,1)S(1)} collective-permute-done((s16[32,8,256]{2,1,0:T(8,128)(2,1)S(1)}, s16[32,8,256]{2,1,0:T(8,128)(2,1)S(1)}, u32[]{:S(2)}, u32[]{:S(2)}) %collective-permute-start.9) | collective-permute-done | bytes 131104 | tf_op jit(solution)/shard_map/ppermute | solution.py:362
  85.9 0.2 fusion.4
  86.1 16.0 %all_to_all.10 = s16[32,8,256]{2,1,0:T(8,128)(2,1)S(1)} all-to-all(s16[32,8,256]{2,1,0:T(8,128)(2,1)S(1)} %fusion.4), channel_id=1, replica_groups=mesh['upper'=2,'column'=4,'tile'=32] {'tile'}, dimensions={0} | all-to-all | bytes 262144 | tf_op jit(solution)/shard_map/all_to_all | solution.py:365
  102.1 1.1 collective-permute-start.12
  103.2 2.0 %collective-permute-start.13 = (s16[8,32,256]{2,1,0:T(8,128)(2,1)S(1)}, s16[8,32,256]{2,1,0:T(8,128)(2,1)S(1)}, u32[]{:S(2)}, u32[]{:S(2)}) collective-permute-start(s16[8,32,256]{2,1,0:T(8,128)(2,1)S(1)} %bitcast.39), channel_id=1, source_target_pairs={{0,64},{32,96},{64,0},{96,32},{128,192},{160,224},{192,128},{224,1... | collective-permute-start | bytes 393224 | tf_op jit(solution)/shard_map/ppermute | solution.py:371
  105.1 1.1 collective-permute-start.14
  106.2 2.5 %collective-permute-start.17 = (s16[8,32,256]{2,1,0:T(8,128)(2,1)S(1)}, s16[8,32,256]{2,1,0:T(8,128)(2,1)S(1)}, u32[]{:S(2)}, u32[]{:S(2)}) collective-permute-start(s16[8,32,256]{2,1,0:T(8,128)(2,1)S(1)} %bitcast.41), channel_id=1, source_target_pairs={{0,224},{32,128},{64,160},{96,192},{128,96},{160,0},{192,32},{224,... | collective-permute-start | bytes 393224 | tf_op jit(solution)/shard_map/ppermute | solution.py:371
  108.7 2.7 %collective-permute-start.15 = (s16[8,32,256]{2,1,0:T(8,128)(2,1)S(1)}, s16[8,32,256]{2,1,0:T(8,128)(2,1)S(1)}, u32[]{:S(2)}, u32[]{:S(2)}) collective-permute-start(s16[8,32,256]{2,1,0:T(8,128)(2,1)S(1)} %bitcast.43), channel_id=1, source_target_pairs={{0,96},{32,0},{64,32},{96,64},{128,224},{160,128},{192,160},{224,1... | collective-permute-start | bytes 393224 | tf_op jit(solution)/shard_map/ppermute | solution.py:371
  111.4 0.0 collective-permute-done.13.refs_2_
  111.4 1.2 collective-permute-start.16
  112.6 2.0 %collective-permute-done.14.refs_3_ = s16[8,32,256]{2,1,0:T(8,128)(2,1)S(1)} collective-permute-done((s16[8,32,256]{2,1,0:T(8,128)(2,1)S(1)}, s16[8,32,256]{2,1,0:T(8,128)(2,1)S(1)}, u32[]{:S(2)}, u32[]{:S(2)}) %collective-permute-start.14) | collective-permute-done | bytes 131104 | tf_op jit(solution)/shard_map/ppermute | solution.py:371
  114.5 1.3 %first_kernel.1 = (f32[32,64,256]{2,1,0:T(8,128)}, f32[4,8,32,256]{3,2,1,0:T(8,128)S(1)}) custom-call(f32[32,64,256]{2,1,0:T(8,128)S(1)} %copy-done, s16[8,32,256]{2,1,0:T(8,128)(2,1)S(1)} %bitcast.45, s16[8,32,256]{2,1,0:T(8,128)(2,1)S(1)} %collective-permute-done.12.refs_1_, s16[8,32,256]{2,1,0:T(8,128)(2,1)S(1)} %collective-permute-done.13.refs_2_, ...), custom_call_target="tpu_custom_call" | custom-call | flops 524288 | bytes 2097152 | tf_op jit(solution)/shard_map/first_kernel/pallas_call | solution.py:242
  115.9 0.5 collective-permute-done.18.refs_1_
  116.3 0.9 later_kernel.2.refs_2_
  117.2 1.0 collective-permute-done.16.refs_1_
  118.2 0.9 later_kernel.3
  (15 shorter events, 0.1 us)
Async XLA Ops:
  2.8 70.5 %all-to-all-start = ((bf16[64,32,256]{2,1,0:T(8,128)(2,1)}), bf16[64,32,256]{2,1,0:T(8,128)(2,1)S(1)}, u32[]{:S(2)}, u32[]{:S(2)}) async-start(bf16[64,32,256]{2,1,0:T(8,128)(2,1)} %bitcast.36), calls=%async_computation | async-start | bytes 2097152 | tf_op jit(solution)/shard_map/all_to_all | solution.py:320
  15.9 49.4 %copy-start.1 = (f32[1,256]{1,0:T(1,128)S(1)}, f32[1,256]{1,0:T(1,128)}, u32[]{:S(2)}) copy-start(f32[1,256]{1,0:T(1,128)} %own_profile_ref.3) | copy-start | bytes 3076
  18.0 1.6 %collective-permute-start.1 = (bf16[2,2,2,32,256]{4,3,2,1,0:T(8,128)(2,1)}, bf16[2,2,2,32,256]{4,3,2,1,0:T(8,128)(2,1)S(1)}, u32[]{:S(2)}, u32[]{:S(2)}) collective-permute-start(bf16[2,2,2,32,256]{4,3,2,1,0:T(8,128)(2,1)} %pick_kernel.1), channel_id=1, source_target_pairs={{0,0},{1,1},{2,2},{3,3},{4,4},{5,5},{6,6},{7,7},{8,8},{9,9},{10,10... | collective-permute-start | bytes 393224 | tf_op jit(solution)/shard_map/ppermute | solution.py:318
  19.6 1.8 %collective-permute-start.2 = (bf16[2,2,32,256]{3,2,1,0:T(8,128)(2,1)S(1)}, bf16[2,2,32,256]{3,2,1,0:T(8,128)(2,1)S(1)}, u32[]{:S(2)}, u32[]{:S(2)}) collective-permute-start(bf16[2,2,32,256]{3,2,1,0:T(8,128)(2,1)S(1)} %get-tuple-element.14), channel_id=1, source_target_pairs={{0,1},{1,0},{2,3},{3,2},{4,5},{5,4},{6,7},{7,6},{8,9},{9,8},{10,11... | collective-permute-start | bytes 196616 | tf_op jit(solution)/shard_map/ppermute | solution.py:289
  21.5 34.8 %collective-permute-start.4 = (bf16[2,32,256]{2,1,0:T(8,128)(2,1)S(1)}, bf16[2,32,256]{2,1,0:T(8,128)(2,1)S(1)}, u32[]{:S(2)}, u32[]{:S(2)}) collective-permute-start(bf16[2,32,256]{2,1,0:T(8,128)(2,1)S(1)} %get-tuple-element.18), channel_id=1, source_target_pairs={{0,128},{128,0},{1,129},{129,1},{2,130},{130,2},{3,131},{131,3},{4... | collective-permute-start | bytes 98312 | tf_op jit(solution)/shard_map/ppermute | solution.py:328
  53.6 4.0 %collective-permute-start.5 = (bf16[2,32,256]{2,1,0:T(8,128)(2,1)S(1)}, bf16[2,32,256]{2,1,0:T(8,128)(2,1)S(1)}, u32[]{:S(2)}, u32[]{:S(2)}) collective-permute-start(bf16[2,32,256]{2,1,0:T(8,128)(2,1)S(1)} %get-tuple-element.19), channel_id=1, source_target_pairs={{0,144},{1,145},{2,146},{3,147},{4,148},{5,149},{6,150},{7,151},{8... | collective-permute-start | bytes 98312 | tf_op jit(solution)/shard_map/ppermute | solution.py:326
  55.1 4.3 %collective-permute-start.3 = (bf16[2,32,256]{2,1,0:T(8,128)(2,1)S(1)}, bf16[2,32,256]{2,1,0:T(8,128)(2,1)S(1)}, u32[]{:S(2)}, u32[]{:S(2)}) collective-permute-start(bf16[2,32,256]{2,1,0:T(8,128)(2,1)S(1)} %get-tuple-element.17), channel_id=1, source_target_pairs={{0,16},{1,17},{2,18},{3,19},{4,20},{5,21},{6,22},{7,23},{8,24},{9,... | collective-permute-start | bytes 98312 | tf_op jit(solution)/shard_map/ppermute | solution.py:327
  59.4 8.8 %collective-permute-start.6 = (bf16[2,2,2,32,256]{4,3,2,1,0:T(8,128)(2,1)S(1)}, bf16[2,2,2,32,256]{4,3,2,1,0:T(8,128)(2,1)S(1)}, u32[]{:S(2)}, u32[]{:S(2)}) collective-permute-start(bf16[2,2,2,32,256]{4,3,2,1,0:T(8,128)(2,1)S(1)} %bitcast.46), channel_id=1, source_target_pairs={{0,32},{32,64},{64,96},{96,0},{1,33},{33,65},{65,97},{97,1},{2,34}... | collective-permute-start | bytes 393224 | tf_op jit(solution)/shard_map/ppermute | solution.py:333
  59.5 10.2 %collective-permute-start.7 = (bf16[2,2,2,32,256]{4,3,2,1,0:T(8,128)(2,1)S(1)}, bf16[2,2,2,32,256]{4,3,2,1,0:T(8,128)(2,1)S(1)}, u32[]{:S(2)}, u32[]{:S(2)}) collective-permute-start(bf16[2,2,2,32,256]{4,3,2,1,0:T(8,128)(2,1)S(1)} %bitcast.47), channel_id=1, source_target_pairs={{0,64},{32,96},{64,0},{96,32},{1,65},{33,97},{65,1},{97,33},{2,66}... | collective-permute-start | bytes 393224 | tf_op jit(solution)/shard_map/ppermute | solution.py:333
  65.3 5.0 %collective-permute-start.8 = (bf16[2,2,2,32,256]{4,3,2,1,0:T(8,128)(2,1)S(1)}, bf16[2,2,2,32,256]{4,3,2,1,0:T(8,128)(2,1)S(1)}, u32[]{:S(2)}, u32[]{:S(2)}) collective-permute-start(bf16[2,2,2,32,256]{4,3,2,1,0:T(8,128)(2,1)S(1)} %bitcast.48), channel_id=1, source_target_pairs={{0,96},{32,0},{64,32},{96,64},{1,97},{33,1},{65,33},{97,65},{2,98}... | collective-permute-start | bytes 393224 | tf_op jit(solution)/shard_map/ppermute | solution.py:333
  65.3 2.8 %collective-permute-start = (f32[1,384]{1,0:T(1,128)S(1)}, f32[1,384]{1,0:T(1,128)S(1)}, u32[]{:S(2)}, u32[]{:S(2)}) collective-permute-start(f32[1,384]{1,0:T(1,128)S(1)} %pad_maximum_fusion.1), channel_id=1, source_target_pairs={{0,128},{128,0},{1,129},{129,1},{2,130},{130,2},{3,131},{131,3},{4... | collective-permute-start | bytes 4616 | tf_op jit(solution)/shard_map/ppermute | solution.py:302
  73.3 41.3 %copy-start = (f32[32,64,256]{2,1,0:T(8,128)S(1)}, f32[32,64,256]{2,1,0:T(8,128)}, u32[]{:S(2)}) copy-start(f32[32,64,256]{2,1,0:T(8,128)} %est_ref.3) | copy-start | bytes 6291460
  76.6 5.1 %collective-permute-start.10 = (s16[32,8,256]{2,1,0:T(8,128)(2,1)S(1)}, s16[32,8,256]{2,1,0:T(8,128)(2,1)S(1)}, u32[]{:S(2)}, u32[]{:S(2)}) collective-permute-start(s16[32,8,256]{2,1,0:T(8,128)(2,1)S(1)} %get-tuple-element.11), channel_id=1, source_target_pairs={{0,32},{32,64},{64,96},{96,0},{1,33},{33,65},{65,97},{97,1},{2,34}... | collective-permute-start | bytes 393224 | tf_op jit(solution)/shard_map/ppermute | solution.py:362
  76.7 6.0 %collective-permute-start.11 = (s16[32,8,256]{2,1,0:T(8,128)(2,1)S(1)}, s16[32,8,256]{2,1,0:T(8,128)(2,1)S(1)}, u32[]{:S(2)}, u32[]{:S(2)}) collective-permute-start(s16[32,8,256]{2,1,0:T(8,128)(2,1)S(1)} %get-tuple-element.10), channel_id=1, source_target_pairs={{0,96},{32,0},{64,32},{96,64},{1,97},{33,1},{65,33},{97,65},{2,98}... | collective-permute-start | bytes 393224 | tf_op jit(solution)/shard_map/ppermute | solution.py:362
  79.3 6.6 %collective-permute-start.9 = (s16[32,8,256]{2,1,0:T(8,128)(2,1)S(1)}, s16[32,8,256]{2,1,0:T(8,128)(2,1)S(1)}, u32[]{:S(2)}, u32[]{:S(2)}) collective-permute-start(s16[32,8,256]{2,1,0:T(8,128)(2,1)S(1)} %get-tuple-element.9), channel_id=1, source_target_pairs={{0,64},{32,96},{64,0},{96,32},{1,65},{33,97},{65,1},{97,33},{2,66}... | collective-permute-start | bytes 393224 | tf_op jit(solution)/shard_map/ppermute | solution.py:362
  102.1 6.6 %collective-permute-start.12 = (s16[8,32,256]{2,1,0:T(8,128)(2,1)S(1)}, s16[8,32,256]{2,1,0:T(8,128)(2,1)S(1)}, u32[]{:S(2)}, u32[]{:S(2)}) collective-permute-start(s16[8,32,256]{2,1,0:T(8,128)(2,1)S(1)} %bitcast.38), channel_id=1, source_target_pairs={{0,192},{32,224},{64,128},{96,160},{128,64},{160,96},{192,0},{224,... | collective-permute-start | bytes 393224 | tf_op jit(solution)/shard_map/ppermute | solution.py:371
  103.2 8.2 %collective-permute-start.13 = (s16[8,32,256]{2,1,0:T(8,128)(2,1)S(1)}, s16[8,32,256]{2,1,0:T(8,128)(2,1)S(1)}, u32[]{:S(2)}, u32[]{:S(2)}) collective-permute-start(s16[8,32,256]{2,1,0:T(8,128)(2,1)S(1)} %bitcast.39), channel_id=1, source_target_pairs={{0,64},{32,96},{64,0},{96,32},{128,192},{160,224},{192,128},{224,1... | collective-permute-start | bytes 393224 | tf_op jit(solution)/shard_map/ppermute | solution.py:371
  105.1 9.4 %collective-permute-start.14 = (s16[8,32,256]{2,1,0:T(8,128)(2,1)S(1)}, s16[8,32,256]{2,1,0:T(8,128)(2,1)S(1)}, u32[]{:S(2)}, u32[]{:S(2)}) collective-permute-start(s16[8,32,256]{2,1,0:T(8,128)(2,1)S(1)} %bitcast.40), channel_id=1, source_target_pairs={{0,160},{32,192},{64,224},{96,128},{128,32},{160,64},{192,96},{224... | collective-permute-start | bytes 393224 | tf_op jit(solution)/shard_map/ppermute | solution.py:371
  106.2 9.6 %collective-permute-start.17 = (s16[8,32,256]{2,1,0:T(8,128)(2,1)S(1)}, s16[8,32,256]{2,1,0:T(8,128)(2,1)S(1)}, u32[]{:S(2)}, u32[]{:S(2)}) collective-permute-start(s16[8,32,256]{2,1,0:T(8,128)(2,1)S(1)} %bitcast.41), channel_id=1, source_target_pairs={{0,224},{32,128},{64,160},{96,192},{128,96},{160,0},{192,32},{224,... | collective-permute-start | bytes 393224 | tf_op jit(solution)/shard_map/ppermute | solution.py:371
  108.7 7.6 %collective-permute-start.18 = (s16[8,32,256]{2,1,0:T(8,128)(2,1)S(1)}, s16[8,32,256]{2,1,0:T(8,128)(2,1)S(1)}, u32[]{:S(2)}, u32[]{:S(2)}) collective-permute-start(s16[8,32,256]{2,1,0:T(8,128)(2,1)S(1)} %bitcast.42), channel_id=1, source_target_pairs={{0,32},{32,64},{64,96},{96,0},{128,160},{160,192},{192,224},{224,1... | collective-permute-start | bytes 393224 | tf_op jit(solution)/shard_map/ppermute | solution.py:371
  108.7 8.5 %collective-permute-start.15 = (s16[8,32,256]{2,1,0:T(8,128)(2,1)S(1)}, s16[8,32,256]{2,1,0:T(8,128)(2,1)S(1)}, u32[]{:S(2)}, u32[]{:S(2)}) collective-permute-start(s16[8,32,256]{2,1,0:T(8,128)(2,1)S(1)} %bitcast.43), channel_id=1, source_target_pairs={{0,96},{32,0},{64,32},{96,64},{128,224},{160,128},{192,160},{224,1... | collective-permute-start | bytes 393224 | tf_op jit(solution)/shard_map/ppermute | solution.py:371
  111.4 6.8 %collective-permute-start.16 = (s16[8,32,256]{2,1,0:T(8,128)(2,1)S(1)}, s16[8,32,256]{2,1,0:T(8,128)(2,1)S(1)}, u32[]{:S(2)}, u32[]{:S(2)}) collective-permute-start(s16[8,32,256]{2,1,0:T(8,128)(2,1)S(1)} %bitcast.44), channel_id=1, source_target_pairs={{0,128},{32,160},{64,192},{96,224},{128,0},{160,32},{192,64},{224,... | collective-permute-start | bytes 393224 | tf_op jit(solution)/shard_map/ppermute | solution.py:371

commit v6 on v5

--- a/solution.py
+++ b/solution.py
@@ -41,7 +41,10 @@
     return lax.axis_index("upper"), lax.axis_index("column"), tile
 
 
-def pick_kernel(est_ref, out_ref, lines_ref, sem):
+def pick_kernel(
+    est_ref, image_ref, out_ref, turned_ref,
+    lines_ref, block_ref, wide_ref, part_ref, sem, in_sem, out_sem,
+):
     upper, column, tile = place()
     tile_y, tile_z = lax.div(tile, 16), lax.rem(lax.div(tile, 2), 8)
     z = lax.rem(tile_z + column + 4 * upper, 8)
@@ -57,6 +60,13 @@
                 )
                 copy.start()
                 copies.append(copy)
+    loads, stores = [], []
+    for j in range(8):
+        load = pltpu.make_async_copy(
+            image_ref.at[:, pl.ds(8 * j, 8)], block_ref.at[j], in_sem.at[j]
+        )
+        load.start()
+        loads.append(load)
     rows_ref = lines_ref.reshape(2, 2, 2, ROWS * 8, 128)
     for k in range(2):
         for u in range(2):
@@ -65,6 +75,22 @@
                 for c in range(2):
                     rows = rows_ref[k, u, h, pl.ds(2 * lax.rem(z, 4) + c, ROWS, stride=8)]
                     out_ref[c, k, u, :, pl.ds(128 * h, 128)] = rows.astype(jnp.bfloat16)
+    flat_ref = wide_ref.reshape(8, 2, ROWS * 8, 128)
+    for j in range(8):
+        loads[j].wait()
+        for h in range(2):
+            lanes = pl.ds(128 * h, 128)
+            wide_ref[j, h] = block_ref[j, :, :, lanes].astype(jnp.float32)
+            for y in range(8):
+                rows = flat_ref[j, h, pl.ds(y, ROWS, stride=8)]
+                part_ref[j, y, :, lanes] = rows.astype(jnp.bfloat16)
+        store = pltpu.make_async_copy(
+            part_ref.at[j], turned_ref.at[pl.ds(8 * j, 8)], out_sem.at[j]
+        )
+        store.start()
+        stores.append(store)
+    for store in stores:
+        store.wait()
 
 
 def forward_kernel(
@@ -302,21 +328,28 @@
     other = lax.ppermute(info, "upper", swap)
 
     tile = lax.axis_index("tile")
-    chip = pl.pallas_call(
+    chip, image = pl.pallas_call(
         pick_kernel,
-        out_shape=jax.ShapeDtypeStruct((2, 2, 2, ROWS, LENGTH), jnp.bfloat16),
-        in_specs=[pl.BlockSpec(memory_space=pl.ANY)],
-        out_specs=VMEM,
+        out_shape=(
+            jax.ShapeDtypeStruct((2, 2, 2, ROWS, LENGTH), jnp.bfloat16),
+            jax.ShapeDtypeStruct((64, ROWS, LENGTH), jnp.bfloat16),
+        ),
+        in_specs=[ANY, ANY],
+        out_specs=(VMEM, ANY),
         scratch_shapes=[
             pltpu.VMEM((2, 2, 2, ROWS, 8, 128), jnp.float32),
+            pltpu.VMEM((8, ROWS, 8, LENGTH), jnp.bfloat16),
+            pltpu.VMEM((8, 2, ROWS, 8, 128), jnp.float32),
+            pltpu.VMEM((8, 8, ROWS, LENGTH), jnp.bfloat16),
             pltpu.SemaphoreType.DMA((2, 2, 2)),
+            pltpu.SemaphoreType.DMA((8,)),
+            pltpu.SemaphoreType.DMA((8,)),
         ],
-        cost_estimate=pl.CostEstimate(flops=0, bytes_accessed=2 << 20, transcendentals=0),
+        cost_estimate=pl.CostEstimate(flops=0, bytes_accessed=4 << 20, transcendentals=0),
         compiler_params=pltpu.CompilerParams(vmem_limit_bytes=125 << 19),
         name="pick_kernel",
-    )(estimate)
+    )(estimate, measured[0])
     block = lax.ppermute(chip, ("upper", "column", "tile"), distance_route())
-    image = measured[0].transpose(1, 0, 2)
     image_lines = lax.all_to_all(image, ("upper", "tile"), 0, 0, tiled=True)
 
     pair = swap_halves(block, "tile", [(i, i ^ 1) for i in range(32)], tile % 2)
@@ -364,11 +397,12 @@
     logs = ((total + 2) >> 2).astype(jnp.int16)
     logs = lax.all_to_all(logs, "tile", 0, 0, tiled=True)
     logs = logs.transpose(1, 0, 2)
-    places = [(0, 0), (1, 2), (0, 2), (1, 1), (1, 3), (0, 1), (0, 3), (1, 0)]
-    pieces = [logs]
-    for u, d in places[1:]:
-        route = [(i, 4 * ((i // 4 + u) % 2) + (i + d) % 4) for i in range(8)]
-        pieces.append(lax.ppermute(logs, ("upper", "column"), route))
+    partner = lax.ppermute(logs, "upper", swap)
+    places, pieces = [(0, 0), (1, 0)], [logs, partner]
+    for u, d in [(0, 2), (0, 1), (0, 3), (1, 2), (1, 1), (1, 3)]:
+        route = [(i, (i + d) % 4) for i in range(4)]
+        places.append((u, d))
+        pieces.append(lax.ppermute(pieces[u], "column", route))
     return finish(places, estimate, pieces, 4, 2)
 
 

time: 119 us -> 122 us (1.025)
  starting transfers between devices: 69.5 us -> 67.8 us
  blocking collectives: 16 us -> 17.6 us
  Pallas kernels: 11.3 us -> 12.9 us
    ppermute x1, starting transfers between devices: 1.42 us -> 36.4 us  [update(): lax.ppermute(other_line[1], ('upper', 'tile'), [(i, i ^ 48) for i in rang...]
    ppermute x1, starting transfers between devices: 32.2 us -> 0.22 us  [update(): beside = lax.ppermute(other_line[0], 'upper', swap)]
    ppermute x7, starting transfers between devices: 10.5 us -> 7.27 us  [the longest x6 6.67 us: update(): pieces.append(lax.ppermute(pieces[u], 'column', route))]
    all_to_all x1, blocking collectives: 16 us -> 17.6 us  [update(): logs = lax.all_to_all(logs, 'tile', 0, 0, tiled=True)]
    pallas_call x1, Pallas kernels: 2.06 us -> 3.67 us  [update(): pl.pallas_call(pick_kernel, out_shape=(jax.ShapeDtypeStruct((2, 2, 2, ROW...]
    ppermute x3, starting transfers between devices: 5.92 us -> 4.33 us  [update(): est_lines.append(lax.ppermute(piece, 'column', route))]
    unnamed x5 -> x10, local copies, waits for them, and re-layouts: 2.79 us -> 3.07 us
  transfers between devices with their start and end apart: 20 -> 20, of which waited for: 11 -> 10; matrix products, arithmetic and copies ran while one was open for 0% -> 0% of each run, Pallas kernels for 6% -> 4%
where the time goes in v6:
time: 122 us; the launch traced here: 121 us
  starting transfers between devices  67.8 us (56%)
  waiting for transfers between devices  17.8 us (15%)
  blocking collectives  17.6 us (14%)
  Pallas kernels  12.9 us (11%)
  local copies, waits for them, and re-layouts  3.15 us (3%)
  between operations  1.69 us (1%)
    ppermute x1, starting transfers between devices, update(): lax.ppermute(other_line[1], ('upper', 'tile'), [(i, i ^ 48) for i in rang...  36.4 us
    all_to_all x1, blocking collectives, update(): logs = lax.all_to_all(logs, 'tile', 0, 0, tiled=True)  17.6 us
    all_to_all x1, starting transfers between devices, update(): image_lines = lax.all_to_all(image, ('upper', 'tile'), 0, 0, tiled=True)  13.3 us
    ppermute x6, starting transfers between devices, update(): pieces.append(lax.ppermute(pieces[u], 'column', route))  6.67 us
    ppermute x3, waiting for transfers between devices, update(): arrived = lax.ppermute(codes[d], 'column', route)  5.65 us
    ppermute x3, starting transfers between devices, update(): est_lines.append(lax.ppermute(piece, 'column', route))  4.33 us
    ppermute x6, waiting for transfers between devices, update(): pieces.append(lax.ppermute(pieces[u], 'column', route))  3.9 us
    pallas_call x1, Pallas kernels, update(): pl.pallas_call(pick_kernel, out_shape=(jax.ShapeDtypeStruct((2, 2, 2, ROW...  3.67 us
  transfers between devices with their start and end apart: 20, of which 10 were waited for; matrix products, arithmetic and copies ran while one was open for 0% of the time, Pallas kernels for 4%

profile of v6, /device:TPU:1, one launch (start us, length us, event | category | flops | bytes accessed | tf_op | source)
XLA Modules:
  0.0 121.3 jit_solution(189003307733240986)
XLA Ops:
  0.0 3.7 %pick_kernel.1 = (bf16[2,2,2,32,256]{4,3,2,1,0:T(8,128)(2,1)}, bf16[64,32,256]{2,1,0:T(8,128)(2,1)}) custom-call(f32[32,64,256]{2,1,0:T(8,128)} %est_ref.3, bf16[32,64,256]{2,1,0:T(8,128)(2,1)} %bitcast.43), custom_call_target="tpu_custom_call" | custom-call | bytes 4194304 | tf_op jit(solution)/shard_map/pick_kernel/pallas_call | solution.py:331
  3.7 0.0 copy-start.4
  3.7 0.0 copy-start.3
  3.7 13.3 %all-to-all-start = ((bf16[64,32,256]{2,1,0:T(8,128)(2,1)}), bf16[64,32,256]{2,1,0:T(8,128)(2,1)S(1)}, u32[]{:S(2)}, u32[]{:S(2)}) async-start(bf16[64,32,256]{2,1,0:T(8,128)(2,1)} %get-tuple-element.9), calls=%async_computation | async-start | bytes 2097152 | tf_op jit(solution)/shard_map/all_to_all | solution.py:353
  17.0 0.7 collective-permute-start.1
  17.7 0.0 collective-permute-done.1
  17.7 0.5 collective-permute-start.2
  19.6 36.4 %collective-permute-start.5 = (bf16[2,32,256]{2,1,0:T(8,128)(2,1)S(1)}, bf16[2,32,256]{2,1,0:T(8,128)(2,1)S(1)}, u32[]{:S(2)}, u32[]{:S(2)}) collective-permute-start(bf16[2,32,256]{2,1,0:T(8,128)(2,1)S(1)} %get-tuple-element.23), channel_id=1, source_target_pairs={{0,144},{1,145},{2,146},{3,147},{4,148},{5,149},{6,150},{7,151},{8... | collective-permute-start | bytes 98312 | tf_op jit(solution)/shard_map/ppermute | solution.py:359
  56.0 0.5 collective-permute-start.3
  56.5 0.2 collective-permute-start.4
  56.7 0.1 add_convert_fusion
  56.8 1.0 collective-permute-done.5
  57.8 2.5 %collective-permute-done.3 = bf16[2,32,256]{2,1,0:T(8,128)(2,1)S(1)} collective-permute-done((bf16[2,32,256]{2,1,0:T(8,128)(2,1)S(1)}, bf16[2,32,256]{2,1,0:T(8,128)(2,1)S(1)}, u32[]{:S(2)}, u32[]{:S(2)}) %collective-permute-start.3) | collective-permute-done | bytes 32800 | tf_op jit(solution)/shard_map/ppermute | solution.py:360
  60.3 0.0 collective-permute-done.4
  60.3 0.1 collective-permute-start.6
  60.4 4.2 %collective-permute-start.7 = (bf16[2,2,2,32,256]{4,3,2,1,0:T(8,128)(2,1)S(1)}, bf16[2,2,2,32,256]{4,3,2,1,0:T(8,128)(2,1)S(1)}, u32[]{:S(2)}, u32[]{:S(2)}) collective-permute-start(bf16[2,2,2,32,256]{4,3,2,1,0:T(8,128)(2,1)S(1)} %bitcast.40), channel_id=1, source_target_pairs={{0,64},{32,96},{64,0},{96,32},{1,65},{33,97},{65,1},{97,33},{2,66}... | collective-permute-start | bytes 393224 | tf_op jit(solution)/shard_map/ppermute | solution.py:366
  64.7 0.0 collective-permute-start.8
  64.7 1.2 collective-permute-start
  65.9 1.6 %collective-permute-done.other_ref.other_profile_ref = f32[1,384]{1,0:T(1,128)S(1)} collective-permute-done((f32[1,384]{1,0:T(1,128)S(1)}, f32[1,384]{1,0:T(1,128)S(1)}, u32[]{:S(2)}, u32[]{:S(2)}) %collective-permute-start) | collective-permute-done | bytes 1568 | tf_op jit(solution)/shard_map/ppermute | solution.py:328
  67.5 1.8 %collective-permute-done.7.est2_ref = bf16[2,2,2,32,256]{4,3,2,1,0:T(8,128)(2,1)S(1)} collective-permute-done((bf16[2,2,2,32,256]{4,3,2,1,0:T(8,128)(2,1)S(1)}, bf16[2,2,2,32,256]{4,3,2,1,0:T(8,128)(2,1)S(1)}, u32[]{:S(2)}, u32[]{:S(2)}) %collective-permute-start.7) | collective-permute-done | bytes 131104 | tf_op jit(solution)/shard_map/ppermute | solution.py:366
  69.3 0.9 collective-permute-done.8.est3_ref
  70.2 3.0 %forward_kernel.1.inverse_ref = f32[2,1024,256]{2,1,0:T(8,128)S(1)} custom-call(s32[1]{0:T(128)S(6)} %copy.18.shift_ref, s32[1]{0:T(128)S(6)} %copy.17.offset_ref, f32[1,384]{1,0:T(1,128)S(1)} %collective-permute-done.other_ref.other_profile_ref, f32[1,256]{1,0:T(1,128)S(1)} %copy-done.3, f32[1,384]{1,0:T(1,128)S(1)} %collective-permute-done.other_ref.other_profile_ref, ...), custom_call_target="tpu_custom_call" | custom-call | flops 268435456 | bytes 8388608 | tf_op jit(solution)/shard_map/forward_kernel/pallas_call | solution.py:368
  73.2 0.0 copy-start.1
  73.2 1.3 %copy-done.1 = f32[2,1024,256]{2,1,0:T(8,128)} copy-done((f32[2,1024,256]{2,1,0:T(8,128)}, f32[2,1024,256]{2,1,0:T(8,128)S(1)}, u32[]{:S(2)}) %copy-start.1) | copy-done | bytes 2097176
  74.5 1.7 %copy-done.2 = f32[2,1024,256]{2,1,0:T(8,128)S(1)} copy-done((f32[2,1024,256]{2,1,0:T(8,128)S(1)}, f32[2,1024,256]{2,1,0:T(8,128)}, u32[]{:S(2)}) %copy-start.2) | copy-done | bytes 2097176
  76.2 3.3 %back_kernel.1 = s16[4,32,8,256]{3,2,1,0:T(8,128)(2,1)S(1)} custom-call(s32[1]{0:T(128)S(6)} %copy.18.shift_ref, s32[1]{0:T(128)S(6)} %copy.17.offset_ref, f32[1,384]{1,0:T(1,128)S(1)} %collective-permute-done.other_ref.other_profile_ref, f32[1,256]{1,0:T(1,128)S(1)} %copy-done.3, f32[1,384]{1,0:T(1,128)S(1)} %collective-permute-done.other_ref.other_profile_ref, ...), custom_call_target="tpu_custom_call" | custom-call | tf_op jit(solution)/shard_map/back_kernel/pallas_call | solution.py:380
  79.5 0.1 collective-permute-start.10
  79.6 2.7 %collective-permute-start.11 = (s16[32,8,256]{2,1,0:T(8,128)(2,1)S(1)}, s16[32,8,256]{2,1,0:T(8,128)(2,1)S(1)}, u32[]{:S(2)}, u32[]{:S(2)}) collective-permute-start(s16[32,8,256]{2,1,0:T(8,128)(2,1)S(1)} %get-tuple-element.14), channel_id=1, source_target_pairs={{0,96},{32,0},{64,32},{96,64},{1,97},{33,1},{65,33},{97,65},{2,98}... | collective-permute-start | bytes 393224 | tf_op jit(solution)/shard_map/ppermute | solution.py:395
  82.3 0.7 collective-permute-start.9
  83.0 1.7 %collective-permute-done.10 = s16[32,8,256]{2,1,0:T(8,128)(2,1)S(1)} collective-permute-done((s16[32,8,256]{2,1,0:T(8,128)(2,1)S(1)}, s16[32,8,256]{2,1,0:T(8,128)(2,1)S(1)}, u32[]{:S(2)}, u32[]{:S(2)}) %collective-permute-start.10) | collective-permute-done | bytes 131104 | tf_op jit(solution)/shard_map/ppermute | solution.py:395
  84.6 0.0 collective-permute-done.11
  84.6 4.0 %collective-permute-done.9 = s16[32,8,256]{2,1,0:T(8,128)(2,1)S(1)} collective-permute-done((s16[32,8,256]{2,1,0:T(8,128)(2,1)S(1)}, s16[32,8,256]{2,1,0:T(8,128)(2,1)S(1)}, u32[]{:S(2)}, u32[]{:S(2)}) %collective-permute-start.9) | collective-permute-done | bytes 131104 | tf_op jit(solution)/shard_map/ppermute | solution.py:395
  88.6 0.2 fusion.4
  88.8 17.6 %all_to_all.10 = s16[32,8,256]{2,1,0:T(8,128)(2,1)S(1)} all-to-all(s16[32,8,256]{2,1,0:T(8,128)(2,1)S(1)} %fusion.4), channel_id=1, replica_groups=mesh['upper'=2,'column'=4,'tile'=32] {'tile'}, dimensions={0} | all-to-all | bytes 262144 | tf_op jit(solution)/shard_map/all_to_all | solution.py:398
  106.5 0.6 collective-permute-start.12
  107.1 0.2 collective-permute-start.13
  107.2 2.1 %collective-permute-start.14 = (s16[8,32,256]{2,1,0:T(8,128)(2,1)S(1)}, s16[8,32,256]{2,1,0:T(8,128)(2,1)S(1)}, u32[]{:S(2)}, u32[]{:S(2)}) collective-permute-start(s16[8,32,256]{2,1,0:T(8,128)(2,1)S(1)} %bitcast.36), channel_id=1, source_target_pairs={{0,32},{32,64},{64,96},{96,0},{1,33},{33,65},{65,97},{97,1},{2,34}... | collective-permute-start | bytes 393224 | tf_op jit(solution)/shard_map/ppermute | solution.py:405
  109.3 0.6 collective-permute-start.17
  109.9 0.4 collective-permute-done.12.refs_1_
  110.4 1.1 collective-permute-start.18
  111.5 1.3 %collective-permute-start.15 = (s16[8,32,256]{2,1,0:T(8,128)(2,1)S(1)}, s16[8,32,256]{2,1,0:T(8,128)(2,1)S(1)}, u32[]{:S(2)}, u32[]{:S(2)}) collective-permute-start(s16[8,32,256]{2,1,0:T(8,128)(2,1)S(1)} %collective-permute-done.12.refs_1_), channel_id=1, source_target_pairs={{0,32},{32,64},{64,96},{96,0},{1,33},{33,65},{65,97},{97,1},{2,34}... | collective-permute-start | bytes 393224 | tf_op jit(solution)/shard_map/ppermute | solution.py:405
  112.8 1.4 %collective-permute-start.16 = (s16[8,32,256]{2,1,0:T(8,128)(2,1)S(1)}, s16[8,32,256]{2,1,0:T(8,128)(2,1)S(1)}, u32[]{:S(2)}, u32[]{:S(2)}) collective-permute-start(s16[8,32,256]{2,1,0:T(8,128)(2,1)S(1)} %collective-permute-done.12.refs_1_), channel_id=1, source_target_pairs={{0,96},{32,0},{64,32},{96,64},{1,97},{33,1},{65,33},{97,65},{2,98}... | collective-permute-start | bytes 393224 | tf_op jit(solution)/shard_map/ppermute | solution.py:405
  114.2 2.4 %collective-permute-done.14.refs_3_ = s16[8,32,256]{2,1,0:T(8,128)(2,1)S(1)} collective-permute-done((s16[8,32,256]{2,1,0:T(8,128)(2,1)S(1)}, s16[8,32,256]{2,1,0:T(8,128)(2,1)S(1)}, u32[]{:S(2)}, u32[]{:S(2)}) %collective-permute-start.14) | collective-permute-done | bytes 131104 | tf_op jit(solution)/shard_map/ppermute | solution.py:405
  116.6 1.3 %first_kernel.1 = (f32[32,64,256]{2,1,0:T(8,128)}, f32[4,8,32,256]{3,2,1,0:T(8,128)S(1)}) custom-call(f32[32,64,256]{2,1,0:T(8,128)S(1)} %copy-done, s16[8,32,256]{2,1,0:T(8,128)(2,1)S(1)} %bitcast.38, s16[8,32,256]{2,1,0:T(8,128)(2,1)S(1)} %collective-permute-done.12.refs_1_, s16[8,32,256]{2,1,0:T(8,128)(2,1)S(1)} %collective-permute-done.13.refs_2_, ...), custom_call_target="tpu_custom_call" | custom-call | flops 524288 | bytes 2097152 | tf_op jit(solution)/shard_map/first_kernel/pallas_call | solution.py:268
  117.9 0.0 collective-permute-done.17.refs_0_
  117.9 0.9 later_kernel.2.refs_2_
  118.8 1.4 %collective-permute-done.15.refs_0_ = s16[8,32,256]{2,1,0:T(8,128)(2,1)S(1)} collective-permute-done((s16[8,32,256]{2,1,0:T(8,128)(2,1)S(1)}, s16[8,32,256]{2,1,0:T(8,128)(2,1)S(1)}, u32[]{:S(2)}, u32[]{:S(2)}) %collective-permute-start.15) | collective-permute-done | bytes 131104 | tf_op jit(solution)/shard_map/ppermute | solution.py:405
  120.3 0.9 later_kernel.3
  (20 shorter events, 0.2 us)
Async XLA Ops:
  3.7 13.3 %copy-start.4 = (bf16[2,2,2,32,256]{4,3,2,1,0:T(8,128)(2,1)S(1)}, bf16[2,2,2,32,256]{4,3,2,1,0:T(8,128)(2,1)}, u32[]{:S(2)}) copy-start(bf16[2,2,2,32,256]{4,3,2,1,0:T(8,128)(2,1)} %get-tuple-element.10) | copy-start | bytes 393220
  3.7 61.0 %copy-start.3 = (f32[1,256]{1,0:T(1,128)S(1)}, f32[1,256]{1,0:T(1,128)}, u32[]{:S(2)}) copy-start(f32[1,256]{1,0:T(1,128)} %own_profile_ref.3) | copy-start | bytes 3076
  3.7 70.8 %all-to-all-start = ((bf16[64,32,256]{2,1,0:T(8,128)(2,1)}), bf16[64,32,256]{2,1,0:T(8,128)(2,1)S(1)}, u32[]{:S(2)}, u32[]{:S(2)}) async-start(bf16[64,32,256]{2,1,0:T(8,128)(2,1)} %get-tuple-element.9), calls=%async_computation | async-start | bytes 2097152 | tf_op jit(solution)/shard_map/all_to_all | solution.py:353
  17.0 0.7 collective-permute-start.1
  17.7 1.8 %collective-permute-start.2 = (bf16[2,2,32,256]{3,2,1,0:T(8,128)(2,1)S(1)}, bf16[2,2,32,256]{3,2,1,0:T(8,128)(2,1)S(1)}, u32[]{:S(2)}, u32[]{:S(2)}) collective-permute-start(bf16[2,2,32,256]{3,2,1,0:T(8,128)(2,1)S(1)} %get-tuple-element.18), channel_id=1, source_target_pairs={{0,1},{1,0},{2,3},{3,2},{4,5},{5,4},{6,7},{7,6},{8,9},{9,8},{10,11... | collective-permute-start | bytes 196616 | tf_op jit(solution)/shard_map/ppermute | solution.py:315
  19.6 38.1 %collective-permute-start.5 = (bf16[2,32,256]{2,1,0:T(8,128)(2,1)S(1)}, bf16[2,32,256]{2,1,0:T(8,128)(2,1)S(1)}, u32[]{:S(2)}, u32[]{:S(2)}) collective-permute-start(bf16[2,32,256]{2,1,0:T(8,128)(2,1)S(1)} %get-tuple-element.23), channel_id=1, source_target_pairs={{0,144},{1,145},{2,146},{3,147},{4,148},{5,149},{6,150},{7,151},{8... | collective-permute-start | bytes 98312 | tf_op jit(solution)/shard_map/ppermute | solution.py:359
  56.0 4.3 %collective-permute-start.3 = (bf16[2,32,256]{2,1,0:T(8,128)(2,1)S(1)}, bf16[2,32,256]{2,1,0:T(8,128)(2,1)S(1)}, u32[]{:S(2)}, u32[]{:S(2)}) collective-permute-start(bf16[2,32,256]{2,1,0:T(8,128)(2,1)S(1)} %get-tuple-element.21), channel_id=1, source_target_pairs={{0,16},{1,17},{2,18},{3,19},{4,20},{5,21},{6,22},{7,23},{8,24},{9,... | collective-permute-start | bytes 98312 | tf_op jit(solution)/shard_map/ppermute | solution.py:360
  56.5 3.8 %collective-permute-start.4 = (bf16[2,32,256]{2,1,0:T(8,128)(2,1)S(1)}, bf16[2,32,256]{2,1,0:T(8,128)(2,1)S(1)}, u32[]{:S(2)}, u32[]{:S(2)}) collective-permute-start(bf16[2,32,256]{2,1,0:T(8,128)(2,1)S(1)} %get-tuple-element.22), channel_id=1, source_target_pairs={{0,128},{128,0},{1,129},{129,1},{2,130},{130,2},{3,131},{131,3},{4... | collective-permute-start | bytes 98312 | tf_op jit(solution)/shard_map/ppermute | solution.py:361
  60.3 7.2 %collective-permute-start.6 = (bf16[2,2,2,32,256]{4,3,2,1,0:T(8,128)(2,1)S(1)}, bf16[2,2,2,32,256]{4,3,2,1,0:T(8,128)(2,1)S(1)}, u32[]{:S(2)}, u32[]{:S(2)}) collective-permute-start(bf16[2,2,2,32,256]{4,3,2,1,0:T(8,128)(2,1)S(1)} %bitcast.39), channel_id=1, source_target_pairs={{0,32},{32,64},{64,96},{96,0},{1,33},{33,65},{65,97},{97,1},{2,34}... | collective-permute-start | bytes 393224 | tf_op jit(solution)/shard_map/ppermute | solution.py:366
  60.4 8.9 %collective-permute-start.7 = (bf16[2,2,2,32,256]{4,3,2,1,0:T(8,128)(2,1)S(1)}, bf16[2,2,2,32,256]{4,3,2,1,0:T(8,128)(2,1)S(1)}, u32[]{:S(2)}, u32[]{:S(2)}) collective-permute-start(bf16[2,2,2,32,256]{4,3,2,1,0:T(8,128)(2,1)S(1)} %bitcast.40), channel_id=1, source_target_pairs={{0,64},{32,96},{64,0},{96,32},{1,65},{33,97},{65,1},{97,33},{2,66}... | collective-permute-start | bytes 393224 | tf_op jit(solution)/shard_map/ppermute | solution.py:366
  64.7 5.5 %collective-permute-start.8 = (bf16[2,2,2,32,256]{4,3,2,1,0:T(8,128)(2,1)S(1)}, bf16[2,2,2,32,256]{4,3,2,1,0:T(8,128)(2,1)S(1)}, u32[]{:S(2)}, u32[]{:S(2)}) collective-permute-start(bf16[2,2,2,32,256]{4,3,2,1,0:T(8,128)(2,1)S(1)} %bitcast.41), channel_id=1, source_target_pairs={{0,96},{32,0},{64,32},{96,64},{1,97},{33,1},{65,33},{97,65},{2,98}... | collective-permute-start | bytes 393224 | tf_op jit(solution)/shard_map/ppermute | solution.py:366
  64.7 2.8 %collective-permute-start = (f32[1,384]{1,0:T(1,128)S(1)}, f32[1,384]{1,0:T(1,128)S(1)}, u32[]{:S(2)}, u32[]{:S(2)}) collective-permute-start(f32[1,384]{1,0:T(1,128)S(1)} %pad_maximum_fusion.1), channel_id=1, source_target_pairs={{0,128},{128,0},{1,129},{129,1},{2,130},{130,2},{3,131},{131,3},{4... | collective-permute-start | bytes 4616 | tf_op jit(solution)/shard_map/ppermute | solution.py:328
  73.2 1.3 %copy-start.1 = (f32[2,1024,256]{2,1,0:T(8,128)}, f32[2,1024,256]{2,1,0:T(8,128)S(1)}, u32[]{:S(2)}) copy-start(f32[2,1024,256]{2,1,0:T(8,128)S(1)} %forward_kernel.1.inverse_ref) | copy-start | bytes 6291460
  74.5 42.1 %copy-start = (f32[32,64,256]{2,1,0:T(8,128)S(1)}, f32[32,64,256]{2,1,0:T(8,128)}, u32[]{:S(2)}) copy-start(f32[32,64,256]{2,1,0:T(8,128)} %est_ref.3) | copy-start | bytes 6291460
  74.5 1.7 %copy-start.2 = (f32[2,1024,256]{2,1,0:T(8,128)S(1)}, f32[2,1024,256]{2,1,0:T(8,128)}, u32[]{:S(2)}) copy-start(f32[2,1024,256]{2,1,0:T(8,128)} %copy-done.1) | copy-start | bytes 6291460
  79.5 5.1 %collective-permute-start.10 = (s16[32,8,256]{2,1,0:T(8,128)(2,1)S(1)}, s16[32,8,256]{2,1,0:T(8,128)(2,1)S(1)}, u32[]{:S(2)}, u32[]{:S(2)}) collective-permute-start(s16[32,8,256]{2,1,0:T(8,128)(2,1)S(1)} %get-tuple-element.15), channel_id=1, source_target_pairs={{0,32},{32,64},{64,96},{96,0},{1,33},{33,65},{65,97},{97,1},{2,34}... | collective-permute-start | bytes 393224 | tf_op jit(solution)/shard_map/ppermute | solution.py:395
  79.6 5.0 %collective-permute-start.11 = (s16[32,8,256]{2,1,0:T(8,128)(2,1)S(1)}, s16[32,8,256]{2,1,0:T(8,128)(2,1)S(1)}, u32[]{:S(2)}, u32[]{:S(2)}) collective-permute-start(s16[32,8,256]{2,1,0:T(8,128)(2,1)S(1)} %get-tuple-element.14), channel_id=1, source_target_pairs={{0,96},{32,0},{64,32},{96,64},{1,97},{33,1},{65,33},{97,65},{2,98}... | collective-permute-start | bytes 393224 | tf_op jit(solution)/shard_map/ppermute | solution.py:395
  82.3 6.3 %collective-permute-start.9 = (s16[32,8,256]{2,1,0:T(8,128)(2,1)S(1)}, s16[32,8,256]{2,1,0:T(8,128)(2,1)S(1)}, u32[]{:S(2)}, u32[]{:S(2)}) collective-permute-start(s16[32,8,256]{2,1,0:T(8,128)(2,1)S(1)} %get-tuple-element.13), channel_id=1, source_target_pairs={{0,64},{32,96},{64,0},{96,32},{1,65},{33,97},{65,1},{97,33},{2,66}... | collective-permute-start | bytes 393224 | tf_op jit(solution)/shard_map/ppermute | solution.py:395
  106.5 3.9 %collective-permute-start.12 = (s16[8,32,256]{2,1,0:T(8,128)(2,1)S(1)}, s16[8,32,256]{2,1,0:T(8,128)(2,1)S(1)}, u32[]{:S(2)}, u32[]{:S(2)}) collective-permute-start(s16[8,32,256]{2,1,0:T(8,128)(2,1)S(1)} %bitcast.34), channel_id=1, source_target_pairs={{0,128},{128,0},{1,129},{129,1},{2,130},{130,2},{3,131},{131,3},{4... | collective-permute-start | bytes 393224 | tf_op jit(solution)/shard_map/ppermute | solution.py:400
  107.1 5.8 %collective-permute-start.13 = (s16[8,32,256]{2,1,0:T(8,128)(2,1)S(1)}, s16[8,32,256]{2,1,0:T(8,128)(2,1)S(1)}, u32[]{:S(2)}, u32[]{:S(2)}) collective-permute-start(s16[8,32,256]{2,1,0:T(8,128)(2,1)S(1)} %bitcast.35), channel_id=1, source_target_pairs={{0,64},{32,96},{64,0},{96,32},{1,65},{33,97},{65,1},{97,33},{2,66}... | collective-permute-start | bytes 393224 | tf_op jit(solution)/shard_map/ppermute | solution.py:405
  107.2 9.4 %collective-permute-start.14 = (s16[8,32,256]{2,1,0:T(8,128)(2,1)S(1)}, s16[8,32,256]{2,1,0:T(8,128)(2,1)S(1)}, u32[]{:S(2)}, u32[]{:S(2)}) collective-permute-start(s16[8,32,256]{2,1,0:T(8,128)(2,1)S(1)} %bitcast.36), channel_id=1, source_target_pairs={{0,32},{32,64},{64,96},{96,0},{1,33},{33,65},{65,97},{97,1},{2,34}... | collective-permute-start | bytes 393224 | tf_op jit(solution)/shard_map/ppermute | solution.py:405
  109.3 8.6 %collective-permute-start.17 = (s16[8,32,256]{2,1,0:T(8,128)(2,1)S(1)}, s16[8,32,256]{2,1,0:T(8,128)(2,1)S(1)}, u32[]{:S(2)}, u32[]{:S(2)}) collective-permute-start(s16[8,32,256]{2,1,0:T(8,128)(2,1)S(1)} %bitcast.37), channel_id=1, source_target_pairs={{0,96},{32,0},{64,32},{96,64},{1,97},{33,1},{65,33},{97,65},{2,98}... | collective-permute-start | bytes 393224 | tf_op jit(solution)/shard_map/ppermute | solution.py:405
  110.4 7.6 %collective-permute-start.18 = (s16[8,32,256]{2,1,0:T(8,128)(2,1)S(1)}, s16[8,32,256]{2,1,0:T(8,128)(2,1)S(1)}, u32[]{:S(2)}, u32[]{:S(2)}) collective-permute-start(s16[8,32,256]{2,1,0:T(8,128)(2,1)S(1)} %collective-permute-done.12.refs_1_), channel_id=1, source_target_pairs={{0,64},{32,96},{64,0},{96,32},{1,65},{33,97},{65,1},{97,33},{2,66}... | collective-permute-start | bytes 393224 | tf_op jit(solution)/shard_map/ppermute | solution.py:405
  111.5 8.8 %collective-permute-start.15 = (s16[8,32,256]{2,1,0:T(8,128)(2,1)S(1)}, s16[8,32,256]{2,1,0:T(8,128)(2,1)S(1)}, u32[]{:S(2)}, u32[]{:S(2)}) collective-permute-start(s16[8,32,256]{2,1,0:T(8,128)(2,1)S(1)} %collective-permute-done.12.refs_1_), channel_id=1, source_target_pairs={{0,32},{32,64},{64,96},{96,0},{1,33},{33,65},{65,97},{97,1},{2,34}... | collective-permute-start | bytes 393224 | tf_op jit(solution)/shard_map/ppermute | solution.py:405
  112.8 7.5 %collective-permute-start.16 = (s16[8,32,256]{2,1,0:T(8,128)(2,1)S(1)}, s16[8,32,256]{2,1,0:T(8,128)(2,1)S(1)}, u32[]{:S(2)}, u32[]{:S(2)}) collective-permute-start(s16[8,32,256]{2,1,0:T(8,128)(2,1)S(1)} %collective-permute-done.12.refs_1_), channel_id=1, source_target_pairs={{0,96},{32,0},{64,32},{96,64},{1,97},{33,1},{65,33},{97,65},{2,98}... | collective-permute-start | bytes 393224 | tf_op jit(solution)/shard_map/ppermute | solution.py:405

commit v7 on v5

--- a/solution.py
+++ b/solution.py
@@ -364,12 +364,19 @@
     logs = ((total + 2) >> 2).astype(jnp.int16)
     logs = lax.all_to_all(logs, "tile", 0, 0, tiled=True)
     logs = logs.transpose(1, 0, 2)
-    places = [(0, 0), (1, 2), (0, 2), (1, 1), (1, 3), (0, 1), (0, 3), (1, 0)]
-    pieces = [logs]
-    for u, d in places[1:]:
-        route = [(i, 4 * ((i // 4 + u) % 2) + (i + d) % 4) for i in range(8)]
-        pieces.append(lax.ppermute(logs, ("upper", "column"), route))
-    return finish(places, estimate, pieces, 4, 2)
+    partner = lax.ppermute(logs, "upper", swap)
+
+    def give(piece, d):
+        return lax.ppermute(piece, "column", [(i, (i + d) % 4) for i in range(4)])
+
+    pieces = {(0, 0): logs, (1, 0): partner}
+    pieces[0, 1] = give(logs, 1)
+    pieces[0, 3] = give(logs, 3)
+    both = give(jnp.stack([logs, partner]), 2)
+    pieces[1, 1] = give(partner, 1)
+    pieces[1, 3] = give(partner, 3)
+    pieces[0, 2], pieces[1, 2] = both[0], both[1]
+    return finish(list(pieces), estimate, list(pieces.values()), 4, 2)
 
 
 def solution(mesh):

time: 119 us -> 124 us (1.042)
  waiting for transfers between devices: 17.6 us -> 31.6 us
  starting transfers between devices: 69.5 us -> 60.4 us
    ppermute x7 -> x6, waiting for transfers between devices: 3.39 us -> 13.1 us  [the longest x5 9.33 us: give(): return lax.ppermute(piece, 'column', [(i, (i + d) % 4) for i in range(4)])]
    ppermute x7 -> x6, starting transfers between devices: 10.5 us -> 3.88 us  [the longest x5 3.78 us: give(): return lax.ppermute(piece, 'column', [(i, (i + d) % 4) for i in range(4)])]
    ppermute x3, waiting for transfers between devices: 2.17 us -> 5.54 us  [update(): est_lines.append(lax.ppermute(piece, 'column', route))]
    ppermute x1, waiting for transfers between devices: 1.72 us -> 0.01 us  [update(): across = lax.ppermute(own_line[1], 'tile', [(i, i ^ 16) for i in range(32)])]
    ppermute x1, starting transfers between devices: 1.17 us -> 2.89 us  [update(): across = lax.ppermute(own_line[1], 'tile', [(i, i ^ 16) for i in range(32)])]
    ppermute x3, starting transfers between devices: 2.99 us -> 1.63 us  [update(): arrived = lax.ppermute(codes[d], 'column', route)]
  transfers between devices with their start and end apart: 20 -> 19, of which waited for: 11 -> 13; matrix products, arithmetic and copies ran while one was open for 0% -> 0% of each run, Pallas kernels for 6% -> 6%
where the time goes in v7:
time: 124 us
  starting transfers between devices  60.4 us (49%)
  waiting for transfers between devices  31.6 us (25%)
  blocking collectives  15.7 us (13%)
  Pallas kernels  11.3 us (9%)
  local copies, waits for them, and re-layouts  2.89 us (2%)
  between operations  1.64 us (1%)
    ppermute x1, starting transfers between devices, update(): beside = lax.ppermute(other_line[0], 'upper', swap)  31.2 us
    all_to_all x1, blocking collectives, update(): logs = lax.all_to_all(logs, 'tile', 0, 0, tiled=True)  15.7 us
    all_to_all x1, starting transfers between devices, update(): image_lines = lax.all_to_all(image, ('upper', 'tile'), 0, 0, tiled=True)  13.1 us
    ppermute x5, waiting for transfers between devices, give(): return lax.ppermute(piece, 'column', [(i, (i + d) % 4) for i in range(4)])  9.33 us
    ppermute x3, waiting for transfers between devices, update(): arrived = lax.ppermute(codes[d], 'column', route)  7.31 us
    ppermute x3, waiting for transfers between devices, update(): est_lines.append(lax.ppermute(piece, 'column', route))  5.54 us
    ppermute x3, starting transfers between devices, update(): est_lines.append(lax.ppermute(piece, 'column', route))  4.75 us
    ppermute x1, waiting for transfers between devices, update(): partner = lax.ppermute(logs, 'upper', swap)  3.8 us
  transfers between devices with their start and end apart: 19, of which 13 were waited for; matrix products, arithmetic and copies ran while one was open for 0% of the time, Pallas kernels for 6%

profile of v7, /device:TPU:1, one launch (start us, length us, event | category | flops | bytes accessed | tf_op | source)
XLA Modules:
  0.0 123.8 jit_solution(4926317753418375226)
XLA Ops:
  0.0 2.8 %copy.18 = bf16[1,32,64,256]{3,1,2,0:T(8,128)(2,1)} copy(bf16[1,32,64,256]{3,2,1,0:T(8,128)(2,1)} %param.6) | data formatting | bytes 2097152 | tf_op args[1]
  2.8 13.1 %all-to-all-start = ((bf16[64,32,256]{2,1,0:T(8,128)(2,1)}), bf16[64,32,256]{2,1,0:T(8,128)(2,1)S(1)}, u32[]{:S(2)}, u32[]{:S(2)}) async-start(bf16[64,32,256]{2,1,0:T(8,128)(2,1)} %bitcast.44), calls=%async_computation | async-start | bytes 2097152 | tf_op jit(solution)/shard_map/all_to_all | solution.py:320
  15.9 0.0 copy-start.1
  15.9 2.1 %pick_kernel.1 = bf16[2,2,2,32,256]{4,3,2,1,0:T(8,128)(2,1)} custom-call(f32[32,64,256]{2,1,0:T(8,128)} %est_ref.3), custom_call_target="tpu_custom_call" | custom-call | bytes 2097152 | tf_op jit(solution)/shard_map/pick_kernel/pallas_call | solution.py:305
  18.0 1.6 %collective-permute-start.1 = (bf16[2,2,2,32,256]{4,3,2,1,0:T(8,128)(2,1)}, bf16[2,2,2,32,256]{4,3,2,1,0:T(8,128)(2,1)S(1)}, u32[]{:S(2)}, u32[]{:S(2)}) collective-permute-start(bf16[2,2,2,32,256]{4,3,2,1,0:T(8,128)(2,1)} %pick_kernel.1), channel_id=1, source_target_pairs={{0,0},{1,1},{2,2},{3,3},{4,4},{5,5},{6,6},{7,7},{8,8},{9,9},{10,10... | collective-permute-start | bytes 393224 | tf_op jit(solution)/shard_map/ppermute | solution.py:318
  19.6 0.0 collective-permute-done.1
  19.6 0.5 collective-permute-start.2
  21.4 0.0 collective-permute-done.2
  21.5 2.9 %collective-permute-start.3 = (bf16[2,32,256]{2,1,0:T(8,128)(2,1)S(1)}, bf16[2,32,256]{2,1,0:T(8,128)(2,1)S(1)}, u32[]{:S(2)}, u32[]{:S(2)}) collective-permute-start(bf16[2,32,256]{2,1,0:T(8,128)(2,1)S(1)} %get-tuple-element.21), channel_id=1, source_target_pairs={{0,16},{1,17},{2,18},{3,19},{4,20},{5,21},{6,22},{7,23},{8,24},{9,... | collective-permute-start | bytes 98312 | tf_op jit(solution)/shard_map/ppermute | solution.py:327
  24.4 31.2 %collective-permute-start.4 = (bf16[2,32,256]{2,1,0:T(8,128)(2,1)S(1)}, bf16[2,32,256]{2,1,0:T(8,128)(2,1)S(1)}, u32[]{:S(2)}, u32[]{:S(2)}) collective-permute-start(bf16[2,32,256]{2,1,0:T(8,128)(2,1)S(1)} %get-tuple-element.22), channel_id=1, source_target_pairs={{0,128},{128,0},{1,129},{129,1},{2,130},{130,2},{3,131},{131,3},{4... | collective-permute-start | bytes 98312 | tf_op jit(solution)/shard_map/ppermute | solution.py:328
  55.5 0.6 collective-permute-start.5
  56.1 0.1 add_convert_fusion
  56.2 0.0 collective-permute-done.3
  56.2 1.2 collective-permute-done.4
  57.4 2.1 %collective-permute-done.5 = bf16[2,32,256]{2,1,0:T(8,128)(2,1)S(1)} collective-permute-done((bf16[2,32,256]{2,1,0:T(8,128)(2,1)S(1)}, bf16[2,32,256]{2,1,0:T(8,128)(2,1)S(1)}, u32[]{:S(2)}, u32[]{:S(2)}) %collective-permute-start.5) | collective-permute-done | bytes 32800 | tf_op jit(solution)/shard_map/ppermute | solution.py:326
  59.5 4.1 %collective-permute-start.8 = (bf16[2,2,2,32,256]{4,3,2,1,0:T(8,128)(2,1)S(1)}, bf16[2,2,2,32,256]{4,3,2,1,0:T(8,128)(2,1)S(1)}, u32[]{:S(2)}, u32[]{:S(2)}) collective-permute-start(bf16[2,2,2,32,256]{4,3,2,1,0:T(8,128)(2,1)S(1)} %bitcast.51), channel_id=1, source_target_pairs={{0,96},{32,0},{64,32},{96,64},{1,97},{33,1},{65,33},{97,65},{2,98}... | collective-permute-start | bytes 393224 | tf_op jit(solution)/shard_map/ppermute | solution.py:333
  63.6 0.7 collective-permute-start.6
  64.3 0.2 collective-permute-start
  64.6 2.3 %collective-permute-done.other_ref.other_profile_ref = f32[1,384]{1,0:T(1,128)S(1)} collective-permute-done((f32[1,384]{1,0:T(1,128)S(1)}, f32[1,384]{1,0:T(1,128)S(1)}, u32[]{:S(2)}, u32[]{:S(2)}) %collective-permute-start) | collective-permute-done | bytes 1568 | tf_op jit(solution)/shard_map/ppermute | solution.py:302
  66.8 1.9 %collective-permute-done.8.est3_ref = bf16[2,2,2,32,256]{4,3,2,1,0:T(8,128)(2,1)S(1)} collective-permute-done((bf16[2,2,2,32,256]{4,3,2,1,0:T(8,128)(2,1)S(1)}, bf16[2,2,2,32,256]{4,3,2,1,0:T(8,128)(2,1)S(1)}, u32[]{:S(2)}, u32[]{:S(2)}) %collective-permute-start.8) | collective-permute-done | bytes 131104 | tf_op jit(solution)/shard_map/ppermute | solution.py:333
  68.7 0.3 collective-permute-done.7.est2_ref
  69.0 3.3 %collective-permute-done.6.est1_ref = bf16[2,2,2,32,256]{4,3,2,1,0:T(8,128)(2,1)S(1)} collective-permute-done((bf16[2,2,2,32,256]{4,3,2,1,0:T(8,128)(2,1)S(1)}, bf16[2,2,2,32,256]{4,3,2,1,0:T(8,128)(2,1)S(1)}, u32[]{:S(2)}, u32[]{:S(2)}) %collective-permute-start.6) | collective-permute-done | bytes 131104 | tf_op jit(solution)/shard_map/ppermute | solution.py:333
  72.4 3.0 %forward_kernel.1.inverse_ref = f32[2,1024,256]{2,1,0:T(8,128)S(1)} custom-call(s32[1]{0:T(128)S(6)} %copy.23.shift_ref, s32[1]{0:T(128)S(6)} %copy.22.offset_ref, f32[1,384]{1,0:T(1,128)S(1)} %collective-permute-done.other_ref.other_profile_ref, f32[1,256]{1,0:T(1,128)S(1)} %copy-done.1, f32[1,384]{1,0:T(1,128)S(1)} %collective-permute-done.other_ref.other_profile_ref, ...), custom_call_target="tpu_custom_call" | custom-call | flops 268435456 | bytes 8388608 | tf_op jit(solution)/shard_map/forward_kernel/pallas_call | solution.py:335
  75.4 3.3 %back_kernel.1 = s16[4,32,8,256]{3,2,1,0:T(8,128)(2,1)S(1)} custom-call(s32[1]{0:T(128)S(6)} %copy.23.shift_ref, s32[1]{0:T(128)S(6)} %copy.22.offset_ref, f32[1,384]{1,0:T(1,128)S(1)} %collective-permute-done.other_ref.other_profile_ref, f32[1,256]{1,0:T(1,128)S(1)} %copy-done.1, f32[1,384]{1,0:T(1,128)S(1)} %collective-permute-done.other_ref.other_profile_ref, ...), custom_call_target="tpu_custom_call" | custom-call | tf_op jit(solution)/shard_map/back_kernel/pallas_call | solution.py:347
  78.6 0.0 copy-start
  78.7 0.1 collective-permute-start.9
  78.8 0.1 collective-permute-start.11
  78.9 1.5 %collective-permute-start.10 = (s16[32,8,256]{2,1,0:T(8,128)(2,1)S(1)}, s16[32,8,256]{2,1,0:T(8,128)(2,1)S(1)}, u32[]{:S(2)}, u32[]{:S(2)}) collective-permute-start(s16[32,8,256]{2,1,0:T(8,128)(2,1)S(1)} %get-tuple-element.11), channel_id=1, source_target_pairs={{0,32},{32,64},{64,96},{96,0},{1,33},{33,65},{65,97},{97,1},{2,34}... | collective-permute-start | bytes 393224 | tf_op jit(solution)/shard_map/ppermute | solution.py:362
  80.3 3.9 %collective-permute-done.9 = s16[32,8,256]{2,1,0:T(8,128)(2,1)S(1)} collective-permute-done((s16[32,8,256]{2,1,0:T(8,128)(2,1)S(1)}, s16[32,8,256]{2,1,0:T(8,128)(2,1)S(1)}, u32[]{:S(2)}, u32[]{:S(2)}) %collective-permute-start.9) | collective-permute-done | bytes 131104 | tf_op jit(solution)/shard_map/ppermute | solution.py:362
  84.2 0.0 collective-permute-done.11
  84.2 3.4 %collective-permute-done.10 = s16[32,8,256]{2,1,0:T(8,128)(2,1)S(1)} collective-permute-done((s16[32,8,256]{2,1,0:T(8,128)(2,1)S(1)}, s16[32,8,256]{2,1,0:T(8,128)(2,1)S(1)}, u32[]{:S(2)}, u32[]{:S(2)}) %collective-permute-start.10) | collective-permute-done | bytes 131104 | tf_op jit(solution)/shard_map/ppermute | solution.py:362
  87.6 0.2 fusion.4
  87.8 15.7 %all_to_all.10 = s16[32,8,256]{2,1,0:T(8,128)(2,1)S(1)} all-to-all(s16[32,8,256]{2,1,0:T(8,128)(2,1)S(1)} %fusion.4), channel_id=1, replica_groups=mesh['upper'=2,'column'=4,'tile'=32] {'tile'}, dimensions={0} | all-to-all | bytes 262144 | tf_op jit(solution)/shard_map/all_to_all | solution.py:365
  103.5 0.1 collective-permute-start.12
  103.6 3.8 %collective-permute-done.12.refs_1_ = s16[8,32,256]{2,1,0:T(8,128)(2,1)S(1)} collective-permute-done((s16[8,32,256]{2,1,0:T(8,128)(2,1)S(1)}, s16[8,32,256]{2,1,0:T(8,128)(2,1)S(1)}, u32[]{:S(2)}, u32[]{:S(2)}) %collective-permute-start.12) | collective-permute-done | bytes 131104 | tf_op jit(solution)/shard_map/ppermute | solution.py:367
  107.4 0.2 collective-permute-start.15
  107.6 1.0 collective-permute-start.14
  108.6 0.7 collective-permute-start.13
  109.3 2.0 %collective-permute-start.17 = (s16[8,32,256]{2,1,0:T(8,128)(2,1)S(1)}, s16[8,32,256]{2,1,0:T(8,128)(2,1)S(1)}, u32[]{:S(2)}, u32[]{:S(2)}) collective-permute-start(s16[8,32,256]{2,1,0:T(8,128)(2,1)S(1)} %collective-permute-done.12.refs_1_), channel_id=1, source_target_pairs={{0,96},{32,0},{64,32},{96,64},{1,97},{33,1},{65,33},{97,65},{2,98}... | collective-permute-start | bytes 393224 | tf_op jit(solution)/shard_map/ppermute | solution.py:370
  111.2 0.0 collective-permute-start.16
  111.2 3.3 %collective-permute-done.14.refs_3_ = s16[8,32,256]{2,1,0:T(8,128)(2,1)S(1)} collective-permute-done((s16[8,32,256]{2,1,0:T(8,128)(2,1)S(1)}, s16[8,32,256]{2,1,0:T(8,128)(2,1)S(1)}, u32[]{:S(2)}, u32[]{:S(2)}) %collective-permute-start.14) | collective-permute-done | bytes 131104 | tf_op jit(solution)/shard_map/ppermute | solution.py:370
  114.6 2.9 %collective-permute-done.13.refs_2_ = s16[8,32,256]{2,1,0:T(8,128)(2,1)S(1)} collective-permute-done((s16[8,32,256]{2,1,0:T(8,128)(2,1)S(1)}, s16[8,32,256]{2,1,0:T(8,128)(2,1)S(1)}, u32[]{:S(2)}, u32[]{:S(2)}) %collective-permute-start.13) | collective-permute-done | bytes 131104 | tf_op jit(solution)/shard_map/ppermute | solution.py:370
  117.5 1.3 %first_kernel.1 = (f32[32,64,256]{2,1,0:T(8,128)}, f32[4,8,32,256]{3,2,1,0:T(8,128)S(1)}) custom-call(f32[32,64,256]{2,1,0:T(8,128)S(1)} %copy-done, s16[8,32,256]{2,1,0:T(8,128)(2,1)S(1)} %bitcast.50, s16[8,32,256]{2,1,0:T(8,128)(2,1)S(1)} %collective-permute-done.12.refs_1_, s16[8,32,256]{2,1,0:T(8,128)(2,1)S(1)} %collective-permute-done.13.refs_2_, ...), custom_call_target="tpu_custom_call" | custom-call | flops 524288 | bytes 2097152 | tf_op jit(solution)/shard_map/first_kernel/pallas_call | solution.py:242
  118.8 0.3 collective-permute-done.17.refs_1_
  119.0 2.8 %collective-permute-done.16.refs_0_ = s16[8,32,256]{2,1,0:T(8,128)(2,1)S(1)} collective-permute-done((s16[8,32,256]{2,1,0:T(8,128)(2,1)S(1)}, s16[8,32,256]{2,1,0:T(8,128)(2,1)S(1)}, u32[]{:S(2)}, u32[]{:S(2)}) %collective-permute-start.16) | collective-permute-done | bytes 131104 | tf_op jit(solution)/shard_map/ppermute | solution.py:370
  121.9 0.9 later_kernel.2.refs_2_
  122.7 0.0 collective-permute-done.15
  122.8 0.9 later_kernel.3
  (15 shorter events, 0.2 us)
Async XLA Ops:
  2.8 72.6 %all-to-all-start = ((bf16[64,32,256]{2,1,0:T(8,128)(2,1)}), bf16[64,32,256]{2,1,0:T(8,128)(2,1)S(1)}, u32[]{:S(2)}, u32[]{:S(2)}) async-start(bf16[64,32,256]{2,1,0:T(8,128)(2,1)} %bitcast.44), calls=%async_computation | async-start | bytes 2097152 | tf_op jit(solution)/shard_map/all_to_all | solution.py:320
  15.9 48.4 %copy-start.1 = (f32[1,256]{1,0:T(1,128)S(1)}, f32[1,256]{1,0:T(1,128)}, u32[]{:S(2)}) copy-start(f32[1,256]{1,0:T(1,128)} %own_profile_ref.3) | copy-start | bytes 3076
  18.0 1.6 %collective-permute-start.1 = (bf16[2,2,2,32,256]{4,3,2,1,0:T(8,128)(2,1)}, bf16[2,2,2,32,256]{4,3,2,1,0:T(8,128)(2,1)S(1)}, u32[]{:S(2)}, u32[]{:S(2)}) collective-permute-start(bf16[2,2,2,32,256]{4,3,2,1,0:T(8,128)(2,1)} %pick_kernel.1), channel_id=1, source_target_pairs={{0,0},{1,1},{2,2},{3,3},{4,4},{5,5},{6,6},{7,7},{8,8},{9,9},{10,10... | collective-permute-start | bytes 393224 | tf_op jit(solution)/shard_map/ppermute | solution.py:318
  19.6 1.8 %collective-permute-start.2 = (bf16[2,2,32,256]{3,2,1,0:T(8,128)(2,1)S(1)}, bf16[2,2,32,256]{3,2,1,0:T(8,128)(2,1)S(1)}, u32[]{:S(2)}, u32[]{:S(2)}) collective-permute-start(bf16[2,2,32,256]{3,2,1,0:T(8,128)(2,1)S(1)} %get-tuple-element.18), channel_id=1, source_target_pairs={{0,1},{1,0},{2,3},{3,2},{4,5},{5,4},{6,7},{7,6},{8,9},{9,8},{10,11... | collective-permute-start | bytes 196616 | tf_op jit(solution)/shard_map/ppermute | solution.py:289
  21.5 34.7 %collective-permute-start.3 = (bf16[2,32,256]{2,1,0:T(8,128)(2,1)S(1)}, bf16[2,32,256]{2,1,0:T(8,128)(2,1)S(1)}, u32[]{:S(2)}, u32[]{:S(2)}) collective-permute-start(bf16[2,32,256]{2,1,0:T(8,128)(2,1)S(1)} %get-tuple-element.21), channel_id=1, source_target_pairs={{0,16},{1,17},{2,18},{3,19},{4,20},{5,21},{6,22},{7,23},{8,24},{9,... | collective-permute-start | bytes 98312 | tf_op jit(solution)/shard_map/ppermute | solution.py:327
  24.4 33.0 %collective-permute-start.4 = (bf16[2,32,256]{2,1,0:T(8,128)(2,1)S(1)}, bf16[2,32,256]{2,1,0:T(8,128)(2,1)S(1)}, u32[]{:S(2)}, u32[]{:S(2)}) collective-permute-start(bf16[2,32,256]{2,1,0:T(8,128)(2,1)S(1)} %get-tuple-element.22), channel_id=1, source_target_pairs={{0,128},{128,0},{1,129},{129,1},{2,130},{130,2},{3,131},{131,3},{4... | collective-permute-start | bytes 98312 | tf_op jit(solution)/shard_map/ppermute | solution.py:328
  55.5 4.0 %collective-permute-start.5 = (bf16[2,32,256]{2,1,0:T(8,128)(2,1)S(1)}, bf16[2,32,256]{2,1,0:T(8,128)(2,1)S(1)}, u32[]{:S(2)}, u32[]{:S(2)}) collective-permute-start(bf16[2,32,256]{2,1,0:T(8,128)(2,1)S(1)} %get-tuple-element.23), channel_id=1, source_target_pairs={{0,144},{1,145},{2,146},{3,147},{4,148},{5,149},{6,150},{7,151},{8... | collective-permute-start | bytes 98312 | tf_op jit(solution)/shard_map/ppermute | solution.py:326
  59.5 9.2 %collective-permute-start.8 = (bf16[2,2,2,32,256]{4,3,2,1,0:T(8,128)(2,1)S(1)}, bf16[2,2,2,32,256]{4,3,2,1,0:T(8,128)(2,1)S(1)}, u32[]{:S(2)}, u32[]{:S(2)}) collective-permute-start(bf16[2,2,2,32,256]{4,3,2,1,0:T(8,128)(2,1)S(1)} %bitcast.51), channel_id=1, source_target_pairs={{0,96},{32,0},{64,32},{96,64},{1,97},{33,1},{65,33},{97,65},{2,98}... | collective-permute-start | bytes 393224 | tf_op jit(solution)/shard_map/ppermute | solution.py:333
  63.6 5.4 %collective-permute-start.7 = (bf16[2,2,2,32,256]{4,3,2,1,0:T(8,128)(2,1)S(1)}, bf16[2,2,2,32,256]{4,3,2,1,0:T(8,128)(2,1)S(1)}, u32[]{:S(2)}, u32[]{:S(2)}) collective-permute-start(bf16[2,2,2,32,256]{4,3,2,1,0:T(8,128)(2,1)S(1)} %bitcast.52), channel_id=1, source_target_pairs={{0,64},{32,96},{64,0},{96,32},{1,65},{33,97},{65,1},{97,33},{2,66}... | collective-permute-start | bytes 393224 | tf_op jit(solution)/shard_map/ppermute | solution.py:333
  63.6 8.8 %collective-permute-start.6 = (bf16[2,2,2,32,256]{4,3,2,1,0:T(8,128)(2,1)S(1)}, bf16[2,2,2,32,256]{4,3,2,1,0:T(8,128)(2,1)S(1)}, u32[]{:S(2)}, u32[]{:S(2)}) collective-permute-start(bf16[2,2,2,32,256]{4,3,2,1,0:T(8,128)(2,1)S(1)} %bitcast.53), channel_id=1, source_target_pairs={{0,32},{32,64},{64,96},{96,0},{1,33},{33,65},{65,97},{97,1},{2,34}... | collective-permute-start | bytes 393224 | tf_op jit(solution)/shard_map/ppermute | solution.py:333
  64.3 2.5 %collective-permute-start = (f32[1,384]{1,0:T(1,128)S(1)}, f32[1,384]{1,0:T(1,128)S(1)}, u32[]{:S(2)}, u32[]{:S(2)}) collective-permute-start(f32[1,384]{1,0:T(1,128)S(1)} %pad_maximum_fusion.1), channel_id=1, source_target_pairs={{0,128},{128,0},{1,129},{129,1},{2,130},{130,2},{3,131},{131,3},{4... | collective-permute-start | bytes 4616 | tf_op jit(solution)/shard_map/ppermute | solution.py:302
  78.6 38.8 %copy-start = (f32[32,64,256]{2,1,0:T(8,128)S(1)}, f32[32,64,256]{2,1,0:T(8,128)}, u32[]{:S(2)}) copy-start(f32[32,64,256]{2,1,0:T(8,128)} %est_ref.3) | copy-start | bytes 6291460
  78.7 5.5 %collective-permute-start.9 = (s16[32,8,256]{2,1,0:T(8,128)(2,1)S(1)}, s16[32,8,256]{2,1,0:T(8,128)(2,1)S(1)}, u32[]{:S(2)}, u32[]{:S(2)}) collective-permute-start(s16[32,8,256]{2,1,0:T(8,128)(2,1)S(1)} %get-tuple-element.9), channel_id=1, source_target_pairs={{0,64},{32,96},{64,0},{96,32},{1,65},{33,97},{65,1},{97,33},{2,66}... | collective-permute-start | bytes 393224 | tf_op jit(solution)/shard_map/ppermute | solution.py:362
  78.8 5.4 %collective-permute-start.11 = (s16[32,8,256]{2,1,0:T(8,128)(2,1)S(1)}, s16[32,8,256]{2,1,0:T(8,128)(2,1)S(1)}, u32[]{:S(2)}, u32[]{:S(2)}) collective-permute-start(s16[32,8,256]{2,1,0:T(8,128)(2,1)S(1)} %get-tuple-element.10), channel_id=1, source_target_pairs={{0,96},{32,0},{64,32},{96,64},{1,97},{33,1},{65,33},{97,65},{2,98}... | collective-permute-start | bytes 393224 | tf_op jit(solution)/shard_map/ppermute | solution.py:362
  78.9 8.8 %collective-permute-start.10 = (s16[32,8,256]{2,1,0:T(8,128)(2,1)S(1)}, s16[32,8,256]{2,1,0:T(8,128)(2,1)S(1)}, u32[]{:S(2)}, u32[]{:S(2)}) collective-permute-start(s16[32,8,256]{2,1,0:T(8,128)(2,1)S(1)} %get-tuple-element.11), channel_id=1, source_target_pairs={{0,32},{32,64},{64,96},{96,0},{1,33},{33,65},{65,97},{97,1},{2,34}... | collective-permute-start | bytes 393224 | tf_op jit(solution)/shard_map/ppermute | solution.py:362
  103.5 3.9 %collective-permute-start.12 = (s16[8,32,256]{2,1,0:T(8,128)(2,1)S(1)}, s16[8,32,256]{2,1,0:T(8,128)(2,1)S(1)}, u32[]{:S(2)}, u32[]{:S(2)}) collective-permute-start(s16[8,32,256]{2,1,0:T(8,128)(2,1)S(1)} %bitcast.46), channel_id=1, source_target_pairs={{0,128},{128,0},{1,129},{129,1},{2,130},{130,2},{3,131},{131,3},{4... | collective-permute-start | bytes 393224 | tf_op jit(solution)/shard_map/ppermute | solution.py:367
  107.4 15.3 %collective-permute-start.15 = (s16[2,8,32,256]{3,2,1,0:T(8,128)(2,1)S(1)}, s16[2,8,32,256]{3,2,1,0:T(8,128)(2,1)S(1)}, u32[]{:S(2)}, u32[]{:S(2)}) collective-permute-start(s16[2,8,32,256]{3,2,1,0:T(8,128)(2,1)S(1)} %pad_add_fusion), channel_id=1, source_target_pairs={{0,64},{32,96},{64,0},{96,32},{1,65},{33,97},{65,1},{97,33},{2,66}... | collective-permute-start | bytes 786440 | tf_op jit(solution)/shard_map/ppermute | solution.py:370
  107.6 7.0 %collective-permute-start.14 = (s16[8,32,256]{2,1,0:T(8,128)(2,1)S(1)}, s16[8,32,256]{2,1,0:T(8,128)(2,1)S(1)}, u32[]{:S(2)}, u32[]{:S(2)}) collective-permute-start(s16[8,32,256]{2,1,0:T(8,128)(2,1)S(1)} %bitcast.48), channel_id=1, source_target_pairs={{0,96},{32,0},{64,32},{96,64},{1,97},{33,1},{65,33},{97,65},{2,98}... | collective-permute-start | bytes 393224 | tf_op jit(solution)/shard_map/ppermute | solution.py:370
  108.6 8.9 %collective-permute-start.13 = (s16[8,32,256]{2,1,0:T(8,128)(2,1)S(1)}, s16[8,32,256]{2,1,0:T(8,128)(2,1)S(1)}, u32[]{:S(2)}, u32[]{:S(2)}) collective-permute-start(s16[8,32,256]{2,1,0:T(8,128)(2,1)S(1)} %bitcast.49), channel_id=1, source_target_pairs={{0,32},{32,64},{64,96},{96,0},{1,33},{33,65},{65,97},{97,1},{2,34}... | collective-permute-start | bytes 393224 | tf_op jit(solution)/shard_map/ppermute | solution.py:370
  109.3 9.7 %collective-permute-start.17 = (s16[8,32,256]{2,1,0:T(8,128)(2,1)S(1)}, s16[8,32,256]{2,1,0:T(8,128)(2,1)S(1)}, u32[]{:S(2)}, u32[]{:S(2)}) collective-permute-start(s16[8,32,256]{2,1,0:T(8,128)(2,1)S(1)} %collective-permute-done.12.refs_1_), channel_id=1, source_target_pairs={{0,96},{32,0},{64,32},{96,64},{1,97},{33,1},{65,33},{97,65},{2,98}... | collective-permute-start | bytes 393224 | tf_op jit(solution)/shard_map/ppermute | solution.py:370
  111.2 10.6 %collective-permute-start.16 = (s16[8,32,256]{2,1,0:T(8,128)(2,1)S(1)}, s16[8,32,256]{2,1,0:T(8,128)(2,1)S(1)}, u32[]{:S(2)}, u32[]{:S(2)}) collective-permute-start(s16[8,32,256]{2,1,0:T(8,128)(2,1)S(1)} %collective-permute-done.12.refs_1_), channel_id=1, source_target_pairs={{0,32},{32,64},{64,96},{96,0},{1,33},{33,65},{65,97},{97,1},{2,34}... | collective-permute-start | bytes 393224 | tf_op jit(solution)/shard_map/ppermute | solution.py:370

commit v8 on v5

--- a/solution.py
+++ b/solution.py
@@ -312,7 +312,7 @@
             pltpu.SemaphoreType.DMA((2, 2, 2)),
         ],
         cost_estimate=pl.CostEstimate(flops=0, bytes_accessed=2 << 20, transcendentals=0),
-        compiler_params=pltpu.CompilerParams(vmem_limit_bytes=125 << 19),
+        compiler_params=pltpu.CompilerParams(vmem_limit_bytes=32 << 19),
         name="pick_kernel",
     )(estimate)
     block = lax.ppermute(chip, ("upper", "column", "tile"), distance_route())
@@ -364,11 +364,12 @@
     logs = ((total + 2) >> 2).astype(jnp.int16)
     logs = lax.all_to_all(logs, "tile", 0, 0, tiled=True)
     logs = logs.transpose(1, 0, 2)
-    places = [(0, 0), (1, 2), (0, 2), (1, 1), (1, 3), (0, 1), (0, 3), (1, 0)]
-    pieces = [logs]
-    for u, d in places[1:]:
-        route = [(i, 4 * ((i // 4 + u) % 2) + (i + d) % 4) for i in range(8)]
-        pieces.append(lax.ppermute(logs, ("upper", "column"), route))
+    partner = lax.ppermute(logs, "upper", swap)
+    places, pieces = [(0, 0), (1, 0)], [logs, partner]
+    for u, d in [(0, 2), (0, 1), (0, 3), (1, 2), (1, 1), (1, 3)]:
+        route = [(i, (i + d) % 4) for i in range(4)]
+        places.append((u, d))
+        pieces.append(lax.ppermute(pieces[u], "column", route))
     return finish(places, estimate, pieces, 4, 2)
 
 

time: 119 us -> 118 us (level)
  Pallas kernels: 11.3 us -> 9.57 us
  starting transfers between devices: 69.5 us -> 67.9 us
  waiting for transfers between devices: 17.6 us -> 18.8 us
    ppermute x7, starting transfers between devices: 10.5 us -> 7.19 us  [the longest x6 6.81 us: update(): pieces.append(lax.ppermute(pieces[u], 'column', route))]
    ppermute x1, starting transfers between devices: 32.2 us -> 34.7 us  [update(): beside = lax.ppermute(other_line[0], 'upper', swap)]
    pallas_call x1, Pallas kernels: 2.06 us -> 0.33 us  [update(): pl.pallas_call(pick_kernel, out_shape=jax.ShapeDtypeStruct((2, 2, 2, ROWS...]
    unnamed x5 -> x7, local copies, waits for them, and re-layouts: 2.79 us -> 2.94 us
  transfers between devices with their start and end apart: 20 -> 20, of which waited for: 11 -> 12; matrix products, arithmetic and copies ran while one was open for 0% -> 0% of each run, Pallas kernels for 6% -> 5%
where the time goes in v8:
time: 118 us; the launch traced here: 117 us
  starting transfers between devices  67.9 us (58%)
  waiting for transfers between devices  18.8 us (16%)
  blocking collectives  16 us (14%)
  Pallas kernels  9.57 us (8%)
  local copies, waits for them, and re-layouts  3.03 us (3%)
  between operations  1.68 us (1%)
    ppermute x1, starting transfers between devices, update(): beside = lax.ppermute(other_line[0], 'upper', swap)  34.7 us
    all_to_all x1, blocking collectives, update(): logs = lax.all_to_all(logs, 'tile', 0, 0, tiled=True)  16 us
    all_to_all x1, starting transfers between devices, update(): image_lines = lax.all_to_all(image, ('upper', 'tile'), 0, 0, tiled=True)  13.1 us
    ppermute x6, starting transfers between devices, update(): pieces.append(lax.ppermute(pieces[u], 'column', route))  6.81 us
    ppermute x3, waiting for transfers between devices, update(): arrived = lax.ppermute(codes[d], 'column', route)  6.35 us
    ppermute x3, starting transfers between devices, update(): est_lines.append(lax.ppermute(piece, 'column', route))  5.92 us
    ppermute x6, waiting for transfers between devices, update(): pieces.append(lax.ppermute(pieces[u], 'column', route))  4.5 us
    pallas_call x1, Pallas kernels, update(): pl.pallas_call(back_kernel, out_shape=jax.ShapeDtypeStruct((4, SLABS, 8,...  3.25 us
  transfers between devices with their start and end apart: 20, of which 12 were waited for; matrix products, arithmetic and copies ran while one was open for 0% of the time, Pallas kernels for 5%

profile of v8, /device:TPU:1, one launch (start us, length us, event | category | flops | bytes accessed | tf_op | source)
XLA Modules:
  0.0 117.1 jit_solution(1503495804874753819)
XLA Ops:
  0.0 2.9 %copy.17 = bf16[1,32,64,256]{3,1,2,0:T(8,128)(2,1)} copy(bf16[1,32,64,256]{3,2,1,0:T(8,128)(2,1)} %param.6) | data formatting | bytes 2097152 | tf_op args[1]
  2.9 13.1 %all-to-all-start = ((bf16[64,32,256]{2,1,0:T(8,128)(2,1)}), bf16[64,32,256]{2,1,0:T(8,128)(2,1)S(1)}, u32[]{:S(2)}, u32[]{:S(2)}) async-start(bf16[64,32,256]{2,1,0:T(8,128)(2,1)} %bitcast.47), calls=%async_computation | async-start | bytes 2097152 | tf_op jit(solution)/shard_map/all_to_all | solution.py:320
  16.1 0.0 copy-start.2
  16.1 0.3 pick_kernel.1
  16.4 0.7 collective-permute-start.1
  17.1 0.0 collective-permute-done.1
  17.2 0.5 collective-permute-start.2
  19.0 0.0 collective-permute-done.2
  19.1 34.7 %collective-permute-start.4 = (bf16[2,32,256]{2,1,0:T(8,128)(2,1)S(1)}, bf16[2,32,256]{2,1,0:T(8,128)(2,1)S(1)}, u32[]{:S(2)}, u32[]{:S(2)}) collective-permute-start(bf16[2,32,256]{2,1,0:T(8,128)(2,1)S(1)} %get-tuple-element.18), channel_id=1, source_target_pairs={{0,128},{128,0},{1,129},{129,1},{2,130},{130,2},{3,131},{131,3},{4... | collective-permute-start | bytes 98312 | tf_op jit(solution)/shard_map/ppermute | solution.py:328
  53.8 1.4 %collective-permute-start.5 = (bf16[2,32,256]{2,1,0:T(8,128)(2,1)S(1)}, bf16[2,32,256]{2,1,0:T(8,128)(2,1)S(1)}, u32[]{:S(2)}, u32[]{:S(2)}) collective-permute-start(bf16[2,32,256]{2,1,0:T(8,128)(2,1)S(1)} %get-tuple-element.19), channel_id=1, source_target_pairs={{0,144},{1,145},{2,146},{3,147},{4,148},{5,149},{6,150},{7,151},{8... | collective-permute-start | bytes 98312 | tf_op jit(solution)/shard_map/ppermute | solution.py:326
  55.2 1.2 %collective-permute-start.3 = (bf16[2,32,256]{2,1,0:T(8,128)(2,1)S(1)}, bf16[2,32,256]{2,1,0:T(8,128)(2,1)S(1)}, u32[]{:S(2)}, u32[]{:S(2)}) collective-permute-start(bf16[2,32,256]{2,1,0:T(8,128)(2,1)S(1)} %get-tuple-element.17), channel_id=1, source_target_pairs={{0,16},{1,17},{2,18},{3,19},{4,20},{5,21},{6,22},{7,23},{8,24},{9,... | collective-permute-start | bytes 98312 | tf_op jit(solution)/shard_map/ppermute | solution.py:327
  56.4 0.1 add_convert_fusion
  56.5 0.0 collective-permute-done.4
  56.5 1.3 %collective-permute-done.5 = bf16[2,32,256]{2,1,0:T(8,128)(2,1)S(1)} collective-permute-done((bf16[2,32,256]{2,1,0:T(8,128)(2,1)S(1)}, bf16[2,32,256]{2,1,0:T(8,128)(2,1)S(1)}, u32[]{:S(2)}, u32[]{:S(2)}) %collective-permute-start.5) | collective-permute-done | bytes 32800 | tf_op jit(solution)/shard_map/ppermute | solution.py:326
  57.8 1.7 %collective-permute-done.3 = bf16[2,32,256]{2,1,0:T(8,128)(2,1)S(1)} collective-permute-done((bf16[2,32,256]{2,1,0:T(8,128)(2,1)S(1)}, bf16[2,32,256]{2,1,0:T(8,128)(2,1)S(1)}, u32[]{:S(2)}, u32[]{:S(2)}) %collective-permute-start.3) | collective-permute-done | bytes 32800 | tf_op jit(solution)/shard_map/ppermute | solution.py:327
  59.5 0.1 collective-permute-start.6
  59.6 5.8 %collective-permute-start.7 = (bf16[2,2,2,32,256]{4,3,2,1,0:T(8,128)(2,1)S(1)}, bf16[2,2,2,32,256]{4,3,2,1,0:T(8,128)(2,1)S(1)}, u32[]{:S(2)}, u32[]{:S(2)}) collective-permute-start(bf16[2,2,2,32,256]{4,3,2,1,0:T(8,128)(2,1)S(1)} %bitcast.44), channel_id=1, source_target_pairs={{0,64},{32,96},{64,0},{96,32},{1,65},{33,97},{65,1},{97,33},{2,66}... | collective-permute-start | bytes 393224 | tf_op jit(solution)/shard_map/ppermute | solution.py:333
  65.5 0.1 collective-permute-start
  65.6 2.7 %collective-permute-done.other_ref.other_profile_ref = f32[1,384]{1,0:T(1,128)S(1)} collective-permute-done((f32[1,384]{1,0:T(1,128)S(1)}, f32[1,384]{1,0:T(1,128)S(1)}, u32[]{:S(2)}, u32[]{:S(2)}) %collective-permute-start) | collective-permute-done | bytes 1568 | tf_op jit(solution)/shard_map/ppermute | solution.py:302
  68.3 0.0 collective-permute-done.6.est1_ref
  68.3 1.5 %collective-permute-done.7.est2_ref = bf16[2,2,2,32,256]{4,3,2,1,0:T(8,128)(2,1)S(1)} collective-permute-done((bf16[2,2,2,32,256]{4,3,2,1,0:T(8,128)(2,1)S(1)}, bf16[2,2,2,32,256]{4,3,2,1,0:T(8,128)(2,1)S(1)}, u32[]{:S(2)}, u32[]{:S(2)}) %collective-permute-start.7) | collective-permute-done | bytes 131104 | tf_op jit(solution)/shard_map/ppermute | solution.py:333
  69.8 0.6 collective-permute-done.8.est3_ref
  70.4 3.0 %forward_kernel.1.inverse_ref = f32[2,1024,256]{2,1,0:T(8,128)S(1)} custom-call(s32[1]{0:T(128)S(6)} %copy.22.shift_ref, s32[1]{0:T(128)S(6)} %copy.21.offset_ref, f32[1,384]{1,0:T(1,128)S(1)} %collective-permute-done.other_ref.other_profile_ref, f32[1,256]{1,0:T(1,128)S(1)} %copy-done.2, f32[1,384]{1,0:T(1,128)S(1)} %collective-permute-done.other_ref.other_profile_ref, ...), custom_call_target="tpu_custom_call" | custom-call | flops 268435456 | bytes 8388608 | tf_op jit(solution)/shard_map/forward_kernel/pallas_call | solution.py:335
  73.4 0.0 copy-start.1
  73.4 3.3 %back_kernel.1 = s16[4,32,8,256]{3,2,1,0:T(8,128)(2,1)S(1)} custom-call(s32[1]{0:T(128)S(6)} %copy.22.shift_ref, s32[1]{0:T(128)S(6)} %copy.21.offset_ref, f32[1,384]{1,0:T(1,128)S(1)} %collective-permute-done.other_ref.other_profile_ref, f32[1,256]{1,0:T(1,128)S(1)} %copy-done.2, f32[1,384]{1,0:T(1,128)S(1)} %collective-permute-done.other_ref.other_profile_ref, ...), custom_call_target="tpu_custom_call" | custom-call | tf_op jit(solution)/shard_map/back_kernel/pallas_call | solution.py:347
  76.7 0.1 collective-permute-start.10
  76.8 2.7 %collective-permute-start.11 = (s16[32,8,256]{2,1,0:T(8,128)(2,1)S(1)}, s16[32,8,256]{2,1,0:T(8,128)(2,1)S(1)}, u32[]{:S(2)}, u32[]{:S(2)}) collective-permute-start(s16[32,8,256]{2,1,0:T(8,128)(2,1)S(1)} %get-tuple-element.10), channel_id=1, source_target_pairs={{0,96},{32,0},{64,32},{96,64},{1,97},{33,1},{65,33},{97,65},{2,98}... | collective-permute-start | bytes 393224 | tf_op jit(solution)/shard_map/ppermute | solution.py:362
  79.5 0.2 collective-permute-start.9
  79.7 2.1 %collective-permute-done.10 = s16[32,8,256]{2,1,0:T(8,128)(2,1)S(1)} collective-permute-done((s16[32,8,256]{2,1,0:T(8,128)(2,1)S(1)}, s16[32,8,256]{2,1,0:T(8,128)(2,1)S(1)}, u32[]{:S(2)}, u32[]{:S(2)}) %collective-permute-start.10) | collective-permute-done | bytes 131104 | tf_op jit(solution)/shard_map/ppermute | solution.py:362
  81.8 1.0 collective-permute-done.11
  82.8 3.3 %collective-permute-done.9 = s16[32,8,256]{2,1,0:T(8,128)(2,1)S(1)} collective-permute-done((s16[32,8,256]{2,1,0:T(8,128)(2,1)S(1)}, s16[32,8,256]{2,1,0:T(8,128)(2,1)S(1)}, u32[]{:S(2)}, u32[]{:S(2)}) %collective-permute-start.9) | collective-permute-done | bytes 131104 | tf_op jit(solution)/shard_map/ppermute | solution.py:362
  86.1 0.2 fusion.4
  86.2 16.0 %all_to_all.10 = s16[32,8,256]{2,1,0:T(8,128)(2,1)S(1)} all-to-all(s16[32,8,256]{2,1,0:T(8,128)(2,1)S(1)} %fusion.4), channel_id=1, replica_groups=mesh['upper'=2,'column'=4,'tile'=32] {'tile'}, dimensions={0} | all-to-all | bytes 262144 | tf_op jit(solution)/shard_map/all_to_all | solution.py:365
  102.2 0.4 collective-permute-start.12
  102.6 1.0 collective-permute-start.13
  103.6 1.2 %collective-permute-start.14 = (s16[8,32,256]{2,1,0:T(8,128)(2,1)S(1)}, s16[8,32,256]{2,1,0:T(8,128)(2,1)S(1)}, u32[]{:S(2)}, u32[]{:S(2)}) collective-permute-start(s16[8,32,256]{2,1,0:T(8,128)(2,1)S(1)} %bitcast.40), channel_id=1, source_target_pairs={{0,32},{32,64},{64,96},{96,0},{1,33},{33,65},{65,97},{97,1},{2,34}... | collective-permute-start | bytes 393224 | tf_op jit(solution)/shard_map/ppermute | solution.py:372
  104.8 1.5 %collective-permute-start.17 = (s16[8,32,256]{2,1,0:T(8,128)(2,1)S(1)}, s16[8,32,256]{2,1,0:T(8,128)(2,1)S(1)}, u32[]{:S(2)}, u32[]{:S(2)}) collective-permute-start(s16[8,32,256]{2,1,0:T(8,128)(2,1)S(1)} %bitcast.41), channel_id=1, source_target_pairs={{0,96},{32,0},{64,32},{96,64},{1,97},{33,1},{65,33},{97,65},{2,98}... | collective-permute-start | bytes 393224 | tf_op jit(solution)/shard_map/ppermute | solution.py:372
  106.3 0.0 collective-permute-done.12.refs_1_
  106.3 0.8 collective-permute-start.18
  107.0 0.7 collective-permute-start.15
  107.7 0.3 collective-permute-done.13.refs_2_
  108.0 1.7 %collective-permute-start.16 = (s16[8,32,256]{2,1,0:T(8,128)(2,1)S(1)}, s16[8,32,256]{2,1,0:T(8,128)(2,1)S(1)}, u32[]{:S(2)}, u32[]{:S(2)}) collective-permute-start(s16[8,32,256]{2,1,0:T(8,128)(2,1)S(1)} %collective-permute-done.12.refs_1_), channel_id=1, source_target_pairs={{0,96},{32,0},{64,32},{96,64},{1,97},{33,1},{65,33},{97,65},{2,98}... | collective-permute-start | bytes 393224 | tf_op jit(solution)/shard_map/ppermute | solution.py:372
  109.7 0.3 collective-permute-done.14.refs_3_
  110.0 1.3 %first_kernel.1 = (f32[32,64,256]{2,1,0:T(8,128)}, f32[4,8,32,256]{3,2,1,0:T(8,128)S(1)}) custom-call(f32[32,64,256]{2,1,0:T(8,128)S(1)} %copy-done.1, s16[8,32,256]{2,1,0:T(8,128)(2,1)S(1)} %bitcast.42, s16[8,32,256]{2,1,0:T(8,128)(2,1)S(1)} %collective-permute-done.12.refs_1_, s16[8,32,256]{2,1,0:T(8,128)(2,1)S(1)} %collective-permute-done.13.refs_2_, ...), custom_call_target="tpu_custom_call" | custom-call | flops 524288 | bytes 2097152 | tf_op jit(solution)/shard_map/first_kernel/pallas_call | solution.py:242
  111.3 1.7 %collective-permute-done.18.refs_1_ = s16[8,32,256]{2,1,0:T(8,128)(2,1)S(1)} collective-permute-done((s16[8,32,256]{2,1,0:T(8,128)(2,1)S(1)}, s16[8,32,256]{2,1,0:T(8,128)(2,1)S(1)}, u32[]{:S(2)}, u32[]{:S(2)}) %collective-permute-start.18) | collective-permute-done | bytes 131104 | tf_op jit(solution)/shard_map/ppermute | solution.py:372
  113.0 0.9 later_kernel.2.refs_2_
  113.9 2.2 %collective-permute-done.15.refs_0_ = s16[8,32,256]{2,1,0:T(8,128)(2,1)S(1)} collective-permute-done((s16[8,32,256]{2,1,0:T(8,128)(2,1)S(1)}, s16[8,32,256]{2,1,0:T(8,128)(2,1)S(1)}, u32[]{:S(2)}, u32[]{:S(2)}) %collective-permute-start.15) | collective-permute-done | bytes 131104 | tf_op jit(solution)/shard_map/ppermute | solution.py:372
  116.1 0.9 later_kernel.3
  (17 shorter events, 0.1 us)
Async XLA Ops:
  0.0 16.1 %copy-start = (f32[32,64,256]{2,1,0:T(8,128)S(1)}, f32[32,64,256]{2,1,0:T(8,128)}, u32[]{:S(2)}) copy-start(f32[32,64,256]{2,1,0:T(8,128)} %est_ref.3) | copy-start | bytes 6291460
  2.9 70.5 %all-to-all-start = ((bf16[64,32,256]{2,1,0:T(8,128)(2,1)}), bf16[64,32,256]{2,1,0:T(8,128)(2,1)S(1)}, u32[]{:S(2)}, u32[]{:S(2)}) async-start(bf16[64,32,256]{2,1,0:T(8,128)(2,1)} %bitcast.47), calls=%async_computation | async-start | bytes 2097152 | tf_op jit(solution)/shard_map/all_to_all | solution.py:320
  16.1 49.4 %copy-start.2 = (f32[1,256]{1,0:T(1,128)S(1)}, f32[1,256]{1,0:T(1,128)}, u32[]{:S(2)}) copy-start(f32[1,256]{1,0:T(1,128)} %own_profile_ref.3) | copy-start | bytes 3076
  16.4 0.7 collective-permute-start.1
  17.2 1.8 %collective-permute-start.2 = (bf16[2,2,32,256]{3,2,1,0:T(8,128)(2,1)S(1)}, bf16[2,2,32,256]{3,2,1,0:T(8,128)(2,1)S(1)}, u32[]{:S(2)}, u32[]{:S(2)}) collective-permute-start(bf16[2,2,32,256]{3,2,1,0:T(8,128)(2,1)S(1)} %get-tuple-element.14), channel_id=1, source_target_pairs={{0,1},{1,0},{2,3},{3,2},{4,5},{5,4},{6,7},{7,6},{8,9},{9,8},{10,11... | collective-permute-start | bytes 196616 | tf_op jit(solution)/shard_map/ppermute | solution.py:289
  19.1 37.4 %collective-permute-start.4 = (bf16[2,32,256]{2,1,0:T(8,128)(2,1)S(1)}, bf16[2,32,256]{2,1,0:T(8,128)(2,1)S(1)}, u32[]{:S(2)}, u32[]{:S(2)}) collective-permute-start(bf16[2,32,256]{2,1,0:T(8,128)(2,1)S(1)} %get-tuple-element.18), channel_id=1, source_target_pairs={{0,128},{128,0},{1,129},{129,1},{2,130},{130,2},{3,131},{131,3},{4... | collective-permute-start | bytes 98312 | tf_op jit(solution)/shard_map/ppermute | solution.py:328
  53.8 4.0 %collective-permute-start.5 = (bf16[2,32,256]{2,1,0:T(8,128)(2,1)S(1)}, bf16[2,32,256]{2,1,0:T(8,128)(2,1)S(1)}, u32[]{:S(2)}, u32[]{:S(2)}) collective-permute-start(bf16[2,32,256]{2,1,0:T(8,128)(2,1)S(1)} %get-tuple-element.19), channel_id=1, source_target_pairs={{0,144},{1,145},{2,146},{3,147},{4,148},{5,149},{6,150},{7,151},{8... | collective-permute-start | bytes 98312 | tf_op jit(solution)/shard_map/ppermute | solution.py:326
  55.2 4.3 %collective-permute-start.3 = (bf16[2,32,256]{2,1,0:T(8,128)(2,1)S(1)}, bf16[2,32,256]{2,1,0:T(8,128)(2,1)S(1)}, u32[]{:S(2)}, u32[]{:S(2)}) collective-permute-start(bf16[2,32,256]{2,1,0:T(8,128)(2,1)S(1)} %get-tuple-element.17), channel_id=1, source_target_pairs={{0,16},{1,17},{2,18},{3,19},{4,20},{5,21},{6,22},{7,23},{8,24},{9,... | collective-permute-start | bytes 98312 | tf_op jit(solution)/shard_map/ppermute | solution.py:327
  59.5 8.8 %collective-permute-start.6 = (bf16[2,2,2,32,256]{4,3,2,1,0:T(8,128)(2,1)S(1)}, bf16[2,2,2,32,256]{4,3,2,1,0:T(8,128)(2,1)S(1)}, u32[]{:S(2)}, u32[]{:S(2)}) collective-permute-start(bf16[2,2,2,32,256]{4,3,2,1,0:T(8,128)(2,1)S(1)} %bitcast.43), channel_id=1, source_target_pairs={{0,32},{32,64},{64,96},{96,0},{1,33},{33,65},{65,97},{97,1},{2,34}... | collective-permute-start | bytes 393224 | tf_op jit(solution)/shard_map/ppermute | solution.py:333
  59.6 10.2 %collective-permute-start.7 = (bf16[2,2,2,32,256]{4,3,2,1,0:T(8,128)(2,1)S(1)}, bf16[2,2,2,32,256]{4,3,2,1,0:T(8,128)(2,1)S(1)}, u32[]{:S(2)}, u32[]{:S(2)}) collective-permute-start(bf16[2,2,2,32,256]{4,3,2,1,0:T(8,128)(2,1)S(1)} %bitcast.44), channel_id=1, source_target_pairs={{0,64},{32,96},{64,0},{96,32},{1,65},{33,97},{65,1},{97,33},{2,66}... | collective-permute-start | bytes 393224 | tf_op jit(solution)/shard_map/ppermute | solution.py:333
  65.4 5.0 %collective-permute-start.8 = (bf16[2,2,2,32,256]{4,3,2,1,0:T(8,128)(2,1)S(1)}, bf16[2,2,2,32,256]{4,3,2,1,0:T(8,128)(2,1)S(1)}, u32[]{:S(2)}, u32[]{:S(2)}) collective-permute-start(bf16[2,2,2,32,256]{4,3,2,1,0:T(8,128)(2,1)S(1)} %bitcast.45), channel_id=1, source_target_pairs={{0,96},{32,0},{64,32},{96,64},{1,97},{33,1},{65,33},{97,65},{2,98}... | collective-permute-start | bytes 393224 | tf_op jit(solution)/shard_map/ppermute | solution.py:333
  65.5 2.8 %collective-permute-start = (f32[1,384]{1,0:T(1,128)S(1)}, f32[1,384]{1,0:T(1,128)S(1)}, u32[]{:S(2)}, u32[]{:S(2)}) collective-permute-start(f32[1,384]{1,0:T(1,128)S(1)} %pad_maximum_fusion.1), channel_id=1, source_target_pairs={{0,128},{128,0},{1,129},{129,1},{2,130},{130,2},{3,131},{131,3},{4... | collective-permute-start | bytes 4616 | tf_op jit(solution)/shard_map/ppermute | solution.py:302
  73.4 36.6 %copy-start.1 = (f32[32,64,256]{2,1,0:T(8,128)S(1)}, f32[32,64,256]{2,1,0:T(8,128)}, u32[]{:S(2)}) copy-start(f32[32,64,256]{2,1,0:T(8,128)} %est_ref.3) | copy-start | bytes 6291460
  76.7 5.1 %collective-permute-start.10 = (s16[32,8,256]{2,1,0:T(8,128)(2,1)S(1)}, s16[32,8,256]{2,1,0:T(8,128)(2,1)S(1)}, u32[]{:S(2)}, u32[]{:S(2)}) collective-permute-start(s16[32,8,256]{2,1,0:T(8,128)(2,1)S(1)} %get-tuple-element.11), channel_id=1, source_target_pairs={{0,32},{32,64},{64,96},{96,0},{1,33},{33,65},{65,97},{97,1},{2,34}... | collective-permute-start | bytes 393224 | tf_op jit(solution)/shard_map/ppermute | solution.py:362
  76.8 6.0 %collective-permute-start.11 = (s16[32,8,256]{2,1,0:T(8,128)(2,1)S(1)}, s16[32,8,256]{2,1,0:T(8,128)(2,1)S(1)}, u32[]{:S(2)}, u32[]{:S(2)}) collective-permute-start(s16[32,8,256]{2,1,0:T(8,128)(2,1)S(1)} %get-tuple-element.10), channel_id=1, source_target_pairs={{0,96},{32,0},{64,32},{96,64},{1,97},{33,1},{65,33},{97,65},{2,98}... | collective-permute-start | bytes 393224 | tf_op jit(solution)/shard_map/ppermute | solution.py:362
  79.5 6.6 %collective-permute-start.9 = (s16[32,8,256]{2,1,0:T(8,128)(2,1)S(1)}, s16[32,8,256]{2,1,0:T(8,128)(2,1)S(1)}, u32[]{:S(2)}, u32[]{:S(2)}) collective-permute-start(s16[32,8,256]{2,1,0:T(8,128)(2,1)S(1)} %get-tuple-element.9), channel_id=1, source_target_pairs={{0,64},{32,96},{64,0},{96,32},{1,65},{33,97},{65,1},{97,33},{2,66}... | collective-permute-start | bytes 393224 | tf_op jit(solution)/shard_map/ppermute | solution.py:362
  102.2 4.0 %collective-permute-start.12 = (s16[8,32,256]{2,1,0:T(8,128)(2,1)S(1)}, s16[8,32,256]{2,1,0:T(8,128)(2,1)S(1)}, u32[]{:S(2)}, u32[]{:S(2)}) collective-permute-start(s16[8,32,256]{2,1,0:T(8,128)(2,1)S(1)} %bitcast.38), channel_id=1, source_target_pairs={{0,128},{128,0},{1,129},{129,1},{2,130},{130,2},{3,131},{131,3},{4... | collective-permute-start | bytes 393224 | tf_op jit(solution)/shard_map/ppermute | solution.py:367
  102.6 5.4 %collective-permute-start.13 = (s16[8,32,256]{2,1,0:T(8,128)(2,1)S(1)}, s16[8,32,256]{2,1,0:T(8,128)(2,1)S(1)}, u32[]{:S(2)}, u32[]{:S(2)}) collective-permute-start(s16[8,32,256]{2,1,0:T(8,128)(2,1)S(1)} %bitcast.39), channel_id=1, source_target_pairs={{0,64},{32,96},{64,0},{96,32},{1,65},{33,97},{65,1},{97,33},{2,66}... | collective-permute-start | bytes 393224 | tf_op jit(solution)/shard_map/ppermute | solution.py:372
  103.6 6.4 %collective-permute-start.14 = (s16[8,32,256]{2,1,0:T(8,128)(2,1)S(1)}, s16[8,32,256]{2,1,0:T(8,128)(2,1)S(1)}, u32[]{:S(2)}, u32[]{:S(2)}) collective-permute-start(s16[8,32,256]{2,1,0:T(8,128)(2,1)S(1)} %bitcast.40), channel_id=1, source_target_pairs={{0,32},{32,64},{64,96},{96,0},{1,33},{33,65},{65,97},{97,1},{2,34}... | collective-permute-start | bytes 393224 | tf_op jit(solution)/shard_map/ppermute | solution.py:372
  104.8 6.5 %collective-permute-start.17 = (s16[8,32,256]{2,1,0:T(8,128)(2,1)S(1)}, s16[8,32,256]{2,1,0:T(8,128)(2,1)S(1)}, u32[]{:S(2)}, u32[]{:S(2)}) collective-permute-start(s16[8,32,256]{2,1,0:T(8,128)(2,1)S(1)} %bitcast.41), channel_id=1, source_target_pairs={{0,96},{32,0},{64,32},{96,64},{1,97},{33,1},{65,33},{97,65},{2,98}... | collective-permute-start | bytes 393224 | tf_op jit(solution)/shard_map/ppermute | solution.py:372
  106.3 6.7 %collective-permute-start.18 = (s16[8,32,256]{2,1,0:T(8,128)(2,1)S(1)}, s16[8,32,256]{2,1,0:T(8,128)(2,1)S(1)}, u32[]{:S(2)}, u32[]{:S(2)}) collective-permute-start(s16[8,32,256]{2,1,0:T(8,128)(2,1)S(1)} %collective-permute-done.12.refs_1_), channel_id=1, source_target_pairs={{0,64},{32,96},{64,0},{96,32},{1,65},{33,97},{65,1},{97,33},{2,66}... | collective-permute-start | bytes 393224 | tf_op jit(solution)/shard_map/ppermute | solution.py:372
  107.0 9.1 %collective-permute-start.15 = (s16[8,32,256]{2,1,0:T(8,128)(2,1)S(1)}, s16[8,32,256]{2,1,0:T(8,128)(2,1)S(1)}, u32[]{:S(2)}, u32[]{:S(2)}) collective-permute-start(s16[8,32,256]{2,1,0:T(8,128)(2,1)S(1)} %collective-permute-done.12.refs_1_), channel_id=1, source_target_pairs={{0,32},{32,64},{64,96},{96,0},{1,33},{33,65},{65,97},{97,1},{2,34}... | collective-permute-start | bytes 393224 | tf_op jit(solution)/shard_map/ppermute | solution.py:372
  108.0 8.1 %collective-permute-start.16 = (s16[8,32,256]{2,1,0:T(8,128)(2,1)S(1)}, s16[8,32,256]{2,1,0:T(8,128)(2,1)S(1)}, u32[]{:S(2)}, u32[]{:S(2)}) collective-permute-start(s16[8,32,256]{2,1,0:T(8,128)(2,1)S(1)} %collective-permute-done.12.refs_1_), channel_id=1, source_target_pairs={{0,96},{32,0},{64,32},{96,64},{1,97},{33,1},{65,33},{97,65},{2,98}... | collective-permute-start | bytes 393224 | tf_op jit(solution)/shard_map/ppermute | solution.py:372
